TPU v7x, 32 devices: a whole 2x2x4 slice. The times are simulated.
32 devices in a mesh: dp: 16 (over z, y, x), mp: 2 (over core).
Axes of the slice: x: 2, y: 2, z: 4, core: 2. Of those that a mesh axis runs over, the one named last changes fastest.
Arguments:
- tokens: bfloat16 [37632, 768], P('dp'), may hold values from -6 to 6
- counts: int32 [192], P('dp'), may hold values from 1 to 4, as said below
- visible: int32 [768, 49], P('dp'), may hold values from 0 to 195, as said below
- dest_device: int32 [768], P('dp'), may hold values from 0 to 15, as said below
- dest_slot: int32 [768], P('dp'), may hold values from 0 to 47, as said below
- cotangent: bfloat16 [768, 196, 512], P('dp', None, 'mp'), may hold values from -6 to 6
- weight_inproj: float32 [768, 3, 768], P('dp', None, 'mp'), as said below
- moment_inproj: float32 [768, 3, 768], P('dp', None, 'mp'), as said below
- square_inproj: float32 [768, 3, 768], P('dp', None, 'mp'), may hold values from 0.25 to 1
- weight_outproj: float32 [768, 768], P('mp', 'dp'), as said below
- moment_outproj: float32 [768, 768], P('mp', 'dp'), as said below
- square_outproj: float32 [768, 768], P('mp', 'dp'), may hold values from 0.25 to 1
- weight_expand: float32 [768, 3072], P('dp', 'mp'), as said below
- moment_expand: float32 [768, 3072], P('dp', 'mp'), as said below
- square_expand: float32 [768, 3072], P('dp', 'mp'), may hold values from 0.25 to 1
- weight_shrink: float32 [3072, 768], P('mp', 'dp'), as said below
- moment_shrink: float32 [3072, 768], P('mp', 'dp'), as said below
- square_shrink: float32 [3072, 768], P('mp', 'dp'), may hold values from 0.25 to 1
- weight_embedder: float32 [768, 512], P('dp', 'mp'), as said below
- moment_embedder: float32 [768, 512], P('dp', 'mp'), as said below
- square_embedder: float32 [768, 512], P('dp', 'mp'), may hold values from 0.25 to 1
- weight_lnparams: float32 [4, 768], P(None, 'dp'), may hold values from -2 to 2, as said below
- moment_lnparams: float32 [4, 768], P(None, 'dp'), may hold values from -9 to 9
- square_lnparams: float32 [4, 768], P(None, 'dp'), may hold values from 2.25 to 9
- weight_decparams: float32 [2, 2, 256], P(None, 'mp', 'dp'), may hold values from -3 to 3
- moment_decparams: float32 [2, 2, 256], P(None, 'mp', 'dp'), may hold values from -9 to 9
- square_decparams: float32 [2, 2, 256], P(None, 'mp', 'dp'), may hold values from 2.25 to 9
Outputs:
- decoded: bfloat16 [768, 196, 512], P('dp', None, 'mp')
- grad_tokens: bfloat16 [37632, 768], P('dp')
- clip_norm: float32 [1], replicated
- norms: float32 [2, 7], replicated
- grads_inproj: float32 [768, 3, 768], P('dp', None, 'mp')
- momenta_inproj: float32 [768, 3, 768], P('dp', None, 'mp')
- squares_inproj: float32 [768, 3, 768], P('dp', None, 'mp')
- updated_inproj: float32 [768, 3, 768], P('dp', None, 'mp')
- copies_inproj: bfloat16 [768, 3, 768], P('dp', None, 'mp')
- grads_outproj: float32 [768, 768], P('mp', 'dp')
- momenta_outproj: float32 [768, 768], P('mp', 'dp')
- squares_outproj: float32 [768, 768], P('mp', 'dp')
- updated_outproj: float32 [768, 768], P('mp', 'dp')
- copies_outproj: bfloat16 [768, 768], P('mp', 'dp')
- grads_expand: float32 [768, 3072], P('dp', 'mp')
- momenta_expand: float32 [768, 3072], P('dp', 'mp')
- squares_expand: float32 [768, 3072], P('dp', 'mp')
- updated_expand: float32 [768, 3072], P('dp', 'mp')
- copies_expand: bfloat16 [768, 3072], P('dp', 'mp')
- grads_shrink: float32 [3072, 768], P('mp', 'dp')
- momenta_shrink: float32 [3072, 768], P('mp', 'dp')
- squares_shrink: float32 [3072, 768], P('mp', 'dp')
- updated_shrink: float32 [3072, 768], P('mp', 'dp')
- copies_shrink: bfloat16 [3072, 768], P('mp', 'dp')
- grads_embedder: float32 [768, 512], P('dp', 'mp')
- momenta_embedder: float32 [768, 512], P('dp', 'mp')
- squares_embedder: float32 [768, 512], P('dp', 'mp')
- updated_embedder: float32 [768, 512], P('dp', 'mp')
- copies_embedder: bfloat16 [768, 512], P('dp', 'mp')
- grads_lnparams: float32 [4, 768], P(None, 'dp')
- momenta_lnparams: float32 [4, 768], P(None, 'dp')
- squares_lnparams: float32 [4, 768], P(None, 'dp')
- updated_lnparams: float32 [4, 768], P(None, 'dp')
- copies_lnparams: bfloat16 [4, 768], P(None, 'dp')
- grads_decparams: float32 [2, 2, 256], P(None, 'mp', 'dp')
- momenta_decparams: float32 [2, 2, 256], P(None, 'mp', 'dp')
- squares_decparams: float32 [2, 2, 256], P(None, 'mp', 'dp')
- updated_decparams: float32 [2, 2, 256], P(None, 'mp', 'dp')
- copies_decparams: bfloat16 [2, 2, 256], P(None, 'mp', 'dp')
Inputs may be any that keep to these rules, and one draw needn't show every extreme that they name: `counts`: views of each episode; every value from 1 to 4 occurs. `visible`: each row names 49 different grid positions in increasing order. `dest_device`: every index of dp owns exactly 48 views, and no index of dp sends more than 3 of its views to one owner; that bound is reached. `dest_slot`: the views that one owner receives have different slots, so each of its 48 slots is taken once. `weight_lnparams`: rows 0 and 2 are gains, rows 1 and 3 biases. `weight_inproj`: entries of about the inverse root of 768 in size. `moment_inproj`: entries of mean zero. `weight_outproj`: entries of mean zero, of about 4 over the root of 768 in size. `moment_outproj`: entries of mean zero. `weight_expand`: entries of about the inverse root of 768 in size. `moment_expand`: entries of mean zero. `weight_shrink`: entries of mean zero, of about the inverse root of 3072 in size. `moment_shrink`: entries of mean zero. `weight_embedder`: entries of mean zero, of about the inverse root of 768 in size. `moment_embedder`: entries of mean zero.
All inputs are finite; a program needn't handle non-finite values.
Results may differ from a plain program's by a relative error of at most 0.02.
Values may be sent and summed in bfloat16 or wider, within the bound.
No kernel may reach another device: no remote copies, remote signals or barrier semaphores. Data moves between devices by JAX's collectives and lax.ppermute only.
A program may use at most 256 MiB of HBM per device.

v0:
```python
import math

import jax
import jax.numpy as jnp
from jax import lax
from jax.sharding import PartitionSpec as P

HEADDIM = 64
PARAMS = 7475200


NORM_EPS = 1e-06
MASK_FILL = -1e30
BETA_ONE = 0.5
BETA_TWO = 0.5
ADAM_EPS = 1e-06
DECAY_RATE = 0.01
LEARN_RATE = 0.5
TRUST_EPS = 1e-06


def layer_norm(values):
    centre = values - jnp.mean(values, axis=-1, keepdims=True)
    spread = jnp.mean(centre * centre, axis=-1, keepdims=True)
    inverse = lax.rsqrt(spread + NORM_EPS)
    return (centre * inverse, inverse)


def norm_back(grad_out, normed, inverse, gain):
    scaled = grad_out * gain
    return inverse * (
        scaled
        - jnp.mean(scaled, axis=-1, keepdims=True)
        - normed * jnp.mean(scaled * normed, axis=-1, keepdims=True)
    )


def gelu_exact(values):
    return 0.5 * values * (1.0 + lax.erf(values * (1.0 / math.sqrt(2.0))))


def gelu_slope(values):
    cumulative = 0.5 * (1.0 + lax.erf(values * (1.0 / math.sqrt(2.0))))
    return cumulative + values * jnp.exp(-0.5 * values * values) * (1.0 / math.sqrt(2.0 * math.pi))


def allowed_mask(counts, span, per_view):
    slot_view = jnp.arange(span, dtype=jnp.int32) // per_view
    live = slot_view[None, :] < counts[:, None]
    same = slot_view[:, None] == slot_view[None, :]
    return live[:, None, :] | same[None]


def grid_positions(side, width):
    quarter = width // 4
    rate = 1.0 / 10000.0 ** (jnp.arange(quarter, dtype=jnp.float32) / quarter)
    place = jnp.arange(side * side, dtype=jnp.int32)
    row_pos = (place // side).astype(jnp.float32)
    col_pos = (place % side).astype(jnp.float32)
    row_angle = row_pos[:, None] * rate[None, :]
    col_angle = col_pos[:, None] * rate[None, :]
    return jnp.concatenate(
        [jnp.sin(row_angle), jnp.cos(row_angle), jnp.sin(col_angle), jnp.cos(col_angle)], axis=1
    )


def score_logits(query_rows, key_rows, allowed):
    scale = 1.0 / math.sqrt(query_rows.shape[-1])
    logits = (
        jnp.einsum("elhd,emhd->ehlm", query_rows, key_rows, preferred_element_type=jnp.float32)
        * scale
    )
    return jnp.where(allowed[:, None], logits, MASK_FILL)


def pair_layout(targets, peers, room):
    view_count = targets.shape[0]
    same = targets[:, None] == targets[None, :]
    earlier = jnp.arange(view_count)[None, :] < jnp.arange(view_count)[:, None]
    rank = jnp.sum((same & earlier).astype(jnp.int32), axis=1)
    position = targets * room + rank
    return jnp.arange(peers * room, dtype=jnp.int32)[:, None] == position[None, :]


def lamb_terms(grad, moment, square, weight, factor):
    clipped = grad * factor
    moment_new = BETA_ONE * moment + (1.0 - BETA_ONE) * clipped
    square_new = BETA_TWO * square + (1.0 - BETA_TWO) * clipped * clipped
    direction = moment_new / (jnp.sqrt(square_new) + ADAM_EPS) + DECAY_RATE * weight
    return (clipped, moment_new, square_new, direction)


def per_device(
    tokens,
    counts,
    visible,
    dest_device,
    dest_slot,
    cotangent,
    weight_inproj,
    moment_inproj,
    square_inproj,
    weight_outproj,
    moment_outproj,
    square_outproj,
    weight_expand,
    moment_expand,
    square_expand,
    weight_shrink,
    moment_shrink,
    square_shrink,
    weight_embedder,
    moment_embedder,
    square_embedder,
    weight_lnparams,
    moment_lnparams,
    square_lnparams,
    weight_decparams,
    moment_decparams,
    square_decparams,
):
    masters = (
        weight_inproj,
        weight_outproj,
        weight_expand,
        weight_shrink,
        weight_embedder,
        weight_lnparams,
        weight_decparams,
    )
    moments = (
        moment_inproj,
        moment_outproj,
        moment_expand,
        moment_shrink,
        moment_embedder,
        moment_lnparams,
        moment_decparams,
    )
    squares = (
        square_inproj,
        square_outproj,
        square_expand,
        square_shrink,
        square_embedder,
        square_lnparams,
        square_decparams,
    )
    in_weight, out_weight, up_weight, down_weight, embed_weight, norm_gains, dec_small = (
        lax.all_gather(weight_inproj.astype(jnp.bfloat16), "dp", axis=0, tiled=True),
        lax.all_gather(weight_outproj.astype(jnp.bfloat16), "dp", axis=1, tiled=True),
        lax.all_gather(weight_expand.astype(jnp.bfloat16), "dp", axis=0, tiled=True),
        lax.all_gather(weight_shrink.astype(jnp.bfloat16), "dp", axis=1, tiled=True),
        lax.all_gather(weight_embedder.astype(jnp.bfloat16), "dp", axis=0, tiled=True),
        lax.all_gather(weight_lnparams.astype(jnp.bfloat16), "dp", axis=1, tiled=True),
        lax.all_gather(weight_decparams.astype(jnp.bfloat16), "dp", axis=2, tiled=True),
    )
    model_width = tokens.shape[1]
    row_count = tokens.shape[0]
    view_count = visible.shape[0]
    per_view = visible.shape[1]
    episode_count = counts.shape[0]
    views_each = view_count // episode_count
    span = views_each * per_view
    grid_cells = cotangent.shape[1]
    dec_part = cotangent.shape[2]
    part_model = in_weight.shape[2]
    heads_here = part_model // HEADDIM
    mp_index = lax.axis_index("mp")
    peers = lax.axis_size("dp")
    room = (view_count + peers - 1) // peers
    gains = norm_gains.astype(jnp.float32)
    dec_bias = dec_small[0, 0].astype(jnp.float32)
    mask_token = dec_small[1, 0].astype(jnp.float32)
    inputs = tokens.astype(jnp.float32)
    normed_one, inverse_one = layer_norm(inputs)
    first_low = (normed_one * gains[0] + gains[1]).astype(jnp.bfloat16)
    packed = jnp.dot(
        first_low,
        in_weight.reshape(model_width, 3 * part_model),
        preferred_element_type=jnp.float32,
    ).astype(jnp.bfloat16)
    packed = packed.reshape(episode_count, span, 3, heads_here, HEADDIM)
    query_rows = packed[:, :, 0]
    key_rows = packed[:, :, 1]
    value_rows = packed[:, :, 2]
    allowed = allowed_mask(counts, span, per_view)
    logits = score_logits(query_rows, key_rows, allowed)
    row_top = jnp.max(logits, axis=-1, keepdims=True)
    exponent = jnp.exp(logits - row_top)
    row_total = jnp.sum(exponent, axis=-1, keepdims=True)
    probs_low = (exponent / row_total).astype(jnp.bfloat16)
    logsum = row_top + jnp.log(row_total)
    attended = jnp.einsum(
        "ehlm,emhd->elhd", probs_low, value_rows, preferred_element_type=jnp.float32
    )
    attended_low = attended.reshape(row_count, part_model).astype(jnp.bfloat16)
    attn_out = lax.psum(
        jnp.dot(attended_low, out_weight, preferred_element_type=jnp.float32).astype(jnp.bfloat16),
        "mp",
    ).astype(jnp.float32)
    middle = inputs + attn_out
    normed_two, inverse_two = layer_norm(middle)
    second_low = (normed_two * gains[2] + gains[3]).astype(jnp.bfloat16)
    hidden_pre = jnp.dot(second_low, up_weight, preferred_element_type=jnp.float32)
    hidden_low = gelu_exact(hidden_pre).astype(jnp.bfloat16)
    mlp_out = lax.psum(
        jnp.dot(hidden_low, down_weight, preferred_element_type=jnp.float32).astype(jnp.bfloat16),
        "mp",
    ).astype(jnp.float32)
    final_low = (middle + mlp_out).astype(jnp.bfloat16)
    live_view = (
        jnp.arange(view_count, dtype=jnp.int32) % views_each < jnp.repeat(counts, views_each)
    ).astype(jnp.int32)
    layout = pair_layout(dest_device, peers, room)
    layout_low = layout.astype(jnp.bfloat16)
    details = jnp.concatenate(
        [jnp.ones((view_count, 1), jnp.int32), dest_slot[:, None], live_view[:, None], visible],
        axis=1,
    )
    sent_details = jnp.dot(layout.astype(jnp.int32), details)
    embedded = (
        jnp.dot(final_low, embed_weight, preferred_element_type=jnp.float32) + dec_bias
    ).astype(jnp.bfloat16)
    outgoing = (
        jnp.dot(
            layout_low,
            embedded.reshape(view_count, per_view * dec_part),
            preferred_element_type=jnp.float32,
        )
        .astype(jnp.bfloat16)
        .reshape(peers * room, per_view, dec_part)
    )
    arrived, got_details = (
        lax.all_to_all(outgoing, "dp", split_axis=0, concat_axis=0, tiled=True),
        lax.all_to_all(sent_details, "dp", split_axis=0, concat_axis=0, tiled=True),
    )
    by_slot = (got_details[:, 1][None, :] == jnp.arange(view_count, dtype=jnp.int32)[:, None]) & (
        got_details[:, 0][None, :] > 0
    )
    pick_low = by_slot.astype(jnp.bfloat16)
    pick_int = by_slot.astype(jnp.int32)
    owned = (
        jnp.dot(pick_low, arrived.reshape(peers * room, -1), preferred_element_type=jnp.float32)
        .astype(jnp.bfloat16)
        .reshape(view_count, per_view, -1)
    )
    owned_live = jnp.dot(pick_int, got_details[:, 2]).astype(jnp.float32)
    owned_visible = jnp.dot(pick_int, got_details[:, 3:])
    place = (
        owned_visible[:, None, :] == jnp.arange(grid_cells, dtype=jnp.int32)[None, :, None]
    ).astype(jnp.bfloat16)
    covered = jnp.sum(place.astype(jnp.float32), axis=2)
    spread_rows = jnp.einsum("vgi,viw->vgw", place, owned, preferred_element_type=jnp.float32)
    side = math.isqrt(grid_cells)
    positions = lax.dynamic_slice_in_dim(
        grid_positions(side, dec_part * lax.axis_size("mp")), mp_index * dec_part, dec_part, 1
    )
    decoded = (
        owned_live[:, None, None] * (spread_rows + (1.0 - covered)[:, :, None] * mask_token)
        + positions[None]
    ).astype(jnp.bfloat16)
    owned_grad = (
        jnp.einsum("vgi,vgw->viw", place, cotangent, preferred_element_type=jnp.float32)
        * owned_live[:, None, None]
    ).astype(jnp.bfloat16)
    masked_cells = ((1.0 - covered) * owned_live[:, None]).astype(jnp.bfloat16)
    grad_mask = jnp.einsum("vg,vgw->w", masked_cells, cotangent, preferred_element_type=jnp.float32)
    grad_bias = jnp.sum(owned_grad.astype(jnp.float32), axis=(0, 1))
    returned = (
        jnp.einsum(
            "vp,vx->px",
            pick_low,
            owned_grad.reshape(view_count, -1),
            preferred_element_type=jnp.float32,
        )
        .astype(jnp.bfloat16)
        .reshape(peers * room, per_view, dec_part)
    )
    came_back = lax.all_to_all(returned, "dp", split_axis=0, concat_axis=0, tiled=True)
    embed_rows_grad = (
        jnp.einsum(
            "pv,px->vx",
            layout_low,
            came_back.reshape(peers * room, -1),
            preferred_element_type=jnp.float32,
        )
        .astype(jnp.bfloat16)
        .reshape(row_count, dec_part)
    )
    grad_embed = jnp.einsum(
        "tm,tw->mw", final_low, embed_rows_grad, preferred_element_type=jnp.float32
    )
    partial_final = jnp.einsum(
        "tw,mw->tm", embed_rows_grad, embed_weight, preferred_element_type=jnp.float32
    )
    grad_final = lax.psum(partial_final.astype(jnp.bfloat16), "mp").astype(jnp.float32)
    grad_mlp_low = grad_final.astype(jnp.bfloat16)
    grad_shrink = jnp.einsum(
        "tf,tm->fm", hidden_low, grad_mlp_low, preferred_element_type=jnp.float32
    )
    grad_hidden = jnp.einsum(
        "tm,fm->tf", grad_mlp_low, down_weight, preferred_element_type=jnp.float32
    )
    grad_pre = (grad_hidden * gelu_slope(hidden_pre)).astype(jnp.bfloat16)
    grad_expand = jnp.einsum("tm,tf->mf", second_low, grad_pre, preferred_element_type=jnp.float32)
    grad_dec = jnp.stack([grad_bias, grad_mask])[:, None, :]
    grad_second = lax.psum(
        jnp.einsum("tf,mf->tm", grad_pre, up_weight, preferred_element_type=jnp.float32).astype(
            jnp.bfloat16
        ),
        "mp",
    ).astype(jnp.float32)
    gain_two = jnp.sum(grad_second * normed_two, axis=0)
    bias_two = jnp.sum(grad_second, axis=0)
    grad_middle = grad_final + norm_back(grad_second, normed_two, inverse_two, gains[2])
    grad_attn_low = grad_middle.astype(jnp.bfloat16)
    grad_outproj = jnp.einsum(
        "tc,tm->cm", attended_low, grad_attn_low, preferred_element_type=jnp.float32
    )
    grad_att = jnp.einsum(
        "tm,cm->tc", grad_attn_low, out_weight, preferred_element_type=jnp.float32
    ).astype(jnp.bfloat16)
    grad_att = grad_att.reshape(episode_count, span, heads_here, HEADDIM)
    probs = jnp.exp(score_logits(query_rows, key_rows, allowed) - logsum)
    probs_again = probs.astype(jnp.bfloat16)
    grad_probs = jnp.einsum(
        "elhd,emhd->ehlm", grad_att, value_rows, preferred_element_type=jnp.float32
    )
    centre = jnp.sum(probs * grad_probs, axis=-1, keepdims=True)
    grad_scores = (probs * (grad_probs - centre) * (1.0 / math.sqrt(HEADDIM))).astype(jnp.bfloat16)
    grad_query = jnp.einsum(
        "ehlm,emhd->elhd", grad_scores, key_rows, preferred_element_type=jnp.float32
    ).astype(jnp.bfloat16)
    grad_keys = jnp.einsum(
        "ehlm,elhd->emhd", grad_scores, query_rows, preferred_element_type=jnp.float32
    ).astype(jnp.bfloat16)
    grad_values = jnp.einsum(
        "ehlm,elhd->emhd", probs_again, grad_att, preferred_element_type=jnp.float32
    ).astype(jnp.bfloat16)
    grad_packed = jnp.stack([grad_query, grad_keys, grad_values], axis=2).reshape(
        row_count, 3 * part_model
    )
    grad_inproj = jnp.einsum(
        "tm,tc->mc", first_low, grad_packed, preferred_element_type=jnp.float32
    ).reshape(model_width, 3, part_model)
    grad_first = lax.psum(
        jnp.einsum(
            "tc,mc->tm",
            grad_packed,
            in_weight.reshape(model_width, 3 * part_model),
            preferred_element_type=jnp.float32,
        ).astype(jnp.bfloat16),
        "mp",
    ).astype(jnp.float32)
    gain_one = jnp.sum(grad_first * normed_one, axis=0)
    bias_one = jnp.sum(grad_first, axis=0)
    grad_inputs = grad_middle + norm_back(grad_first, normed_one, inverse_one, gains[0])
    grad_norms = jnp.stack([gain_one, bias_one, gain_two, bias_two])
    reduced = (
        lax.psum_scatter(grad_inproj, "dp", scatter_dimension=0, tiled=True),
        lax.psum_scatter(grad_outproj, "dp", scatter_dimension=1, tiled=True),
        lax.psum_scatter(grad_expand, "dp", scatter_dimension=0, tiled=True),
        lax.psum_scatter(grad_shrink, "dp", scatter_dimension=1, tiled=True),
        lax.psum_scatter(grad_embed, "dp", scatter_dimension=0, tiled=True),
        lax.psum_scatter(grad_norms, "dp", scatter_dimension=1, tiled=True),
        lax.psum_scatter(grad_dec, "dp", scatter_dimension=2, tiled=True),
    )
    single_copy = (mp_index == 0).astype(jnp.float32)
    weights_each = [1.0, 1.0, 1.0, 1.0, 1.0, single_copy, 1.0]
    grad_sq = jnp.stack(
        [jnp.sum(reduced[index] * reduced[index]) * weights_each[index] for index in range(7)]
    )
    weight_sq = jnp.stack(
        [jnp.sum(masters[index] * masters[index]) * weights_each[index] for index in range(7)]
    )
    grad_total, weight_total = lax.psum((grad_sq, weight_sq), ("dp", "mp"))
    clip_norm = jnp.sqrt(jnp.sum(grad_total))
    factor = jnp.minimum(1.0, 0.5 * math.sqrt(PARAMS) / clip_norm)
    pieces = [
        lamb_terms(reduced[index], moments[index], squares[index], masters[index], factor)
        for index in range(7)
    ]
    update_sq = jnp.stack(
        [jnp.sum(pieces[index][3] * pieces[index][3]) * weights_each[index] for index in range(7)]
    )
    update_total = lax.psum(update_sq, ("dp", "mp"))
    weight_norm = jnp.sqrt(weight_total)
    update_norm = jnp.sqrt(update_total)
    ratio = weight_norm / (update_norm + TRUST_EPS)
    res = []
    for index in range(7):
        updated = masters[index] - LEARN_RATE * ratio[index] * pieces[index][3]
        res.extend(
            [
                pieces[index][0],
                pieces[index][1],
                pieces[index][2],
                updated,
                updated.astype(jnp.bfloat16),
            ]
        )
    return (
        decoded,
        grad_inputs.astype(jnp.bfloat16),
        clip_norm.reshape(1),
        jnp.stack([weight_norm, update_norm]),
        res[0],
        res[1],
        res[2],
        res[3],
        res[4],
        res[5],
        res[6],
        res[7],
        res[8],
        res[9],
        res[10],
        res[11],
        res[12],
        res[13],
        res[14],
        res[15],
        res[16],
        res[17],
        res[18],
        res[19],
        res[20],
        res[21],
        res[22],
        res[23],
        res[24],
        res[25],
        res[26],
        res[27],
        res[28],
        res[29],
        res[30],
        res[31],
        res[32],
        res[33],
        res[34],
    )


def solution(mesh):
    in_specs = (
        P("dp", None),
        P("dp"),
        P("dp", None),
        P("dp"),
        P("dp"),
        P("dp", None, "mp"),
        P("dp", None, "mp"),
        P("dp", None, "mp"),
        P("dp", None, "mp"),
        P("mp", "dp"),
        P("mp", "dp"),
        P("mp", "dp"),
        P("dp", "mp"),
        P("dp", "mp"),
        P("dp", "mp"),
        P("mp", "dp"),
        P("mp", "dp"),
        P("mp", "dp"),
        P("dp", "mp"),
        P("dp", "mp"),
        P("dp", "mp"),
        P(None, "dp"),
        P(None, "dp"),
        P(None, "dp"),
        P(None, "mp", "dp"),
        P(None, "mp", "dp"),
        P(None, "mp", "dp"),
    )
    out_specs = (
        P("dp", None, "mp"),
        P("dp", None),
        P(),
        P(),
        P("dp", None, "mp"),
        P("dp", None, "mp"),
        P("dp", None, "mp"),
        P("dp", None, "mp"),
        P("dp", None, "mp"),
        P("mp", "dp"),
        P("mp", "dp"),
        P("mp", "dp"),
        P("mp", "dp"),
        P("mp", "dp"),
        P("dp", "mp"),
        P("dp", "mp"),
        P("dp", "mp"),
        P("dp", "mp"),
        P("dp", "mp"),
        P("mp", "dp"),
        P("mp", "dp"),
        P("mp", "dp"),
        P("mp", "dp"),
        P("mp", "dp"),
        P("dp", "mp"),
        P("dp", "mp"),
        P("dp", "mp"),
        P("dp", "mp"),
        P("dp", "mp"),
        P(None, "dp"),
        P(None, "dp"),
        P(None, "dp"),
        P(None, "dp"),
        P(None, "dp"),
        P(None, "mp", "dp"),
        P(None, "mp", "dp"),
        P(None, "mp", "dp"),
        P(None, "mp", "dp"),
        P(None, "mp", "dp"),
    )
    return jax.shard_map(
        per_device, mesh=mesh, in_specs=in_specs, out_specs=out_specs, check_vma=False
    )
```

profile of v0, /device:TPU:0, one launch (start us, length us, event | category | flops | bytes accessed | tf_op | source)
XLA Modules:
  0.0 1594.5 jit_solution(2399125426496182378)
XLA Ops:
  12.1 8.3 all-to-all-start
  23.5 41.0 %all-gather = bf16[16,48,4]{1,2,0:T(4,128)(2,1)S(1)} all-gather(bf16[1,48,4]{1,2,0:T(4,128)(2,1)S(1)} %get-tuple-element.389), channel_id=1, replica_groups=mesh['dp'=16,'mp'=2] {'dp'}, dimensions={0}, use_global_device_ids=true | all-gather | bytes 6528 | tf_op jit(solution)/shard_map/all_gather | solution.py:155
  79.4 57.5 %all_gather.26 = bf16[768,256]{1,0:T(8,128)(2,1)S(1)} all-gather(bf16[48,256]{1,0:T(8,128)(2,1)S(1)} %convert_element_type.249), channel_id=1, replica_groups=mesh['dp'=16,'mp'=2] {'dp'}, dimensions={0}, use_global_device_ids=true | all-gather | bytes 417792 | tf_op jit(solution)/shard_map/all_gather | solution.py:154
  143.6 43.2 %all_gather.23 = bf16[384,768]{0,1:T(8,128)(2,1)} all-gather(bf16[384,48]{0,1:T(8,128)(2,1)S(1)} %convert_element_type.239), channel_id=1, replica_groups=mesh['dp'=16,'mp'=2] {'dp'}, dimensions={1}, use_global_device_ids=true | all-gather | bytes 626688 | tf_op jit(solution)/shard_map/all_gather | solution.py:151
  196.4 10.4 convolution_convert_fusion.4
  206.8 16.9 %reshape.386 = bf16[12,196,3,6,64]{4,3,2,1,0:T(8,128)(2,1)} reshape(bf16[2352,1152]{1,0:T(8,128)(2,1)} %convolution_convert_fusion.4) | data formatting | bytes 10838016 | tf_op jit(solution)/shard_map/reshape | solution.py:183
  223.7 11.2 fusion.155
  239.9 6.9 copy.234
  246.8 6.5 copy.235
  253.3 10.7 fusion.157
  264.0 8.5 fusion.10
  272.5 8.1 convert_bitcast_fusion.3
  287.3 5.6 convolution_convert_fusion.9
  294.5 28.6 %all-reduce.11.cloned.1.call-done = (bf16[2352,768]{1,0:T(8,128)(2,1)}, bf16[2352,768]{1,0:T(8,128)(2,1)}) async-done(((bf16[2352,768]{1,0:T(8,128)(2,1)}, bf16[2352,768]{1,0:T(8,128)(2,1)}), (bf16[2352,768]{1,0:T(8,128)(2,1)}, bf16[2352,768]{1,0:T(8,128)(2,1)})) %all-reduce.11.cloned.1.call-update) | async-done | bytes 7225360 | tf_op jit(solution)/shard_map/psum | solution.py:198
  329.9 60.1 %all-gather.7.cloned.1.call-done = bf16[768,1536]{1,0:T(8,128)(2,1)} async-done(((bf16[48,1536]{1,0:T(8,128)(2,1)}), bf16[768,1536]{1,0:T(8,128)(2,1)}) %all-gather.7.cloned.1.call-update) | async-done | bytes 2359312 | tf_op jit(solution)/shard_map/all_gather | solution.py:152
  389.9 13.6 multiply_convert_fusion.1
  403.5 50.8 %all-gather.9.cloned.1.call-done = bf16[1536,768]{0,1:T(8,128)(2,1)} async-done(((bf16[1536,48]{0,1:T(8,128)(2,1)}), bf16[1536,768]{0,1:T(8,128)(2,1)}) %all-gather.9.cloned.1.call-update) | async-done | bytes 2359312 | tf_op jit(solution)/shard_map/all_gather | solution.py:153
  454.3 12.3 fusion.9
  469.5 7.3 convolution_convert_fusion.6
  483.0 17.0 %all-reduce.7.cloned.1.call-done = bf16[2352,768]{1,0:T(8,128)(2,1)} async-done(((bf16[2352,768]{1,0:T(8,128)(2,1)}), bf16[2352,768]{1,0:T(8,128)(2,1)}) %all-reduce.7.cloned.1.call-update) | async-done | bytes 3612688 | tf_op jit(solution)/shard_map/psum | solution.py:308
  500.0 8.4 fusion.50
  508.5 5.8 fusion.48
  520.5 11.4 fusion.158
  532.1 12.4 fusion.86
  559.5 9.0 fusion.63
  568.4 25.3 %convert_bitcast_fusion.1 = bf16[12,196,1,6,64]{1,4,3,0,2:T(8,128)(2,1)} fusion(f32[12,6,196,196]{2,3,1,0:T(8,128)} %fusion.63, f32[12,6,196,196]{2,3,1,0:T(8,128)} %get-tuple-element.408, f32[12,6,196]{2,1,0:T(8,128)S(1)} %log_add_fusion, bf16[12,196,1,6,64]{1,4,3,0,2:T(8,128)(2,1)} %copy.234), kind=kOutput, calls=%fused_computation.98 | convolution fusion | flops 374320992 | bytes 25796736 | tf_op jit(solution)/shard_map/ehlm,elhd->emhd/dot_general | solution.py:335
  593.8 25.4 %convert_bitcast_fusion.2 = bf16[12,196,1,6,64]{1,4,3,0,2:T(8,128)(2,1)} fusion(f32[12,6,196,196]{2,3,1,0:T(8,128)} %fusion.63, f32[12,6,196,196]{2,3,1,0:T(8,128)} %get-tuple-element.408, f32[12,6,196]{2,1,0:T(8,128)S(1)} %log_add_fusion, bf16[12,196,1,6,64]{1,4,3,0,2:T(8,128)(2,1)} %copy.235), kind=kOutput, calls=%fused_computation.99 | convolution fusion | flops 374320992 | bytes 25796736 | tf_op jit(solution)/shard_map/ehlm,emhd->elhd/dot_general | solution.py:332
  619.2 7.9 convert_bitcast_fusion
  627.1 6.1 pad_maximum_fusion
  633.2 12.1 copy.214
  645.4 15.5 reshape.369
  661.0 11.8 fusion.56
  672.8 10.3 convolution_convert_fusion.8
  683.1 9.1 convolution_convert_fusion.5
  693.7 42.0 %all_gather.27 = bf16[2,1,256]{1,0,2:T(2,128)(2,1)S(1)} all-gather(bf16[2,1,16]{1,0,2:T(2,128)(2,1)S(1)} %copy.206), channel_id=1, replica_groups=mesh['dp'=16,'mp'=2] {'dp'}, dimensions={2}, use_global_device_ids=true | all-gather | bytes 1088 | tf_op jit(solution)/shard_map/all_gather | solution.py:156
  742.0 106.5 %reduce-scatter.18.cloned.1.call-done = f32[1536,48]{0,1:T(8,128)} async-done(((f32[1536,768]{0,1:T(8,128)}), f32[1536,48]{0,1:T(8,128)}) %reduce-scatter.18.cloned.1.call-update) | async-done | bytes 294928 | tf_op jit(solution)/shard_map/reduce_scatter | solution.py:364
  850.1 140.2 %reduce-scatter.16.cloned.1.call-done = f32[48,1536]{1,0:T(8,128)} async-done(((f32[768,1536]{1,0:T(8,128)}), f32[48,1536]{1,0:T(8,128)}) %reduce-scatter.16.cloned.1.call-update) | async-done | bytes 294928 | tf_op jit(solution)/shard_map/reduce_scatter | solution.py:363
  992.0 137.7 %reduce-scatter.12.cloned.1.call-done = f32[48,3,384]{2,0,1:T(8,128)} async-done(((f32[768,3,384]{2,0,1:T(8,128)}), f32[48,3,384]{2,0,1:T(8,128)}) %reduce-scatter.12.cloned.1.call-update) | async-done | bytes 221200 | tf_op jit(solution)/shard_map/reduce_scatter | solution.py:361
  1131.3 34.8 %all-reduce.9.cloned.1.call-done = (bf16[2352,768]{1,0:T(8,128)(2,1)}, bf16[2352,768]{1,0:T(8,128)(2,1)}) async-done(((bf16[2352,768]{1,0:T(8,128)(2,1)}, bf16[2352,768]{1,0:T(8,128)(2,1)}), (bf16[2352,768]{1,0:T(8,128)(2,1)}, bf16[2352,768]{1,0:T(8,128)(2,1)})) %all-reduce.9.cloned.1.call-update) | async-done | bytes 7225360 | tf_op jit(solution)/shard_map/psum | solution.py:207
  1166.1 7.0 fusion.51
  1174.2 6.6 fusion.138
  1180.8 5.8 fusion.55
  1191.4 105.7 %reduce-scatter.22.cloned.1.call-done = f32[48,4]{1,0:T(8,128)} async-done(((f32[768,4]{1,0:T(8,128)}), f32[48,4]{1,0:T(8,128)}) %reduce-scatter.22.cloned.1.call-update) | async-done | bytes 784
  1299.2 124.5 %reduce-scatter.20.cloned.1.call-done = f32[48,256]{1,0:T(8,128)} async-done(((f32[768,256]{1,0:T(8,128)}), f32[48,256]{1,0:T(8,128)}) %reduce-scatter.20.cloned.1.call-update) | async-done | bytes 49168 | tf_op jit(solution)/shard_map/reduce_scatter | solution.py:365
  1433.8 52.2 %psum.61 = f32[7]{0:T(128)S(1)} all-reduce(f32[7]{0:T(128)S(1)} %stack.136), channel_id=1, replica_groups=mesh['dp'=16,'mp'=2] {'dp','mp'}, use_global_device_ids=true, to_apply=%region_37.38 | all-reduce | flops 7 | bytes 56 | tf_op jit(solution)/shard_map/psum | solution.py:377
  1513.4 8.7 fusion.43
  1522.1 38.8 %all-reduce = (f32[7]{0:T(128)S(1)}, f32[7]{0:T(128)S(1)}) all-reduce(f32[7]{0:T(128)} %stack.153, f32[7]{0:T(128)} %stack.144), channel_id=1, replica_groups=mesh['dp'=16,'mp'=2] {'dp','mp'}, use_global_device_ids=true, to_apply=%region_54.55 | all-reduce | flops 14 | bytes 112 | tf_op jit(solution)/shard_map/psum | solution.py:387
  1577.9 5.6 add_convert_fusion
  (264 shorter events, 159.9 us)
Async XLA Ops:
  8.8 178.2 %copy-start.43 = (s32[48]{0:T(128)}, s32[48]{0:T(128)S(1)}, u32[]{:S(2)}) copy-start(s32[48]{0:T(128)S(1)} %multiply_add_fusion.14) | copy-start | bytes 580
  12.1 54.8 %all-to-all-start = ((s32[16,1,156]{2,1,0:T(1,128)}), s32[16,1,156]{2,1,0:T(1,128)S(1)}, u32[]{:S(2)}, u32[]{:S(2)}) async-start(s32[16,1,156]{2,1,0:T(1,128)} %reshape.399), calls=%async_computation | async-start | bytes 32768 | tf_op jit(solution)/shard_map/all_to_all | solution.py:236
  20.5 172.1 %all-gather.5.cloned.1.call-start = ((), (), s32[]{:S(2)}) async-start(), calls=%async_computation.10 | async-start | bytes 1880064 | tf_op jit(solution)/shard_map/all_gather | solution.py:150
  64.6 131.8 %copy-start.36 = (f32[768]{0:T(1024)}, f32[768]{0:T(1024)S(1)}, u32[]{:S(2)}) copy-start(f32[768]{0:T(1024)S(1)} %get-tuple-element.334) | copy-start | bytes 9220
  64.6 131.7 %copy-start.45 = (f32[768]{0:T(1024)}, f32[768]{0:T(1024)S(1)}, u32[]{:S(2)}) copy-start(f32[768]{0:T(1024)S(1)} %get-tuple-element.337) | copy-start | bytes 9220
  68.8 408.1 %copy-start.33 = (s32[48,49]{1,0:T(8,128)}, s32[48,49]{1,0:T(8,128)S(1)}, u32[]{:S(2)}) copy-start(s32[48,49]{1,0:T(8,128)S(1)} %fusion.99) | copy-start | bytes 28228
  68.9 408.8 %copy-start.51 = (f32[48]{0:T(128)}, f32[48]{0:T(128)S(1)}, u32[]{:S(2)}) copy-start(f32[48]{0:T(128)S(1)} %fusion.85) | copy-start | bytes 580
  73.4 63.5 %copy-start.49 = (s32[12]{0:T(128)S(1)}, s32[12]{0:T(128)}, u32[]{:S(2)}) copy-start(s32[12]{0:T(128)} %param.28) | copy-start | bytes 148
  75.7 111.0 %all-to-all-start.2 = ((bf16[48,49,256]{2,1,0:T(8,128)(2,1)}), bf16[48,49,256]{2,1,0:T(8,128)(2,1)S(1)}, u32[]{:S(2)}, u32[]{:S(2)}) async-start(bf16[48,49,256]{2,1,0:T(8,128)(2,1)} %reshape.365), calls=%async_computation.2 | async-start | bytes 2752512 | tf_op jit(solution)/shard_map/all_to_all | solution.py:280
  79.4 243.6 %all-reduce.11.cloned.1.call-start = ((), (), s32[]{:S(2)}) async-start(), calls=%async_computation.22 | async-start | bytes 14450688 | tf_op jit(solution)/shard_map/psum | solution.py:198
  136.9 52.5 %copy-start.18 = (bf16[768,256]{1,0:T(8,128)(2,1)}, bf16[768,256]{1,0:T(8,128)(2,1)S(1)}, u32[]{:S(2)}) copy-start(bf16[768,256]{1,0:T(8,128)(2,1)S(1)} %all_gather.26) | copy-start | bytes 1179652
  139.7 56.7 %copy-start.29 = (f32[2352]{0:T(1024)}, f32[2352]{0:T(1024)S(1)}, u32[]{:S(2)}) copy-start(f32[2352]{0:T(1024)S(1)} %broadcast_multiply_fusion.10) | copy-start | bytes 28228
  142.9 53.5 %copy-start.31 = (f32[2352]{0:T(1024)}, f32[2352]{0:T(1024)S(1)}, u32[]{:S(2)}) copy-start(f32[2352]{0:T(1024)S(1)} %add_rsqrt_fusion.1) | copy-start | bytes 28228
  189.5 17.3 %copy-start.7 = (bf16[2352,256]{1,0:T(8,128)(2,1)}, bf16[2352,256]{1,0:T(8,128)(2,1)S(1)}, u32[]{:S(2)}) copy-start(bf16[2352,256]{1,0:T(8,128)(2,1)S(1)} %reshape.367) | copy-start | bytes 3612676
  239.9 32.6 %copy-start.6 = (bf16[12,196,1,6,64]{1,4,3,0,2:T(8,128)(2,1)}, bf16[12,196,1,6,64]{1,4,3,0,2:T(8,128)(2,1)S(1)}, u32[]{:S(2)}) copy-start(bf16[12,196,1,6,64]{1,4,3,0,2:T(8,128)(2,1)S(1)} %copy.233) | copy-start | bytes 5419012
  292.9 97.0 %all-gather.7.cloned.1.call-start = ((), (), s32[]{:S(2)}) async-start(), calls=%async_computation.11 | async-start | bytes 2506752 | tf_op jit(solution)/shard_map/all_gather | solution.py:152
  293.7 160.7 %all-gather.9.cloned.1.call-start = ((), (), s32[]{:S(2)}) async-start(), calls=%async_computation.12 | async-start | bytes 2506752 | tf_op jit(solution)/shard_map/all_gather | solution.py:153
  294.4 205.6 %all-reduce.7.cloned.1.call-start = ((), (), s32[]{:S(2)}) async-start(), calls=%async_computation.13 | async-start | bytes 7225344 | tf_op jit(solution)/shard_map/psum | solution.py:308
  476.8 262.1 %reduce-scatter.24.cloned.1.call-start = ((), (), s32[]{:S(2)}) async-start(), calls=%async_computation.20 | async-start | bytes 139264
  483.0 257.5 %reduce-scatter.14.cloned.1.call-start = ((), (), s32[]{:S(2)}) async-start(), calls=%async_computation.15 | async-start | bytes 1253376 | tf_op jit(solution)/shard_map/reduce_scatter | solution.py:362
  520.5 328.0 %reduce-scatter.18.cloned.1.call-start = ((), (), s32[]{:S(2)}) async-start(), calls=%async_computation.17 | async-start | bytes 5013504 | tf_op jit(solution)/shard_map/reduce_scatter | solution.py:364
  532.0 458.3 %reduce-scatter.16.cloned.1.call-start = ((), (), s32[]{:S(2)}) async-start(), calls=%async_computation.16 | async-start | bytes 5013504 | tf_op jit(solution)/shard_map/reduce_scatter | solution.py:363
  544.5 585.1 %reduce-scatter.12.cloned.1.call-start = ((), (), s32[]{:S(2)}) async-start(), calls=%async_computation.14 | async-start | bytes 3760128 | tf_op jit(solution)/shard_map/reduce_scatter | solution.py:361
  645.4 15.6 copy-start.37
  645.4 15.6 copy-start.46
  672.8 493.3 %all-reduce.9.cloned.1.call-start = ((), (), s32[]{:S(2)}) async-start(), calls=%async_computation.21 | async-start | bytes 14450688 | tf_op jit(solution)/shard_map/psum | solution.py:207
  692.3 43.4 %copy-start.44 = (f32[196]{0:T(256)S(1)}, f32[196]{0:T(256)}, u32[]{:S(2)}) copy-start(f32[196]{0:T(256)} %get-tuple-element.414) | copy-start | bytes 2356
  692.3 481.9 %copy-start.8 = (bf16[2352,256]{1,0:T(8,128)(2,1)S(1)}, bf16[2352,256]{1,0:T(8,128)(2,1)}, u32[]{:S(2)}) copy-start(bf16[2352,256]{1,0:T(8,128)(2,1)} %copy-done.7) | copy-start | bytes 3612676
  692.3 604.8 %reduce-scatter.22.cloned.1.call-start = ((), (), s32[]{:S(2)}) async-start(), calls=%async_computation.19 | async-start | bytes 417792
  739.8 426.3 %copy-start.47 = (f32[2,1,16]{2,1,0:T(1,128)}, f32[2,1,16]{2,1,0:T(1,128)S(1)}, u32[]{:S(2)}) copy-start(f32[2,1,16]{2,1,0:T(1,128)S(1)} %copy.227) | copy-start | bytes 388
  1174.1 249.6 %reduce-scatter.20.cloned.1.call-start = ((), (), s32[]{:S(2)}) async-start(), calls=%async_computation.18 | async-start | bytes 835584 | tf_op jit(solution)/shard_map/reduce_scatter | solution.py:365
  1186.7 309.6 %copy-start.15 = (f32[48,3,384]{2,0,1:T(8,128)S(1)}, f32[48,3,384]{2,0,1:T(8,128)}, u32[]{:S(2)}) copy-start(f32[48,3,384]{2,0,1:T(8,128)} %param.33) | copy-start | bytes 663556
  1186.7 312.2 %copy-start.10 = (f32[1536,48]{0,1:T(8,128)S(1)}, f32[1536,48]{0,1:T(8,128)}, u32[]{:S(2)}) copy-start(f32[1536,48]{0,1:T(8,128)} %param.42) | copy-start | bytes 884740
  1186.7 312.2 %copy-start.20 = (f32[1536,48]{0,1:T(8,128)S(1)}, f32[1536,48]{0,1:T(8,128)}, u32[]{:S(2)}) copy-start(f32[1536,48]{0,1:T(8,128)} %reduce-scatter.18.cloned.1.call-done) | copy-start | bytes 884740
  1186.7 314.8 %copy-start.12 = (f32[48,1536]{1,0:T(8,128)S(1)}, f32[48,1536]{1,0:T(8,128)}, u32[]{:S(2)}) copy-start(f32[48,1536]{1,0:T(8,128)} %param.39) | copy-start | bytes 884740
  1189.2 312.3 %copy-start.21 = (f32[48,1536]{1,0:T(8,128)S(1)}, f32[48,1536]{1,0:T(8,128)}, u32[]{:S(2)}) copy-start(f32[48,1536]{1,0:T(8,128)} %reduce-scatter.16.cloned.1.call-done) | copy-start | bytes 884740
  1429.1 147.3 %all-to-all-start.1 = ((bf16[48,49,256]{2,1,0:T(8,128)(2,1)}), bf16[48,49,256]{2,1,0:T(8,128)(2,1)S(1)}, u32[]{:S(2)}, u32[]{:S(2)}) async-start(bf16[48,49,256]{2,1,0:T(8,128)(2,1)} %reshape.361), calls=%async_computation.1 | async-start | bytes 2752512 | tf_op jit(solution)/shard_map/all_to_all | solution.py:235
  1501.5 73.1 %copy-start.22 = (f32[1536,48]{0,1:T(8,128)}, f32[1536,48]{0,1:T(8,128)S(1)}, u32[]{:S(2)}) copy-start(f32[1536,48]{0,1:T(8,128)S(1)} %get-tuple-element.371) | copy-start | bytes 884740
  1501.5 73.1 %copy-start.23 = (f32[1536,48]{0,1:T(8,128)}, f32[1536,48]{0,1:T(8,128)S(1)}, u32[]{:S(2)}) copy-start(f32[1536,48]{0,1:T(8,128)S(1)} %get-tuple-element.372) | copy-start | bytes 884740
  1504.4 71.1 %copy-start.24 = (f32[48,1536]{1,0:T(8,128)}, f32[48,1536]{1,0:T(8,128)S(1)}, u32[]{:S(2)}) copy-start(f32[48,1536]{1,0:T(8,128)S(1)} %get-tuple-element.374) | copy-start | bytes 884740
  1513.4 55.0 %copy-start.38 = (f32[4,48]{1,0:T(4,128)S(1)}, f32[4,48]{1,0:T(4,128)}, u32[]{:S(2)}) copy-start(f32[4,48]{1,0:T(4,128)} %param.48) | copy-start | bytes 2308
  1513.4 56.2 %copy-start.27 = (f32[48,256]{1,0:T(8,128)S(1)}, f32[48,256]{1,0:T(8,128)}, u32[]{:S(2)}) copy-start(f32[48,256]{1,0:T(8,128)} %param.45) | copy-start | bytes 147460
  1513.4 57.7 %copy-start.26 = (f32[384,48]{0,1:T(8,128)S(1)}, f32[384,48]{0,1:T(8,128)}, u32[]{:S(2)}) copy-start(f32[384,48]{0,1:T(8,128)} %param.36) | copy-start | bytes 221188
  1513.4 62.1 %copy-start.25 = (f32[48,1536]{1,0:T(8,128)S(1)}, f32[48,1536]{1,0:T(8,128)}, u32[]{:S(2)}) copy-start(f32[48,1536]{1,0:T(8,128)} %get-tuple-element.375) | copy-start | bytes 884740
  1513.4 63.3 %copy-start.40 = (s32[48]{0:T(128)S(1)}, s32[48]{0:T(128)}, u32[]{:S(2)}) copy-start(s32[48]{0:T(128)} %copy-done.39) | copy-start | bytes 580
  1513.4 63.3 %copy-start.42 = (pred[48,1]{0,1:T(4,128)(4,1)S(1)}, pred[48,1]{0,1:T(4,128)(4,1)}, u32[]{:S(2)}) copy-start(pred[48,1]{0,1:T(4,128)(4,1)} %copy-done.41) | copy-start | bytes 148
  1522.1 55.7 %copy-start.34 = (s32[48,49]{1,0:T(8,128)S(1)}, s32[48,49]{1,0:T(8,128)}, u32[]{:S(2)}) copy-start(s32[48,49]{1,0:T(8,128)} %copy-done.33) | copy-start | bytes 28228
  1522.1 55.7 %copy-start.50 = (f32[256]{0:T(256)S(1)}, f32[256]{0:T(256)}, u32[]{:S(2)}) copy-start(f32[256]{0:T(256)} %get-tuple-element.327) | copy-start | bytes 3076
  (22 other events, 166.2 us)
Sparse Core Ops, SparseCore 0:
  24.6 71.9 all-gather.4
  293.0 29.9 all-reduce.10
  326.4 63.4 all-gather.6
  393.2 61.0 all-gather.8
  477.0 22.9 all-reduce.6
  502.6 77.1 reduce-scatter.23
  585.4 120.6 reduce-scatter.13
  712.0 136.3 reduce-scatter.17
  853.6 136.6 reduce-scatter.15
  996.1 133.5 reduce-scatter.11
  1133.0 33.0 all-reduce.8
  1174.3 122.8 reduce-scatter.21
  1302.4 121.3 reduce-scatter.19
where the time goes:
time: 1600 us; the launch traced here: 1590 us
  waiting for transfers between devices  806 us (50%)
  blocking collectives  275 us (17%)
  matrix products  232 us (14%)
  local copies, waits for them, and re-layouts  134 us (8%)
  other arithmetic  107 us (7%)
  between operations  23.4 us (1%)
  starting transfers between devices  17.3 us (1%)
    reduce_scatter x1, waiting for transfers between devices, per_device(): lax.psum_scatter(grad_expand, 'dp', scatter_dimension=0, tiled=True)  140 us
    reduce_scatter x1, waiting for transfers between devices, per_device(): lax.psum_scatter(grad_inproj, 'dp', scatter_dimension=0, tiled=True)  138 us
    reduce_scatter x1, waiting for transfers between devices, per_device(): lax.psum_scatter(grad_embed, 'dp', scatter_dimension=0, tiled=True)  125 us
    reduce_scatter x1, waiting for transfers between devices, per_device(): lax.psum_scatter(grad_shrink, 'dp', scatter_dimension=1, tiled=True)  107 us
    unnamed x15, waiting for transfers between devices  106 us
    all_gather x1, waiting for transfers between devices, per_device(): lax.all_gather(weight_expand.astype(jnp.bfloat16), 'dp', axis=0, tiled=True)  60.1 us
    all_gather x1, blocking collectives, per_device(): lax.all_gather(weight_embedder.astype(jnp.bfloat16), 'dp', axis=0, tiled=...  57.5 us
    psum x1, blocking collectives, per_device(): grad_total, weight_total = lax.psum((grad_sq, weight_sq), ('dp', 'mp'))  52.2 us
  transfers between devices with their start and end apart: 16, of which 10 were waited for; matrix products, arithmetic and copies ran while one was open for 20% of the time, Pallas kernels for 0%

commit v1 on v0

v1 whole, which is shorter than its diff:
```python
import math

import jax
import jax.numpy as jnp
from jax import lax
from jax.experimental import pallas as pl
from jax.experimental.pallas import tpu as pltpu
from jax.sharding import PartitionSpec as P

HEADDIM = 64
PARAMS = 7475200
NORM_EPS = 1e-06
MASK_FILL = -1e30
BETA_ONE = 0.5
BETA_TWO = 0.5
ADAM_EPS = 1e-06
DECAY_RATE = 0.01
LEARN_RATE = 0.5
TRUST_EPS = 1e-06

F32 = jnp.float32
BF16 = jnp.bfloat16
AXES = ("dp", "mp")
NT = (((1,), (1,)), ((), ()))
TN = (((0,), (0,)), ((), ()))
ROUND = 16
VMEM_BYTES = 58 << 20


def mm(a, b, dims=(((1,), (0,)), ((), ()))):
    return lax.dot_general(a, b, dims, preferred_element_type=F32)


def norm_rows(values):
    centre = values - jnp.mean(values, axis=-1, keepdims=True)
    spread = jnp.mean(centre * centre, axis=-1, keepdims=True)
    inverse = lax.rsqrt(spread + NORM_EPS)
    return centre * inverse, inverse


def norm_back(scaled, normed, inverse):
    return inverse * (
        scaled
        - jnp.mean(scaled, axis=-1, keepdims=True)
        - normed * jnp.mean(scaled * normed, axis=-1, keepdims=True)
    )


def grid_positions(side, width):
    quarter = width // 4
    rate = 1.0 / 10000.0 ** (jnp.arange(quarter, dtype=F32) / quarter)
    place = jnp.arange(side * side, dtype=jnp.int32)
    row_pos = (place // side).astype(F32)
    col_pos = (place % side).astype(F32)
    row_angle = row_pos[:, None] * rate[None, :]
    col_angle = col_pos[:, None] * rate[None, :]
    return jnp.concatenate(
        [jnp.sin(row_angle), jnp.cos(row_angle), jnp.sin(col_angle), jnp.cos(col_angle)], axis=1
    )


def any_spec():
    return pl.BlockSpec(memory_space=pl.ANY)


def params(limit=VMEM_BYTES):
    return pltpu.CompilerParams(vmem_limit_bytes=limit)


def cost(flops, nbytes):
    return pl.CostEstimate(flops=int(flops), bytes_accessed=int(nbytes), transcendentals=0)


def swap(array, peers, bits, core=0):
    bits = bits if isinstance(bits, tuple) else (bits, bits)
    pairs = [
        (d * 2 + m, (d ^ bits[m]) * 2 + (m ^ core)) for d in range(peers) for m in range(2)
    ]
    return lax.ppermute(array, AXES, pairs)


FAST_PEERS = 16
Z_STEPS = (4, 8, 12)


def gather_chunk(shard, peers):
    if peers != FAST_PEERS:
        return [lax.all_gather(lax.all_gather(shard, "dp", axis=0, tiled=True), "mp", axis=0)]
    along = jnp.stack([shard] + [swap(shard, peers, bits) for bits in Z_STEPS])
    first = swap(along, peers, (1, 2))
    mine = [along, first, swap(along, peers, (2, 1)), swap(first, peers, (2, 1))]
    return mine + [swap(piece, peers, 0, 1) for piece in mine]


def gather_table(me, core):
    one = jnp.where(core == 0, 1, 2)
    two = 3 - one
    zero = jnp.zeros_like(one)
    bases = jnp.stack([zero, one, two, one * 0 + 3, zero, two, one, one * 0 + 3])
    owners = me ^ bases[:, None] ^ jnp.array((0,) + Z_STEPS, jnp.int32)[None, :]
    cores = jnp.stack([core] * 4 + [1 - core] * 4)
    return jnp.concatenate([owners.reshape(-1), cores]).astype(jnp.int32)


def weight_copies(parts, table, target, sems):
    if len(parts) == 1:
        return [pltpu.make_async_copy(parts[0], target, sems.at[0])]
    copies = []
    for index, part in enumerate(parts):
        half = table[len(parts) * 4 + index]
        for inner in range(4):
            rows = part.shape[1]
            start = pl.multiple_of(table[index * 4 + inner] * rows, ROUND)
            copies.append(
                pltpu.make_async_copy(
                    part.at[inner], target.at[half, pl.ds(start, rows), :], sems.at[index * 4 + inner]
                )
            )
    return copies


def place_table(me, core):
    near = jnp.where(core == 0, 2, 1)
    far = 3 - near
    apart = jnp.arange(FAST_PEERS, dtype=jnp.int32) ^ me
    return (
        jnp.where((apart & near) != 0, 8, 0) + jnp.where((apart & far) != 0, 4, 0) + (apart >> 2)
    ).astype(jnp.int32)


def scatter_chunk(mine, other, peers):
    if peers != FAST_PEERS:
        whole = mine.astype(F32) + swap(other, peers, 0, 1).astype(F32)
        return lax.psum_scatter(
            whole.reshape(-1, whole.shape[-1]), "dp", scatter_dimension=0, tiled=True
        )
    got = swap(other, peers, 0, 1)
    add = lambda *terms: sum(term.astype(F32) for term in terms)
    got_one = swap(add(mine[8:], got[8:]).astype(BF16), peers, (2, 1))
    got_two = swap(add(mine[4:8], got[4:8], got_one[4:]).astype(BF16), peers, (1, 2))
    last = [
        swap(add(mine[i], got[i], got_one[i], got_two[i]).astype(BF16), peers, Z_STEPS[i - 1])
        for i in (1, 2, 3)
    ]
    return add(mine[0], got[0], got_one[0], got_two[0], *last)


def view_of(rows, per_view):
    view = jnp.zeros_like(rows)
    for edge in range(1, 5):
        view = view + (rows >= edge * per_view).astype(jnp.int32)
    return view


def allowed_bias(size, count, per_view):
    query = view_of(lax.broadcasted_iota(jnp.int32, (size, size), 0), per_view)
    key = view_of(lax.broadcasted_iota(jnp.int32, (size, size), 1), per_view)
    return jnp.where((key < count) | (key == query), 0.0, MASK_FILL)


def pair_masks(scale):
    lane = lax.broadcasted_iota(jnp.int32, (1, 2 * HEADDIM), 1)
    low = (lane < HEADDIM).astype(F32)
    return (low * scale).astype(BF16), ((1.0 - low) * scale).astype(BF16)


def attn_forward(mp_s, counts_s, table, tokens, norms, *rest, nparts, per_view, part):
    parts, (first_o, packed_o, attended_o, middle_o, second_o, lse_o), (weights, sems) = (
        rest[:nparts],
        rest[nparts : nparts + 6],
        rest[nparts + 6 :],
    )
    step = pl.program_id(0)
    copies = weight_copies(parts, table, weights, sems)

    @pl.when(step == 0)
    def _():
        for copy in copies:
            copy.start()
        for copy in copies:
            copy.wait()

    size = tokens.shape[0]
    scale = 1.0 / math.sqrt(HEADDIM)
    values = tokens[...].astype(F32)
    normed, _ = norm_rows(values)
    first = (normed * norms[0:1, :] + norms[1:2, :]).astype(BF16)
    first_o[...] = first
    bias = allowed_bias(size, counts_s[mp_s[0] * pl.num_programs(0) + step], per_view)
    masks = pair_masks(scale)
    lane = lax.broadcasted_iota(jnp.int32, (size, 2 * HEADDIM), 1)
    wide = 2 * HEADDIM
    lse = jnp.zeros((size, wide), F32)
    attn = jnp.zeros(values.shape, F32)
    for half in range(2):
        packed = mm(first, weights[half, :, : 3 * part]).astype(BF16)
        packed_o[:, half * 3 * part : (half + 1) * 3 * part] = packed
        for pair in range(part // wide):
            at = pair * wide
            query = packed[:, at : at + wide]
            key = packed[:, part + at : part + at + wide]
            value = packed[:, 2 * part + at : 2 * part + at + wide]
            outs = []
            for which in range(2):
                logits = mm(query * masks[which], key, NT) + bias
                top = jnp.max(logits, axis=-1, keepdims=True)
                exponent = jnp.exp(logits - top)
                total = jnp.sum(exponent, axis=-1, keepdims=True)
                probs = (exponent * (1.0 / total)).astype(BF16)
                outs.append(mm(probs, value))
                index = half * (part // HEADDIM) + pair * 2 + which
                lse = jnp.where(lane == index, top + jnp.log(total), lse)
            both = jnp.where(lane < HEADDIM, outs[0], outs[1]).astype(BF16)
            attended_o[:, half * part + at : half * part + at + wide] = both
        attn = attn + mm(
            attended_o[:, half * part : (half + 1) * part], weights[half, :, 3 * part :], NT
        )
    lse_o[...] = lse
    middle = values + attn
    middle_o[...] = middle
    normed, _ = norm_rows(middle)
    second_o[...] = (normed * norms[2:3, :] + norms[3:4, :]).astype(BF16)


def mlp_forward(mp_s, table, second, middle, dec_bias, *rest, nparts, per_view, part, wide, rows_each):
    up_parts, down_parts = rest[:nparts], rest[nparts : 2 * nparts]
    act_o, slope_o, final_o, keep_o, send_o = rest[2 * nparts : 2 * nparts + 5]
    up, down, up_sems, down_sems = rest[2 * nparts + 5 :]
    copies = weight_copies(up_parts, table, up, up_sems) + weight_copies(
        down_parts, table, down, down_sems
    )

    @pl.when(pl.program_id(0) == 0)
    def _():
        for copy in copies:
            copy.start()
        for copy in copies:
            copy.wait()

    acc = middle[...]
    rows = second[...]
    for half in range(2):
        for start in range(0, part, wide):
            pre = mm(rows, up[half, :, start : start + wide])
            cumulative = 0.5 * (1.0 + lax.erf(pre * (1.0 / math.sqrt(2.0))))
            act = (pre * cumulative).astype(BF16)
            slope = cumulative + pre * jnp.exp(-0.5 * pre * pre) * (1.0 / math.sqrt(2.0 * math.pi))
            act_o[:, half * part + start : half * part + start + wide] = act
            slope_o[:, half * part + start : half * part + start + wide] = slope.astype(BF16)
            acc = acc + mm(act, down[half, :, start : start + wide], NT)
    final = acc.astype(BF16)
    final_o[...] = final
    outs = [
        mm(final, down[half, :, part:]) + dec_bias[half : half + 1, :] for half in range(2)
    ]
    mine = jnp.where(mp_s[0] == 0, outs[0], outs[1])
    theirs = jnp.where(mp_s[0] == 0, outs[1], outs[0])
    views = rows_each // per_view
    for view in range(keep_o.shape[0]):
        at = (view // views) * rows_each + (view % views) * per_view
        keep_o[view] = mine[at : at + per_view].astype(BF16)
        send_o[view] = theirs[at : at + per_view].astype(BF16)


def mlp_backward(
    mp_s, where_s, table, mine, theirs, slope, middle, norms, *rest, nparts, per_view, part, wide, rows_each
):
    up_parts, down_parts = rest[:nparts], rest[nparts : 2 * nparts]
    rows_o, low_o, pre_o, mid_o, midlow_o, sums_o = rest[2 * nparts : 2 * nparts + 6]
    up, down, pieces, flat, up_sems, down_sems, piece_sems = rest[2 * nparts + 6 :]
    step = pl.program_id(0)
    nviews = pieces.shape[1]
    copies = weight_copies(up_parts, table, up, up_sems) + weight_copies(
        down_parts, table, down, down_sems
    )
    fetch = []
    for view in range(nviews):
        at = where_s[step * nviews + view]
        fetch.append(
            pltpu.make_async_copy(mine.at[at], pieces.at[mp_s[0], view], piece_sems.at[0, view])
        )
        fetch.append(
            pltpu.make_async_copy(theirs.at[at], pieces.at[1 - mp_s[0], view], piece_sems.at[1, view])
        )
    for copy in fetch:
        copy.start()

    @pl.when(step == 0)
    def _():
        for copy in copies:
            copy.start()
        flat[...] = jnp.zeros_like(flat)
        sums_o[...] = jnp.zeros_like(sums_o)
        for copy in copies:
            copy.wait()

    for copy in fetch:
        copy.wait()
    dec = pieces.shape[3]
    views = rows_each // per_view
    for view in range(nviews):
        at = (view // views) * rows_each + (view % views) * per_view
        for half in range(2):
            flat[at : at + per_view, half * dec : (half + 1) * dec] = pieces[half, view].astype(F32)
    rows = flat[...].astype(BF16)
    rows_o[...] = rows
    final = mm(rows[:, :dec], down[0, :, part:], NT) + mm(rows[:, dec:], down[1, :, part:], NT)
    low = final.astype(BF16)
    low_o[...] = low
    acc = jnp.zeros(final.shape, F32)
    for half in range(2):
        for start in range(0, part, wide):
            at = half * part + start
            hidden = mm(low, down[half, :, start : start + wide])
            pre = (hidden * slope[:, at : at + wide].astype(F32)).astype(BF16)
            pre_o[:, at : at + wide] = pre
            acc = acc + mm(pre, up[half, :, start : start + wide], NT)
    normed, inverse = norm_rows(middle[...])
    sums_o[0:1, :] += jnp.sum(acc * normed, axis=0, keepdims=True)
    sums_o[1:2, :] += jnp.sum(acc, axis=0, keepdims=True)
    mid = final + norm_back(acc * norms[2:3, :], normed, inverse)
    mid_o[...] = mid
    midlow_o[...] = mid.astype(BF16)


def attn_backward(
    mp_s, counts_s, table, tokens, packed, lse, mid, norms, *rest, nparts, per_view, part
):
    parts, (packed_o, tokens_o, sums_o), (weights, sems) = (
        rest[:nparts],
        rest[nparts : nparts + 3],
        rest[nparts + 3 :],
    )
    step = pl.program_id(0)
    copies = weight_copies(parts, table, weights, sems)

    @pl.when(step == 0)
    def _():
        for copy in copies:
            copy.start()
        sums_o[...] = jnp.zeros_like(sums_o)
        for copy in copies:
            copy.wait()

    size = tokens.shape[0]
    scale = 1.0 / math.sqrt(HEADDIM)
    wide = 2 * HEADDIM
    bias = allowed_bias(size, counts_s[mp_s[0] * pl.num_programs(0) + step], per_view)
    scaled_masks, masks = pair_masks(scale), pair_masks(1.0)
    lane = lax.broadcasted_iota(jnp.int32, (size, wide), 1)
    low = lane < HEADDIM
    middle = mid[...]
    middle_low = middle.astype(BF16)
    back = jnp.zeros(middle.shape, F32)
    for half in range(2):
        grad_att = mm(middle_low, weights[half, :, 3 * part :]).astype(BF16)
        base = half * 3 * part
        for pair in range(part // wide):
            at = pair * wide
            query = packed[:, base + at : base + at + wide]
            key = packed[:, base + part + at : base + part + at + wide]
            value = packed[:, base + 2 * part + at : base + 2 * part + at + wide]
            grad = grad_att[:, at : at + wide]
            outs = []
            for which in range(2):
                index = half * (part // HEADDIM) + pair * 2 + which
                logits = mm(query * scaled_masks[which], key, NT) + bias
                probs = jnp.exp(logits - lse[:, index : index + 1])
                grad_probs = mm(grad * masks[which], value, NT)
                weighted = probs * grad_probs
                centre = jnp.sum(weighted, axis=-1, keepdims=True)
                scores = ((weighted - probs * centre) * scale).astype(BF16)
                outs.append(
                    (
                        mm(scores, key),
                        mm(scores, query, TN),
                        mm(probs.astype(BF16), grad, TN),
                    )
                )
            for kind in range(3):
                both = jnp.where(low, outs[0][kind], outs[1][kind]).astype(BF16)
                packed_o[:, base + kind * part + at : base + kind * part + at + wide] = both
        back = back + mm(packed_o[:, base : base + 3 * part], weights[half, :, : 3 * part], NT)
    normed, inverse = norm_rows(tokens[...].astype(F32))
    sums_o[0:1, :] += jnp.sum(back * normed, axis=0, keepdims=True)
    sums_o[1:2, :] += jnp.sum(back, axis=0, keepdims=True)
    grads = middle + norm_back(back * norms[0:1, :], normed, inverse)
    tokens_o[0] = grads[: tokens_o.shape[1]].astype(BF16)


def weight_grad(mp_s, places, *rest, steps, rows_each):
    count = 2 * len(steps)
    sides, (other_o, mine_o), turned = rest[:count], rest[count : count + 2], rest[count + 2 :]
    half, step = pl.program_id(0), pl.program_id(1)
    begin = 0
    blocks = other_o.shape[0]
    for index, length in enumerate(steps):
        left, right, flip = sides[2 * index], sides[2 * index + 1], turned[index]

        @pl.when((half == 0) & (step == begin))
        def _(left=left, flip=flip):
            flip[...] = left[...].T

        @pl.when((step >= begin) & (step < begin + length))
        def _(right=right, flip=flip):
            product = mm(flip[...], right[...]).astype(BF16)

            @pl.when(half == 0)
            def _():
                for block in range(blocks):
                    other_o[places[blocks + block]] = product[block * rows_each : (block + 1) * rows_each]

            @pl.when(half == 1)
            def _():
                for block in range(blocks):
                    mine_o[places[block]] = product[block * rows_each : (block + 1) * rows_each]

        begin += length


def take_cells(slot_s, live_s, spots, *rest, each):
    cells, (rows_o, sums_o) = rest[:each], rest[each:]
    step = pl.program_id(0)

    @pl.when(step == 0)
    def _():
        sums_o[...] = jnp.zeros_like(sums_o)

    grid, width = cells[0].shape[1], spots.shape[1]
    per_view = rows_o.shape[1]
    cell = lax.broadcasted_iota(jnp.int32, (grid, width), 0)
    lane = lax.broadcasted_iota(jnp.int32, (grid, width), 1)
    for index in range(each):
        at = step * each + index
        live = live_s[at].astype(F32)
        place = (spots[pl.ds(at, 1), :] == cell).astype(F32)
        covered = jnp.sum(place, axis=1, keepdims=True)
        pick = (jnp.where(lane == per_view, 1.0 - covered, place) * live).astype(BF16)
        taken = mm(pick, cells[index][0], TN)
        rows_o[index] = taken[:per_view].astype(BF16)
        sums_o[0:1, :] += jnp.sum(taken[:per_view], axis=0, keepdims=True)
        sums_o[1:2, :] += taken[per_view : per_view + 1]


def put_cells(where_s, live_s, spots, mask, positions, *rest, each):
    rows, (cells_o,) = rest[:each], rest[each:]
    step = pl.program_id(0)
    grid, per_view = cells_o.shape[1], rows[0].shape[1]
    cell = lax.broadcasted_iota(jnp.int32, (grid, per_view), 0)
    for index in range(each):
        at = where_s[step * each + index]
        live = live_s[at].astype(F32)
        place = (spots[pl.ds(at, 1), :][:, :per_view] == cell).astype(F32)
        covered = jnp.sum(place, axis=1, keepdims=True)
        filled = mm(place.astype(BF16), rows[index][0]) + (1.0 - covered) * mask[...]
        cells_o[index] = (live * filled + positions[...]).astype(BF16)


def order_views(where_s, mp_s, own, theirs, out, sems):
    count = own.shape[0]
    copies = []
    for view in range(count):
        mine, other = mp_s[0] * count + view, (1 - mp_s[0]) * count + view
        copies.append(pltpu.make_async_copy(own.at[view], out.at[where_s[mine]], sems.at[view]))
        copies.append(
            pltpu.make_async_copy(theirs.at[view], out.at[where_s[other]], sems.at[count + view])
        )
    for copy in copies:
        copy.start()
    for copy in copies:
        copy.wait()


def tile_of(scalars, row):
    lane = lax.broadcasted_iota(jnp.int32, (8, 128), 1)
    line = lax.broadcasted_iota(jnp.int32, (8, 128), 0)
    tile = jnp.zeros((8, 128), F32)
    for index, value in enumerate(scalars):
        tile = jnp.where((lane == index) & (line == row), value, tile)
    return tile


def total(values):
    return jnp.sum(jnp.sum(values, axis=1, keepdims=True), axis=0, keepdims=True)


def squares_kernel(once_s, *refs):
    grads, masters, (tiles_o,) = refs[:7], refs[7:14], refs[14:]
    single = [1.0] * 5 + [once_s[0].astype(F32), 1.0]
    grad_sq, weight_sq = [], []
    for index in range(7):
        value = grads[index][...]
        grad_sq.append(total(value * value) * single[index])
        if index == 0:
            weight = sum(total(masters[0][k] * masters[0][k]) for k in range(3))
        else:
            weight = total(masters[index][...] * masters[index][...])
        weight_sq.append(weight * single[index])
    tile = tile_of(grad_sq, 0) + tile_of(weight_sq, 1)
    for peer in range(tiles_o.shape[0]):
        tiles_o[peer] = tile


def lamb_kernel(once_s, tiles, *refs):
    grads, masters, moments, squares = refs[:7], refs[7:14], refs[14:21], refs[21:28]
    outs = refs[28:]
    clip_o, moment_o, square_o, step_o = outs[:7], outs[7:14], outs[14:21], outs[21:28]
    sum_o, tiles_o = outs[28:]
    summed = jnp.sum(tiles[...], axis=0)
    sum_o[...] = summed
    lane = lax.broadcasted_iota(jnp.int32, (1, 128), 1)
    clip = jnp.sqrt(total(jnp.where(lane < 7, summed[0:1, :], 0.0)))
    factor = jnp.minimum(1.0, 0.5 * math.sqrt(PARAMS) / clip)
    single = [1.0] * 5 + [once_s[0].astype(F32), 1.0]
    update_sq = []
    for index in range(7):
        amount = jnp.zeros((1, 1), F32)
        for piece in range(3 if index == 0 else 1):
            at = piece if index == 0 else Ellipsis
            value = grads[index][...]
            if index == 0:
                width = masters[0].shape[2]
                value = value[:, piece * width : (piece + 1) * width]
            clipped = value * factor
            moment = BETA_ONE * moments[index][at] + (1.0 - BETA_ONE) * clipped
            square = BETA_TWO * squares[index][at] + (1.0 - BETA_TWO) * clipped * clipped
            step = moment / (jnp.sqrt(square) + ADAM_EPS) + DECAY_RATE * masters[index][at]
            clip_o[index][at] = clipped
            moment_o[index][at] = moment
            square_o[index][at] = square
            step_o[index][at] = step
            amount = amount + total(step * step)
        update_sq.append(amount * single[index])
    tile = tile_of(update_sq, 0)
    for peer in range(tiles_o.shape[0]):
        tiles_o[peer] = tile


def update_kernel(tiles, summed, *refs):
    masters, steps, outs = refs[:7], refs[7:14], refs[14:]
    updated_o, copy_o, (norms_o,) = outs[:7], outs[7:14], outs[14:]
    lane = lax.broadcasted_iota(jnp.int32, (1, 128), 1)
    squared = summed[...]
    clip = jnp.sqrt(total(jnp.where(lane < 7, squared[0:1, :], 0.0)))
    weight_norm = jnp.sqrt(squared[1:2, :])
    update_norm = jnp.sqrt(jnp.sum(tiles[...], axis=0)[0:1, :])
    ratio = weight_norm / (update_norm + TRUST_EPS)
    norms_o[0:1, :] = weight_norm
    norms_o[1:2, :] = update_norm
    norms_o[2:3, :] = jnp.broadcast_to(clip, (1, 128))
    for index in range(7):
        rate = LEARN_RATE * total(jnp.where(lane == index, ratio, 0.0))
        for piece in range(3 if index == 0 else 1):
            at = piece if index == 0 else Ellipsis
            updated = masters[index][at] - rate * steps[index][at]
            updated_o[index][at] = updated
            copy_o[index][at] = updated.astype(BF16)


def shape(dims, dtype=F32):
    return jax.ShapeDtypeStruct(tuple(dims), dtype)


def whole(kernel, outs, scalars, operands, **kw):
    return pl.pallas_call(
        kernel,
        out_shape=outs,
        in_specs=[pl.BlockSpec(memory_space=pltpu.SMEM)] * len(scalars)
        + [pl.BlockSpec(memory_space=pltpu.VMEM)] * len(operands),
        out_specs=[pl.BlockSpec(memory_space=pltpu.VMEM)] * len(outs),
        compiler_params=params(),
        **kw,
    )(*scalars, *operands)


def per_device(
    tokens,
    counts,
    visible,
    dest_device,
    dest_slot,
    cotangent,
    *state,
):
    masters = [state[3 * index] for index in range(7)]
    moments = [state[3 * index + 1] for index in range(7)]
    squares = [state[3 * index + 2] for index in range(7)]

    def flat_state(arrays):
        a, b, c, d, e, f, g = arrays
        return [a.transpose(1, 0, 2), b.T, c, d.T, e, f, g[:, 0, :]]

    def natural(arrays):
        a, b, c, d, e, f, g = arrays
        return [a.transpose(1, 0, 2), b.T, c, d.T, e, f, g[:, None, :]]

    masters, moments, squares = flat_state(masters), flat_state(moments), flat_state(squares)

    peers, cores = lax.axis_size("dp"), lax.axis_size("mp")
    me, core = lax.axis_index("dp"), lax.axis_index("mp")
    core_s = core.astype(jnp.int32).reshape(1)
    once_s = 1 - core_s
    model = tokens.shape[1]
    nviews, per_view = visible.shape
    episodes = counts.shape[0]
    views_each = nviews // episodes
    span = views_each * per_view
    size = -(-span // ROUND) * ROUND
    here = episodes // cores
    rows = here * size
    cells, dec = cotangent.shape[1:]
    part = masters[1].shape[1]
    hidden = masters[2].shape[1]
    shard_rows = masters[2].shape[0]
    room = (nviews + peers - 1) // peers
    npos = peers * room
    fast = peers == FAST_PEERS

    low = [m.astype(BF16) for m in masters]
    chunk_a = jnp.concatenate([low[0][0], low[0][1], low[0][2], low[1]], axis=1)
    chunk_b = low[2]
    chunk_c = jnp.concatenate([low[3], low[4]], axis=1)

    same = dest_device[:, None] == dest_device[None, :]
    earlier = jnp.arange(nviews)[None, :] < jnp.arange(nviews)[:, None]
    rank = jnp.sum((same & earlier).astype(jnp.int32), axis=1)
    where_view = (dest_device * room + rank).astype(jnp.int32)
    layout = jnp.arange(npos, dtype=jnp.int32)[:, None] == where_view[None, :]
    live_view = (
        jnp.arange(nviews, dtype=jnp.int32) % views_each < jnp.repeat(counts, views_each)
    ).astype(jnp.int32)
    details = jnp.concatenate(
        [jnp.ones((nviews, 1), jnp.int32), dest_slot[:, None], live_view[:, None], visible], axis=1
    )
    fields = details.shape[1]
    sent = jnp.dot(layout.astype(BF16), details.astype(BF16), preferred_element_type=F32)
    sent = sent.astype(BF16).reshape(peers, room * fields)
    small = jnp.concatenate([low[5].reshape(-1), low[6].reshape(-1)])
    message = jnp.concatenate(
        [sent, jnp.broadcast_to(small[None], (peers, small.shape[0]))], axis=1
    )
    message = jnp.broadcast_to(message[:, None], (peers, cores, message.shape[1]))
    message = lax.all_to_all(
        message.reshape(peers * cores, -1), AXES, split_axis=0, concat_axis=0, tiled=True
    ).reshape(peers, cores, -1)
    got = message[:, 0, : room * fields].reshape(npos, fields).astype(jnp.int32)
    nln = 4 * shard_rows
    ln_full = (
        message[:, 0, room * fields : room * fields + nln]
        .reshape(peers, 4, shard_rows)
        .transpose(1, 0, 2)
        .reshape(4, model)
        .astype(F32)
    )
    norms = jnp.concatenate([ln_full, jnp.zeros((4, model), F32)], axis=0)
    dec_full = (
        message[:, :, room * fields + nln :]
        .reshape(peers, cores, 2, dec // peers)
        .transpose(2, 1, 0, 3)
        .reshape(2, cores, dec)
        .astype(F32)
    )
    mask_token = lax.dynamic_index_in_dim(dec_full[1], core, 0, keepdims=True)
    slot_pos, live_pos = got[:, 1], got[:, 2]
    width = -(-(per_view + 1) // 8) * 8
    spots = jnp.concatenate(
        [got[:, 3:], jnp.full((npos, width - per_view), -1, jnp.int32)], axis=1
    )
    filled = (slot_pos[None, :] == jnp.arange(nviews, dtype=jnp.int32)[:, None]) & (
        got[:, 0][None, :] > 0
    )
    where_slot = jnp.sum(
        jnp.where(filled, jnp.arange(npos, dtype=jnp.int32)[None, :], 0), axis=1
    ).astype(jnp.int32)

    parts_a, parts_b, parts_c = (gather_chunk(c, peers) for c in (chunk_a, chunk_b, chunk_c))
    nparts = len(parts_a)
    table = gather_table(me, core)
    nsem = 4 * nparts if fast else 1

    each = 4
    cot_spec = lambda index: pl.BlockSpec(
        (1, cells, dec), lambda i, slot, live, index=index: (slot[i * each + index], 0, 0)
    )
    returned, dec_sums = pl.pallas_call(
        lambda *refs: take_cells(*refs, each=each),
        out_shape=[shape((npos, per_view, dec), BF16), shape((8, dec))],
        grid_spec=pltpu.PrefetchScalarGridSpec(
            num_scalar_prefetch=2,
            grid=(npos // each,),
            in_specs=[pl.BlockSpec((npos, width), lambda i, *_: (0, 0))]
            + [cot_spec(index) for index in range(each)],
            out_specs=[
                pl.BlockSpec((each, per_view, dec), lambda i, *_: (i, 0, 0)),
                pl.BlockSpec((8, dec), lambda i, *_: (0, 0)),
            ],
        ),
        compiler_params=params(),
        cost_estimate=cost(2 * npos * cells * 56 * dec, cotangent.size * 2),
        name="take_cells",
    )(slot_pos, live_pos, spots, *([cotangent] * each))
    came_mine = lax.all_to_all(returned, "dp", split_axis=0, concat_axis=0, tiled=True)
    came_theirs = swap(came_mine, peers, 0, 1)

    start = core * (here * span)
    own = lax.dynamic_slice_in_dim(tokens, start, here * span, 0).reshape(here, span, model)
    own = jnp.pad(own, ((0, 0), (0, size - span), (0, 0))).reshape(rows, model)
    smem = pl.BlockSpec(memory_space=pltpu.SMEM)
    ep = lambda cols: pl.BlockSpec((size, cols), lambda i: (i, 0))
    fixed = lambda dims: pl.BlockSpec(dims, lambda i: (0,) * len(dims))
    chunk_cols = [chunk_a.shape[1], chunk_b.shape[1], chunk_c.shape[1]]
    weight_bytes = [2 * 2 * model * cols for cols in chunk_cols]
    first, packed, attended, middle, second, lse = pl.pallas_call(
        lambda *refs: attn_forward(*refs, nparts=nparts, per_view=per_view, part=part),
        grid=(here,),
        out_shape=[
            shape((rows, model), BF16),
            shape((rows, 6 * part), BF16),
            shape((rows, 2 * part), BF16),
            shape((rows, model)),
            shape((rows, model), BF16),
            shape((rows, 2 * HEADDIM)),
        ],
        in_specs=[smem, smem, smem, ep(model), fixed((8, model))] + [any_spec()] * nparts,
        out_specs=[ep(model), ep(6 * part), ep(2 * part), ep(model), ep(model), ep(2 * HEADDIM)],
        scratch_shapes=[
            pltpu.VMEM((2, model, chunk_cols[0]), BF16),
            pltpu.SemaphoreType.DMA((nsem,)),
        ],
        compiler_params=params(),
        cost_estimate=cost(3 * 2 * rows * model * 8 * part, weight_bytes[0] + rows * model * 16),
        name="attn_forward",
    )(core_s, counts, table, own, norms, *parts_a)

    group = 2
    chunk = group * size
    steps = here // group
    gviews = group * views_each
    blk = lambda cols: pl.BlockSpec((chunk, cols), lambda i: (i, 0))
    wide = 512 if hidden % 512 == 0 else hidden
    mlp_scratch = [
        pltpu.VMEM((2, model, chunk_cols[1]), BF16),
        pltpu.VMEM((2, model, chunk_cols[2]), BF16),
    ]
    act, slope, final, emb_keep, emb_send = pl.pallas_call(
        lambda *refs: mlp_forward(
            *refs, nparts=nparts, per_view=per_view, part=hidden, wide=wide, rows_each=size
        ),
        grid=(steps,),
        out_shape=[
            shape((rows, 2 * hidden), BF16),
            shape((rows, 2 * hidden), BF16),
            shape((rows, model), BF16),
            shape((steps * gviews, per_view, dec), BF16),
            shape((steps * gviews, per_view, dec), BF16),
        ],
        in_specs=[smem, smem, blk(model), blk(model), fixed((2, dec))] + [any_spec()] * (2 * nparts),
        out_specs=[
            blk(2 * hidden),
            blk(2 * hidden),
            blk(model),
            pl.BlockSpec((gviews, per_view, dec), lambda i: (i, 0, 0)),
            pl.BlockSpec((gviews, per_view, dec), lambda i: (i, 0, 0)),
        ],
        scratch_shapes=mlp_scratch + [pltpu.SemaphoreType.DMA((nsem,))] * 2,
        compiler_params=params(),
        cost_estimate=cost(
            4 * rows * model * 2 * hidden, weight_bytes[1] + weight_bytes[2] + rows * hidden * 8
        ),
        name="mlp_forward",
    )(core_s, table, second, middle, dec_full[0], *parts_b, *parts_c)

    emb_other = swap(emb_send, peers, 0, 1)
    outgoing = pl.pallas_call(
        order_views,
        out_shape=shape((npos, per_view, dec), BF16),
        in_specs=[smem, smem, any_spec(), any_spec()],
        out_specs=any_spec(),
        scratch_shapes=[pltpu.SemaphoreType.DMA((nviews,))],
        compiler_params=params(8 << 20),
        cost_estimate=cost(0, 4 * nviews * per_view * dec),
        name="order_views",
    )(where_view, core_s, emb_keep, emb_other)
    arrived = lax.all_to_all(outgoing, "dp", split_axis=0, concat_axis=0, tiled=True)

    where_mine = lax.dynamic_slice_in_dim(where_view, core * (nviews // cores), nviews // cores)
    emb_rows, glow, gpre, gmid, gmid_low, ln_two = pl.pallas_call(
        lambda *refs: mlp_backward(
            *refs, nparts=nparts, per_view=per_view, part=hidden, wide=wide, rows_each=size
        ),
        grid=(steps,),
        out_shape=[
            shape((rows, 2 * dec), BF16),
            shape((rows, model), BF16),
            shape((rows, 2 * hidden), BF16),
            shape((rows, model)),
            shape((rows, model), BF16),
            shape((8, model)),
        ],
        in_specs=[smem, smem, smem, any_spec(), any_spec(), blk(2 * hidden), blk(model), fixed((8, model))]
        + [any_spec()] * (2 * nparts),
        out_specs=[blk(2 * dec), blk(model), blk(2 * hidden), blk(model), blk(model), fixed((8, model))],
        scratch_shapes=mlp_scratch
        + [
            pltpu.VMEM((2, gviews, per_view, dec), BF16),
            pltpu.VMEM((chunk, 2 * dec), F32),
            pltpu.SemaphoreType.DMA((nsem,)),
            pltpu.SemaphoreType.DMA((nsem,)),
            pltpu.SemaphoreType.DMA((2, gviews)),
        ],
        compiler_params=params(),
        cost_estimate=cost(
            4 * rows * model * 2 * hidden, weight_bytes[1] + weight_bytes[2] + rows * hidden * 8
        ),
        name="mlp_backward",
    )(core_s, where_mine, table, came_mine, came_theirs, slope, middle, norms, *parts_b, *parts_c)

    blocks = FAST_PEERS
    if fast:
        places = jnp.concatenate([place_table(me, core), place_table(me, 1 - core)])
    else:
        places = jnp.tile(jnp.arange(blocks, dtype=jnp.int32), 2)

    def grads_of(pairs, block, name):
        lengths = [right.shape[1] // 2 // block for _, right in pairs]
        many = sum(lengths)
        begins = [sum(lengths[:index]) for index in range(len(lengths))]

        def column(begin, length):
            def at(h, j, core_ref, places_ref):
                side = jnp.where(h == 0, 1 - core_ref[0], core_ref[0])
                return (0, side * length + jnp.clip(j - begin, 0, length - 1))

            return at

        in_specs, operands = [], []
        for (left, right), begin, length in zip(pairs, begins, lengths):
            in_specs += [
                pl.BlockSpec((rows, model), lambda h, j, *_: (0, 0)),
                pl.BlockSpec((rows, block), column(begin, length)),
            ]
            operands += [left, right]
        other, mine = pl.pallas_call(
            lambda *refs: weight_grad(*refs, steps=lengths, rows_each=model // blocks),
            out_shape=[shape((blocks, model // blocks, many * block), BF16)] * 2,
            grid_spec=pltpu.PrefetchScalarGridSpec(
                num_scalar_prefetch=2,
                grid=(2, many),
                in_specs=in_specs,
                out_specs=[
                    pl.BlockSpec(
                        (blocks, model // blocks, block),
                        lambda h, j, *_: (0, 0, jnp.where(h == 0, j, many - 1)),
                    ),
                    pl.BlockSpec(
                        (blocks, model // blocks, block),
                        lambda h, j, *_: (0, 0, jnp.where(h == 0, 0, j)),
                    ),
                ],
                scratch_shapes=[pltpu.VMEM((model, rows), BF16)] * len(pairs),
            ),
            compiler_params=params(),
            cost_estimate=cost(
                4 * rows * model * many * block, 2 * rows * (2 * many * block + model)
            ),
            name=name,
        )(core_s, places, *operands)
        return scatter_chunk(mine, other, peers)

    sum_c = grads_of([(glow, act), (final, emb_rows)], 256, "grad_down_emb")
    sum_b = grads_of([(second, gpre)], 512, "grad_up")

    grad_packed, grad_own, ln_one = pl.pallas_call(
        lambda *refs: attn_backward(*refs, nparts=nparts, per_view=per_view, part=part),
        grid=(here,),
        out_shape=[
            shape((rows, 6 * part), BF16),
            shape((here, span, model), BF16),
            shape((8, model)),
        ],
        in_specs=[smem, smem, smem, ep(model), ep(6 * part), ep(2 * HEADDIM), ep(model), fixed((8, model))]
        + [any_spec()] * nparts,
        out_specs=[
            ep(6 * part),
            pl.BlockSpec((1, span, model), lambda i: (i, 0, 0)),
            fixed((8, model)),
        ],
        scratch_shapes=[
            pltpu.VMEM((2, model, chunk_cols[0]), BF16),
            pltpu.SemaphoreType.DMA((nsem,)),
        ],
        compiler_params=params(),
        cost_estimate=cost(4 * 2 * rows * model * 8 * part, weight_bytes[0] + rows * model * 16),
        name="attn_backward",
    )(core_s, counts, table, own, packed, lse, gmid, norms, *parts_a)
    sum_a = grads_of([(first, grad_packed), (gmid_low, attended)], part, "grad_in_out")

    grad_other = swap(grad_own, peers, 0, 1)
    grad_tokens = jnp.where(
        core == 0,
        jnp.concatenate([grad_own, grad_other]),
        jnp.concatenate([grad_other, grad_own]),
    ).reshape(tokens.shape)

    ln_sums = jnp.concatenate([ln_one[:2], ln_two[:2]])
    ln_send = ln_sums.reshape(4, peers, shard_rows).transpose(1, 0, 2).reshape(peers, nln)
    dec_send = dec_sums[:2].reshape(2, peers, dec // peers).transpose(1, 0, 2).reshape(peers, -1)
    small_send = jnp.concatenate([ln_send, dec_send], axis=1)
    small_send = jnp.broadcast_to(small_send[:, None], (peers, cores, small_send.shape[1]))
    small_got = lax.all_to_all(
        small_send.reshape(peers * cores, -1), AXES, split_axis=0, concat_axis=0, tiled=True
    ).reshape(peers, cores, -1)
    grad_ln = jnp.sum(small_got[:, :, :nln], axis=(0, 1)).reshape(4, shard_rows)
    grad_dec = jnp.sum(
        lax.dynamic_index_in_dim(small_got[:, :, nln:], core, 1, keepdims=False), axis=0
    ).reshape(2, dec // peers)

    positions = lax.dynamic_slice_in_dim(
        grid_positions(math.isqrt(cells), dec * cores), core * dec, dec, 1
    )
    row_spec = lambda index: pl.BlockSpec(
        (1, per_view, dec), lambda i, where, live, index=index: (where[i * each + index], 0, 0)
    )
    decoded = pl.pallas_call(
        lambda *refs: put_cells(*refs, each=each),
        out_shape=shape((nviews, cells, dec), BF16),
        grid_spec=pltpu.PrefetchScalarGridSpec(
            num_scalar_prefetch=2,
            grid=(nviews // each,),
            in_specs=[
                pl.BlockSpec((npos, width), lambda i, *_: (0, 0)),
                pl.BlockSpec((1, dec), lambda i, *_: (0, 0)),
                pl.BlockSpec((cells, dec), lambda i, *_: (0, 0)),
            ]
            + [row_spec(index) for index in range(each)],
            out_specs=pl.BlockSpec((each, cells, dec), lambda i, *_: (i, 0, 0)),
        ),
        compiler_params=params(),
        cost_estimate=cost(2 * nviews * cells * 56 * dec, cotangent.size * 2),
        name="put_cells",
    )(where_slot, live_pos, spots, mask_token, positions, *([arrived] * each))

    grads = [
        sum_a[:, : 3 * part],
        sum_a[:, 3 * part :],
        sum_b,
        sum_c[:, :hidden],
        sum_c[:, hidden:],
        grad_ln,
        grad_dec,
    ]
    world = peers * cores
    (tiles,) = whole(squares_kernel, [shape((world, 8, 128))], [once_s], grads + masters, name="squares")
    tiles = lax.all_to_all(tiles, AXES, split_axis=0, concat_axis=0, tiled=True)
    same_shapes = [shape(m.shape) for m in masters]
    lamb = whole(
        lamb_kernel,
        same_shapes * 4 + [shape((8, 128)), shape((world, 8, 128))],
        [once_s],
        [tiles] + grads + masters + moments + squares,
        name="lamb",
    )
    summed = lamb[28]
    steps_tiles = lax.all_to_all(lamb[29], AXES, split_axis=0, concat_axis=0, tiled=True)
    update = whole(
        update_kernel,
        same_shapes + [shape(m.shape, BF16) for m in masters] + [shape((8, 128))],
        [],
        [steps_tiles, summed] + masters + list(lamb[21:28]),
        name="update",
    )
    results = [
        natural(group)
        for group in (lamb[:7], lamb[7:14], lamb[14:21], update[:7], update[7:14])
    ]
    outs = [decoded, grad_tokens, update[14][2, :1], update[14][:2, :7]]
    for index in range(7):
        outs += [group[index] for group in results]
    return tuple(outs)


def solution(mesh):
    tensor_specs = [
        P("dp", None, "mp"),
        P("mp", "dp"),
        P("dp", "mp"),
        P("mp", "dp"),
        P("dp", "mp"),
        P(None, "dp"),
        P(None, "mp", "dp"),
    ]
    in_specs = (
        P("dp", None),
        P("dp"),
        P("dp", None),
        P("dp"),
        P("dp"),
        P("dp", None, "mp"),
    ) + tuple(spec for spec in tensor_specs for _ in range(3))
    out_specs = (P("dp", None, "mp"), P("dp", None), P(), P()) + tuple(
        spec for spec in tensor_specs for _ in range(5)
    )
    return jax.shard_map(
        per_device, mesh=mesh, in_specs=in_specs, out_specs=out_specs, check_vma=False
    )
```

time: 1600 us -> 523 us (0.33)
  waiting for transfers between devices: 806 us -> 127 us
  blocking collectives: 275 us -> 0 us
  matrix products: 232 us -> 0.2 us
  Pallas kernels: 0 us -> 208 us
  local copies, waits for them, and re-layouts: 134 us -> 47.5 us
  starting transfers between devices: 17.3 us -> 88.6 us
  other arithmetic: 107 us -> 42.8 us
  between operations: 23.4 us -> 1.46 us
    reduce_scatter x5 -> x0, waiting for transfers between devices: 509 us -> none  [the longest x1 140 us: per_device(): lax.psum_scatter(grad_expand, 'dp', scatter_dimension=0, tiled=True)]
    dot_general x31 -> x1, matrix products: 232 us -> 0.2 us  [per_device(): jnp.dot(layout.astype(BF16), details.astype(BF16), preferred_element_type...]
    pallas_call x0 -> x13, Pallas kernels: none -> 208 us  [the longest x3 47.8 us: grads_of(): pl.pallas_call(lambda *refs: weight_grad(*refs, steps=lengths, rows_each=...]
    all_gather x4 -> x0, blocking collectives: 184 us -> none  [the longest x1 57.5 us: per_device(): lax.all_gather(weight_embedder.astype(jnp.bfloat16), 'dp', axis=0, tiled=...]
    all_gather x3 -> x0, waiting for transfers between devices: 111 us -> none  [the longest x1 60.1 us: per_device(): lax.all_gather(weight_expand.astype(jnp.bfloat16), 'dp', axis=0, tiled=True)]
    unnamed x15 -> x0, waiting for transfers between devices: 106 us -> none
    ppermute x0 -> x51, waiting for transfers between devices: none -> 99.2 us  [swap(): return lax.ppermute(array, AXES, pairs)]
    psum x2 -> x0, blocking collectives: 91 us -> none  [the longest x1 52.2 us: per_device(): grad_total, weight_total = lax.psum((grad_sq, weight_sq), ('dp', 'mp'))]
  transfers between devices with their start and end apart: 16 -> 57, of which waited for: 10 -> 12; matrix products, arithmetic and copies ran while one was open for 20% -> 16% of each run, Pallas kernels for 0% -> 31%
where the time goes in v1:
time: 523 us; the launch traced here: 516 us
  Pallas kernels  208 us (40%)
  waiting for transfers between devices  127 us (24%)
  starting transfers between devices  88.6 us (17%)
  local copies, waits for them, and re-layouts  47.5 us (9%)
  other arithmetic  42.8 us (8%)
    ppermute x51, waiting for transfers between devices, swap(): return lax.ppermute(array, AXES, pairs)  99.2 us
    ppermute x51, starting transfers between devices, swap(): return lax.ppermute(array, AXES, pairs)  64 us
    pallas_call x3, Pallas kernels, grads_of(): pl.pallas_call(lambda *refs: weight_grad(*refs, steps=lengths, rows_each=...  47.8 us
    pallas_call x1, Pallas kernels, per_device(): pl.pallas_call(lambda *refs: attn_backward(*refs, nparts=nparts, per_view...  45.2 us
    pallas_call x1, Pallas kernels, per_device(): pl.pallas_call(lambda *refs: mlp_backward(*refs, nparts=nparts, per_view=...  30.2 us
    all_to_all x1, waiting for transfers between devices, per_device(): lax.all_to_all(small_send.reshape(peers * cores, -1), AXES, split_axis=0,...  27.9 us
    pallas_call x1, Pallas kernels, per_device(): pl.pallas_call(lambda *refs: attn_forward(*refs, nparts=nparts, per_view=...  27.1 us
    pallas_call x1, Pallas kernels, per_device(): pl.pallas_call(lambda *refs: mlp_forward(*refs, nparts=nparts, per_view=p...  25.4 us
  transfers between devices with their start and end apart: 57, of which 12 were waited for; matrix products, arithmetic and copies ran while one was open for 16% of the time, Pallas kernels for 31%

profile of v1, /device:TPU:0, one launch (start us, length us, event | category | flops | bytes accessed | tf_op | source)
XLA Modules:
  0.0 515.9 jit_solution(1405956493800977216)
XLA Ops:
  2.6 3.1 collective-permute-start
  5.7 2.6 collective-permute-start.1
  10.9 3.5 collective-permute-start.11
  22.3 2.8 all-to-all-start
  26.2 6.3 %copy.160.refs_3_.refs_4_.refs_5_.refs_6_ = bf16[48,196,256]{2,1,0:T(8,128)(2,1)} copy(bf16[48,196,256]{2,0,1:T(8,128)(2,1)} %param.33) | data formatting | bytes 9633792 | tf_op args[5]
  34.3 3.6 collective-permute-start.12
  41.0 10.9 %take_cells.1 = (bf16[48,49,256]{2,1,0:T(8,128)(2,1)}, f32[8,256]{1,0:T(8,128)}) custom-call(s32[48]{0:T(128)} %get-tuple-element.420.refs_0_, s32[48]{0:T(128)} %get-tuple-element.419.refs_1_, s32[48,56]{1,0:T(8,128)} %concatenate.52.refs_2_, bf16[48,196,256]{2,1,0:T(8,128)(2,1)} %copy.160.refs_3_.refs_4_.refs_5_.refs_6_, ...), custom_call_target="tpu_custom_call" | custom-call | flops 269746176 | bytes 4816896 | tf_op jit(solution)/shard_map/take_cells/pallas_call | solution.py:685
  51.9 3.9 all-to-all-start.2
  57.8 2.4 collective-permute-start.21
  61.4 21.5 %collective-permute-done.20 = bf16[48,1792]{1,0:T(8,128)(2,1)S(1)} collective-permute-done((bf16[48,1792]{1,0:T(8,128)(2,1)S(1)}, bf16[48,1792]{1,0:T(8,128)(2,1)S(1)}, u32[]{:S(2)}, u32[]{:S(2)}) %collective-permute-start.20) | collective-permute-done | bytes 172064 | tf_op jit(solution)/shard_map/ppermute | solution.py:79
  82.9 17.4 %collective-permute-done.21 = bf16[48,1792]{1,0:T(8,128)(2,1)S(1)} collective-permute-done((bf16[48,1792]{1,0:T(8,128)(2,1)S(1)}, bf16[48,1792]{1,0:T(8,128)(2,1)S(1)}, u32[]{:S(2)}, u32[]{:S(2)}) %collective-permute-start.21) | collective-permute-done | bytes 172064 | tf_op jit(solution)/shard_map/ppermute | solution.py:79
  103.3 2.3 collective-permute-start.14
  105.9 10.8 %collective-permute-done.13.refs_6_.refs_9_ = bf16[4,48,1536]{2,1,0:T(8,128)(2,1)} collective-permute-done((bf16[4,48,1536]{2,1,0:T(8,128)(2,1)S(1)}, bf16[4,48,1536]{2,1,0:T(8,128)(2,1)}, u32[]{:S(2)}, u32[]{:S(2)}) %collective-permute-start.13) | collective-permute-done | bytes 589856 | tf_op jit(solution)/shard_map/ppermute | solution.py:79
  116.6 3.3 collective-permute-done.14.refs_7_.refs_10_
  122.0 9.4 %collective-permute-done.23.refs_14_.refs_17_ = bf16[4,48,1792]{2,1,0:T(8,128)(2,1)} collective-permute-done((bf16[4,48,1792]{2,1,0:T(8,128)(2,1)}, bf16[4,48,1792]{2,1,0:T(8,128)(2,1)}, u32[]{:S(2)}, u32[]{:S(2)}) %collective-permute-start.23) | collective-permute-done | bytes 688160 | tf_op jit(solution)/shard_map/ppermute | solution.py:79
  131.4 2.8 constant_dynamic-slice_fusion
  134.3 2.3 collective-permute-start.25
  137.2 2.4 reshape.393
  145.1 7.4 %collective-permute-done.15.refs_8_.refs_11_ = bf16[4,48,1536]{2,1,0:T(8,128)(2,1)} collective-permute-done((bf16[4,48,1536]{2,1,0:T(8,128)(2,1)}, bf16[4,48,1536]{2,1,0:T(8,128)(2,1)}, u32[]{:S(2)}, u32[]{:S(2)}) %collective-permute-start.15) | collective-permute-done | bytes 589856 | tf_op jit(solution)/shard_map/ppermute | solution.py:79
  153.6 27.1 %attn_forward.1 = (bf16[1248,768]{1,0:T(8,128)(2,1)}, bf16[1248,2304]{1,0:T(8,128)(2,1)}, bf16[1248,768]{1,0:T(8,128)(2,1)}, f32[1248,768]{1,0:T(8,128)}, bf16[1...) custom-call(s32[1]{0:T(128)} %bitcast.3.refs_0_.mp_s, s32[12]{0:T(128)} %refs_1_.3, s32[40]{0:T(128)} %concatenate.54.refs_2_.refs_1_, ...), custom_call_target="tpu_custom_call" | custom-call | flops 17666408448 | bytes 20054016 | tf_op jit(solution)/shard_map/attn_forward/pallas_call | solution.py:713
  181.7 25.4 %mlp_forward.1 = (bf16[1248,3072]{1,0:T(8,128)(2,1)}, bf16[1248,3072]{1,0:T(8,128)(2,1)}, bf16[1248,768]{1,0:T(8,128)(2,1)}, bf16[24,49,256]{2,1,0:T(8,128)(2,1)}, bf16[24,49,256]{2,1,0:T(8,128)(2,1)}) custom-call(s32[1]{0:T(128)} %bitcast.3.refs_0_.mp_s, s32[40]{0:T(128)} %concatenate.54.refs_2_.refs_1_, bf16[1248,768]{1,0:T(8,128)(2,1)} %get-tuple-element.112.refs_2_, ...), custom_call_target="tpu_custom_call" | custom-call | flops 11777605632 | bytes 25559040 | tf_op jit(solution)/shard_map/mlp_forward/pallas_call | solution.py:745
  208.7 30.2 %mlp_backward.1 = (bf16[1248,512]{1,0:T(8,128)(2,1)}, bf16[1248,768]{1,0:T(8,128)(2,1)}, bf16[1248,3072]{1,0:T(8,128)(2,1)}, f32[1248,768]{1,0:T(8,128)}, bf16[1248,768]{1,0:T(8,128)(2,1)}, /*index=5*/f32[8,768]{1,0:T(8,128)}) custom-call(s32[1]{0:T(128)} %bitcast.3.refs_0_.mp_s, s32[24]{0:T(128)} %dynamic_slice.23.refs_1_, s32[40]{0:T(128)} %concatenate.54.refs_2_.refs_1_, ...), custom_call_target="tpu_custom_call" | custom-call | flops 11777605632 | bytes 25559040 | tf_op jit(solution)/shard_map/mlp_backward/pallas_call | solution.py:787
  238.8 12.8 %grad_up.1 = (bf16[16,48,1536]{2,1,0:T(8,128)(2,1)}, bf16[16,48,1536]{2,1,0:T(8,128)(2,1)}) custom-call(s32[1]{0:T(128)} %bitcast.3.refs_0_.mp_s, s32[32]{0:T(128)} %pad_add_fusion.refs_1_, bf16[1248,768]{1,0:T(8,128)(2,1)} %get-tuple-element.112.refs_2_, bf16[1248,3072]{1,0:T(8,128)(2,1)} %get-tuple-element.128.refs_3_), custom_call_target="tpu_custom_call" | custom-call | flops 5888802816 | bytes 9584640 | tf_op jit(solution)/shard_map/grad_up/pallas_call | solution.py:843
  252.1 45.2 %attn_backward.1 = (bf16[1248,2304]{1,0:T(8,128)(2,1)}, bf16[6,196,768]{2,1,0:T(8,128)(2,1)}, f32[8,768]{1,0:T(8,128)}) custom-call(s32[1]{0:T(128)} %bitcast.3.refs_0_.mp_s, s32[12]{0:T(128)} %refs_1_.3, s32[40]{0:T(128)} %concatenate.54.refs_2_.refs_1_, bf16[1248,768]{1,0:T(8,128)(2,1)} %bitcast.132, bf16[1248,2304]{1,0:T(8,128)(2,1)} %get-tuple-element.116.refs_4_, ...), custom_call_target="tpu_custom_call" | custom-call | flops 23555211264 | bytes 20054016 | tf_op jit(solution)/shard_map/attn_backward/pallas_call | solution.py:873
  297.3 16.3 %grad_in_out.1 = (bf16[16,48,1536]{2,1,0:T(8,128)(2,1)}, bf16[16,48,1536]{2,1,0:T(8,128)(2,1)}) custom-call(s32[1]{0:T(128)} %bitcast.3.refs_0_.mp_s, s32[32]{0:T(128)} %pad_add_fusion.refs_1_, bf16[1248,768]{1,0:T(8,128)(2,1)} %get-tuple-element.122.refs_2_, bf16[1248,2304]{1,0:T(8,128)(2,1)} %get-tuple-element.123.refs_3_, ...), custom_call_target="tpu_custom_call" | custom-call | flops 5888802816 | bytes 9584640 | tf_op jit(solution)/shard_map/grad_in_out/pallas_call | solution.py:843
  313.7 18.7 %grad_down_emb.1 = (bf16[16,48,1792]{2,1,0:T(8,128)(2,1)}, bf16[16,48,1792]{2,1,0:T(8,128)(2,1)}) custom-call(s32[1]{0:T(128)} %bitcast.3.refs_0_.mp_s, s32[32]{0:T(128)} %pad_add_fusion.refs_1_, bf16[1248,768]{1,0:T(8,128)(2,1)} %get-tuple-element.131.refs_2_, bf16[1248,3072]{1,0:T(8,128)(2,1)} %get-tuple-element.132.refs_3_, ...), custom_call_target="tpu_custom_call" | custom-call | flops 6870269952 | bytes 10862592 | tf_op jit(solution)/shard_map/grad_down_emb/pallas_call | solution.py:843
  338.0 3.1 add_convert_fusion.1
  342.8 2.7 add_convert_fusion.2
  349.7 2.6 all-to-all-start.3
  357.9 27.9 %all-to-all-done.3 = f32[32,1,224]{2,1,0:T(1,128)S(1)} async-done(((f32[32,1,224]{2,1,0:T(1,128)}), f32[32,1,224]{2,1,0:T(1,128)S(1)}, u32[]{:S(2)}, u32[]{:S(2)}) %all-to-all-start.3) | async-done | bytes 28704 | tf_op jit(solution)/shard_map/all_to_all | solution.py:910
  385.8 3.7 all-to-all-start.1
  400.2 3.7 collective-permute-done.41
  405.5 3.4 collective-permute-start.42
  408.9 2.8 collective-permute-start.43
  411.7 7.8 %collective-permute-done.35 = bf16[4,48,1536]{2,1,0:T(8,128)(2,1)S(1)} collective-permute-done((bf16[4,48,1536]{2,1,0:T(8,128)(2,1)S(1)}, bf16[4,48,1536]{2,1,0:T(8,128)(2,1)S(1)}, u32[]{:S(2)}, u32[]{:S(2)}) %collective-permute-start.35) | collective-permute-done | bytes 589856 | tf_op jit(solution)/shard_map/ppermute | solution.py:79
  421.2 3.2 collective-permute-start.36
  424.4 8.7 %collective-permute-done.43 = bf16[48,1536]{1,0:T(8,128)(2,1)S(1)} collective-permute-done((bf16[48,1536]{1,0:T(8,128)(2,1)S(1)}, bf16[48,1536]{1,0:T(8,128)(2,1)S(1)}, u32[]{:S(2)}, u32[]{:S(2)}) %collective-permute-start.43) | collective-permute-done | bytes 147488 | tf_op jit(solution)/shard_map/ppermute | solution.py:79
  438.5 9.2 %collective-permute-start.48 = (bf16[48,1792]{1,0:T(8,128)(2,1)S(1)}, bf16[48,1792]{1,0:T(8,128)(2,1)S(1)}, u32[]{:S(2)}, u32[]{:S(2)}) collective-permute-start(bf16[48,1792]{1,0:T(8,128)(2,1)S(1)} %get-tuple-element.421), channel_id=1, source_target_pairs={{0,8},{1,9},{2,10},{3,11},{4,12},{5,13},{6,14},{7,15},{8,0},{9,1},... | collective-permute-start | bytes 516104 | tf_op jit(solution)/shard_map/ppermute | solution.py:79
  452.9 8.9 %collective-permute-done.49 = bf16[48,1792]{1,0:T(8,128)(2,1)S(1)} collective-permute-done((bf16[48,1792]{1,0:T(8,128)(2,1)S(1)}, bf16[48,1792]{1,0:T(8,128)(2,1)S(1)}, u32[]{:S(2)}, u32[]{:S(2)}) %collective-permute-start.49) | collective-permute-done | bytes 172064 | tf_op jit(solution)/shard_map/ppermute | solution.py:79
  464.3 2.4 squares.1
  466.7 5.8 %all-to-all-start.4 = ((f32[32,8,128]{2,1,0:T(8,128)}), f32[32,8,128]{2,1,0:T(8,128)S(1)}, u32[]{:S(2)}, u32[]{:S(2)}) async-start(f32[32,8,128]{2,1,0:T(8,128)} %squares.1), calls=%async_computation.4 | async-start | bytes 262144 | tf_op jit(solution)/shard_map/all_to_all | solution.py:954
  473.9 9.6 %put_cells.1 = bf16[48,196,256]{2,1,0:T(8,128)(2,1)} custom-call(s32[48]{0:T(128)} %select_reduce_fusion.refs_0_, s32[48]{0:T(128)} %get-tuple-element.419.refs_1_, s32[48,56]{1,0:T(8,128)} %concatenate.52.refs_2_, f32[1,256]{1,0:T(1,128)} %fusion.37.refs_3_, f32[196,256]{1,0:T(8,128)} %fusion.8.refs_4_, bf16[48,49,256]{2,1,0:T(8,128)(2,1)} %copy-done.1, ...), custom_call_target="tpu_custom_call" | custom-call | flops 269746176 | bytes 4816896 | tf_op jit(solution)/shard_map/put_cells/pallas_call | solution.py:924
  483.5 5.6 %copy.168 = bf16[48,196,256]{2,0,1:T(8,128)(2,1)} copy(bf16[48,196,256]{2,1,0:T(8,128)(2,1)} %put_cells.1) | data formatting | bytes 9633792
  489.8 4.7 lamb.1
  494.4 5.8 %all-to-all-start.5 = ((f32[32,8,128]{2,1,0:T(8,128)}), f32[32,8,128]{2,1,0:T(8,128)S(1)}, u32[]{:S(2)}, u32[]{:S(2)}) async-start(f32[32,8,128]{2,1,0:T(8,128)} %get-tuple-element.140), calls=%async_computation.5 | async-start | bytes 262144 | tf_op jit(solution)/shard_map/all_to_all | solution.py:964
  500.3 3.8 maximum_select_fusion
  504.1 5.7 %select_n.102 = bf16[2352,768]{1,0:T(8,128)(2,1)} reshape(bf16[12,196,768]{2,1,0:T(8,128)(2,1)} %maximum_select_fusion) | data formatting | bytes 7225344 | tf_op jit(solution)/shard_map/jit(_where)/select_n | solution.py:899
  510.4 2.8 update.1
  (241 shorter events, 86.1 us)
Async XLA Ops:
  2.6 31.6 %collective-permute-start = (bf16[48,1536]{1,0:T(8,128)(2,1)S(1)}, bf16[48,1536]{1,0:T(8,128)(2,1)S(1)}, u32[]{:S(2)}, u32[]{:S(2)}) collective-permute-start(bf16[48,1536]{1,0:T(8,128)(2,1)S(1)} %get-tuple-element.433), channel_id=1, source_target_pairs={{0,8},{1,9},{2,10},{3,11},{4,12},{5,13},{6,14},{7,15},{8,0},{9,1},... | collective-permute-start | bytes 442376 | tf_op jit(solution)/shard_map/ppermute | solution.py:79
  5.7 32.2 %collective-permute-start.1 = (bf16[48,1536]{1,0:T(8,128)(2,1)S(1)}, bf16[48,1536]{1,0:T(8,128)(2,1)S(1)}, u32[]{:S(2)}, u32[]{:S(2)}) collective-permute-start(bf16[48,1536]{1,0:T(8,128)(2,1)S(1)} %get-tuple-element.433), channel_id=1, source_target_pairs={{0,16},{1,17},{2,18},{3,19},{4,20},{5,21},{6,22},{7,23},{8,24},{9,... | collective-permute-start | bytes 442376 | tf_op jit(solution)/shard_map/ppermute | solution.py:79
  8.3 29.6 %collective-permute-start.2 = (bf16[48,1536]{1,0:T(8,128)(2,1)S(1)}, bf16[48,1536]{1,0:T(8,128)(2,1)S(1)}, u32[]{:S(2)}, u32[]{:S(2)}) collective-permute-start(bf16[48,1536]{1,0:T(8,128)(2,1)S(1)} %get-tuple-element.433), channel_id=1, source_target_pairs={{0,24},{1,25},{2,26},{3,27},{4,28},{5,29},{6,30},{7,31},{8,16},{9,... | collective-permute-start | bytes 442376 | tf_op jit(solution)/shard_map/ppermute | solution.py:79
  10.0 45.9 %collective-permute-start.10 = (bf16[48,1536]{1,0:T(8,128)(2,1)}, bf16[48,1536]{1,0:T(8,128)(2,1)S(1)}, u32[]{:S(2)}, u32[]{:S(2)}) collective-permute-start(bf16[48,1536]{1,0:T(8,128)(2,1)} %convert_element_type.398), channel_id=1, source_target_pairs={{0,8},{1,9},{2,10},{3,11},{4,12},{5,13},{6,14},{7,15},{8,0},{9,1},... | collective-permute-start | bytes 442376 | tf_op jit(solution)/shard_map/ppermute | solution.py:79
  10.9 47.0 %collective-permute-start.11 = (bf16[48,1536]{1,0:T(8,128)(2,1)}, bf16[48,1536]{1,0:T(8,128)(2,1)S(1)}, u32[]{:S(2)}, u32[]{:S(2)}) collective-permute-start(bf16[48,1536]{1,0:T(8,128)(2,1)} %convert_element_type.398), channel_id=1, source_target_pairs={{0,16},{1,17},{2,18},{3,19},{4,20},{5,21},{6,22},{7,23},{8,24},{9,... | collective-permute-start | bytes 442376 | tf_op jit(solution)/shard_map/ppermute | solution.py:79
  34.3 26.0 %collective-permute-start.12 = (bf16[48,1536]{1,0:T(8,128)(2,1)}, bf16[48,1536]{1,0:T(8,128)(2,1)}, u32[]{:S(2)}, u32[]{:S(2)}) collective-permute-start(bf16[48,1536]{1,0:T(8,128)(2,1)} %convert_element_type.398), channel_id=1, source_target_pairs={{0,24},{1,25},{2,26},{3,27},{4,28},{5,29},{6,30},{7,31},{8,16},{9,... | collective-permute-start | bytes 442376 | tf_op jit(solution)/shard_map/ppermute | solution.py:79
  38.0 65.3 %collective-permute-start.3 = (bf16[4,48,1536]{2,1,0:T(8,128)(2,1)S(1)}, bf16[4,48,1536]{2,1,0:T(8,128)(2,1)}, u32[]{:S(2)}, u32[]{:S(2)}) collective-permute-start(bf16[4,48,1536]{2,1,0:T(8,128)(2,1)S(1)} %pad_maximum_fusion.1.refs_5_.refs_8_), channel_id=1, source_target_pairs={{0,2},{1,5},{2,0},{3,7},{4,6},{5,1},{6,4},{7,3},{8,10},{9,13},{10,... | collective-permute-start | bytes 1769480 | tf_op jit(solution)/shard_map/ppermute | solution.py:79
  39.5 66.0 %collective-permute-start.4 = (bf16[4,48,1536]{2,1,0:T(8,128)(2,1)S(1)}, bf16[4,48,1536]{2,1,0:T(8,128)(2,1)}, u32[]{:S(2)}, u32[]{:S(2)}) collective-permute-start(bf16[4,48,1536]{2,1,0:T(8,128)(2,1)S(1)} %pad_maximum_fusion.1.refs_5_.refs_8_), channel_id=1, source_target_pairs={{0,4},{1,3},{2,6},{3,1},{4,0},{5,7},{6,2},{7,5},{8,12},{9,11},{10,... | collective-permute-start | bytes 1769480 | tf_op jit(solution)/shard_map/ppermute | solution.py:79
  51.9 92.9 %all-to-all-start.2 = ((bf16[48,49,256]{2,1,0:T(8,128)(2,1)}), bf16[48,49,256]{2,1,0:T(8,128)(2,1)S(1)}, u32[]{:S(2)}, u32[]{:S(2)}) async-start(bf16[48,49,256]{2,1,0:T(8,128)(2,1)} %get-tuple-element.118), calls=%async_computation.2 | async-start | bytes 2752512 | tf_op jit(solution)/shard_map/all_to_all | solution.py:702
  55.8 27.1 %collective-permute-start.20 = (bf16[48,1792]{1,0:T(8,128)(2,1)S(1)}, bf16[48,1792]{1,0:T(8,128)(2,1)S(1)}, u32[]{:S(2)}, u32[]{:S(2)}) collective-permute-start(bf16[48,1792]{1,0:T(8,128)(2,1)S(1)} %get-tuple-element.431), channel_id=1, source_target_pairs={{0,8},{1,9},{2,10},{3,11},{4,12},{5,13},{6,14},{7,15},{8,0},{9,1},... | collective-permute-start | bytes 516104 | tf_op jit(solution)/shard_map/ppermute | solution.py:79
  57.8 42.5 %collective-permute-start.21 = (bf16[48,1792]{1,0:T(8,128)(2,1)S(1)}, bf16[48,1792]{1,0:T(8,128)(2,1)S(1)}, u32[]{:S(2)}, u32[]{:S(2)}) collective-permute-start(bf16[48,1792]{1,0:T(8,128)(2,1)S(1)} %get-tuple-element.431), channel_id=1, source_target_pairs={{0,16},{1,17},{2,18},{3,19},{4,20},{5,21},{6,22},{7,23},{8,24},{9,... | collective-permute-start | bytes 516104 | tf_op jit(solution)/shard_map/ppermute | solution.py:79
  60.3 41.5 %collective-permute-start.22 = (bf16[48,1792]{1,0:T(8,128)(2,1)S(1)}, bf16[48,1792]{1,0:T(8,128)(2,1)S(1)}, u32[]{:S(2)}, u32[]{:S(2)}) collective-permute-start(bf16[48,1792]{1,0:T(8,128)(2,1)S(1)} %get-tuple-element.431), channel_id=1, source_target_pairs={{0,24},{1,25},{2,26},{3,27},{4,28},{5,29},{6,30},{7,31},{8,16},{9,... | collective-permute-start | bytes 516104 | tf_op jit(solution)/shard_map/ppermute | solution.py:79
  82.9 22.7 %collective-permute-start.6 = (bf16[4,48,1536]{2,1,0:T(8,128)(2,1)S(1)}, bf16[4,48,1536]{2,1,0:T(8,128)(2,1)}, u32[]{:S(2)}, u32[]{:S(2)}) collective-permute-start(bf16[4,48,1536]{2,1,0:T(8,128)(2,1)S(1)} %pad_maximum_fusion.1.refs_5_.refs_8_), channel_id=1, source_target_pairs={{0,1},{1,0},{2,3},{3,2},{4,5},{5,4},{6,7},{7,6},{8,9},{9,8},{10,11... | collective-permute-start | bytes 1769480 | tf_op jit(solution)/shard_map/ppermute | solution.py:79
  100.3 16.3 %collective-permute-start.13 = (bf16[4,48,1536]{2,1,0:T(8,128)(2,1)S(1)}, bf16[4,48,1536]{2,1,0:T(8,128)(2,1)}, u32[]{:S(2)}, u32[]{:S(2)}) collective-permute-start(bf16[4,48,1536]{2,1,0:T(8,128)(2,1)S(1)} %pad_maximum_fusion.2.refs_5_.refs_8_), channel_id=1, source_target_pairs={{0,2},{1,5},{2,0},{3,7},{4,6},{5,1},{6,4},{7,3},{8,10},{9,13},{10,... | collective-permute-start | bytes 1769480 | tf_op jit(solution)/shard_map/ppermute | solution.py:79
  102.7 28.6 %collective-permute-start.23 = (bf16[4,48,1792]{2,1,0:T(8,128)(2,1)}, bf16[4,48,1792]{2,1,0:T(8,128)(2,1)}, u32[]{:S(2)}, u32[]{:S(2)}) collective-permute-start(bf16[4,48,1792]{2,1,0:T(8,128)(2,1)} %pad_maximum_fusion.refs_13_.refs_16_), channel_id=1, source_target_pairs={{0,2},{1,5},{2,0},{3,7},{4,6},{5,1},{6,4},{7,3},{8,10},{9,13},{10,... | collective-permute-start | bytes 2064392 | tf_op jit(solution)/shard_map/ppermute | solution.py:79
  103.3 16.6 %collective-permute-start.14 = (bf16[4,48,1536]{2,1,0:T(8,128)(2,1)S(1)}, bf16[4,48,1536]{2,1,0:T(8,128)(2,1)}, u32[]{:S(2)}, u32[]{:S(2)}) collective-permute-start(bf16[4,48,1536]{2,1,0:T(8,128)(2,1)S(1)} %pad_maximum_fusion.2.refs_5_.refs_8_), channel_id=1, source_target_pairs={{0,4},{1,3},{2,6},{3,1},{4,0},{5,7},{6,2},{7,5},{8,12},{9,11},{10,... | collective-permute-start | bytes 1769480 | tf_op jit(solution)/shard_map/ppermute | solution.py:79
  105.6 16.4 %collective-permute-start.16 = (bf16[4,48,1536]{2,1,0:T(8,128)(2,1)S(1)}, bf16[4,48,1536]{2,1,0:T(8,128)(2,1)}, u32[]{:S(2)}, u32[]{:S(2)}) collective-permute-start(bf16[4,48,1536]{2,1,0:T(8,128)(2,1)S(1)} %pad_maximum_fusion.2.refs_5_.refs_8_), channel_id=1, source_target_pairs={{0,1},{1,0},{2,3},{3,2},{4,5},{5,4},{6,7},{7,6},{8,9},{9,8},{10,11... | collective-permute-start | bytes 1769480 | tf_op jit(solution)/shard_map/ppermute | solution.py:79
  105.7 28.6 %collective-permute-start.24 = (bf16[4,48,1792]{2,1,0:T(8,128)(2,1)}, bf16[4,48,1792]{2,1,0:T(8,128)(2,1)S(1)}, u32[]{:S(2)}, u32[]{:S(2)}) collective-permute-start(bf16[4,48,1792]{2,1,0:T(8,128)(2,1)} %pad_maximum_fusion.refs_13_.refs_16_), channel_id=1, source_target_pairs={{0,4},{1,3},{2,6},{3,1},{4,0},{5,7},{6,2},{7,5},{8,12},{9,11},{10,... | collective-permute-start | bytes 2064392 | tf_op jit(solution)/shard_map/ppermute | solution.py:79
  116.6 25.6 %collective-permute-start.26 = (bf16[4,48,1792]{2,1,0:T(8,128)(2,1)}, bf16[4,48,1792]{2,1,0:T(8,128)(2,1)}, u32[]{:S(2)}, u32[]{:S(2)}) collective-permute-start(bf16[4,48,1792]{2,1,0:T(8,128)(2,1)} %pad_maximum_fusion.refs_13_.refs_16_), channel_id=1, source_target_pairs={{0,1},{1,0},{2,3},{3,2},{4,5},{5,4},{6,7},{7,6},{8,9},{9,8},{10,11... | collective-permute-start | bytes 2064392 | tf_op jit(solution)/shard_map/ppermute | solution.py:79
  119.9 22.5 %collective-permute-start.5 = (bf16[4,48,1536]{2,1,0:T(8,128)(2,1)}, bf16[4,48,1536]{2,1,0:T(8,128)(2,1)}, u32[]{:S(2)}, u32[]{:S(2)}) collective-permute-start(bf16[4,48,1536]{2,1,0:T(8,128)(2,1)} %collective-permute-done.3.refs_6_.refs_9_), channel_id=1, source_target_pairs={{0,4},{1,3},{2,6},{3,1},{4,0},{5,7},{6,2},{7,5},{8,12},{9,11},{10,... | collective-permute-start | bytes 1769480 | tf_op jit(solution)/shard_map/ppermute | solution.py:79
  122.0 20.5 %collective-permute-start.7 = (bf16[4,48,1536]{2,1,0:T(8,128)(2,1)}, bf16[4,48,1536]{2,1,0:T(8,128)(2,1)}, u32[]{:S(2)}, u32[]{:S(2)}) collective-permute-start(bf16[4,48,1536]{2,1,0:T(8,128)(2,1)} %collective-permute-done.3.refs_6_.refs_9_), channel_id=1, source_target_pairs={{0,1},{1,0},{2,3},{3,2},{4,5},{5,4},{6,7},{7,6},{8,9},{9,8},{10,11... | collective-permute-start | bytes 1769480 | tf_op jit(solution)/shard_map/ppermute | solution.py:79
  134.3 18.8 %collective-permute-start.25 = (bf16[4,48,1792]{2,1,0:T(8,128)(2,1)}, bf16[4,48,1792]{2,1,0:T(8,128)(2,1)}, u32[]{:S(2)}, u32[]{:S(2)}) collective-permute-start(bf16[4,48,1792]{2,1,0:T(8,128)(2,1)} %collective-permute-done.23.refs_14_.refs_17_), channel_id=1, source_target_pairs={{0,4},{1,3},{2,6},{3,1},{4,0},{5,7},{6,2},{7,5},{8,12},{9,11},{10,... | collective-permute-start | bytes 2064392 | tf_op jit(solution)/shard_map/ppermute | solution.py:79
  152.4 28.2 %collective-permute-start.27 = (bf16[4,48,1792]{2,1,0:T(8,128)(2,1)}, bf16[4,48,1792]{2,1,0:T(8,128)(2,1)S(1)}, u32[]{:S(2)}, u32[]{:S(2)}) collective-permute-start(bf16[4,48,1792]{2,1,0:T(8,128)(2,1)} %collective-permute-done.23.refs_14_.refs_17_), channel_id=1, source_target_pairs={{0,1},{1,0},{2,3},{3,2},{4,5},{5,4},{6,7},{7,6},{8,9},{9,8},{10,11... | collective-permute-start | bytes 2064392 | tf_op jit(solution)/shard_map/ppermute | solution.py:79
  152.4 28.2 %collective-permute-start.28 = (bf16[4,48,1792]{2,1,0:T(8,128)(2,1)S(1)}, bf16[4,48,1792]{2,1,0:T(8,128)(2,1)}, u32[]{:S(2)}, u32[]{:S(2)}) collective-permute-start(bf16[4,48,1792]{2,1,0:T(8,128)(2,1)S(1)} %copy-done.19), channel_id=1, source_target_pairs={{0,1},{1,0},{2,3},{3,2},{4,5},{5,4},{6,7},{7,6},{8,9},{9,8},{10,11... | collective-permute-start | bytes 2064392 | tf_op jit(solution)/shard_map/ppermute | solution.py:79
  153.0 27.7 %collective-permute-start.19 = (bf16[4,48,1536]{2,1,0:T(8,128)(2,1)}, bf16[4,48,1536]{2,1,0:T(8,128)(2,1)S(1)}, u32[]{:S(2)}, u32[]{:S(2)}) collective-permute-start(bf16[4,48,1536]{2,1,0:T(8,128)(2,1)} %collective-permute-done.15.refs_8_.refs_11_), channel_id=1, source_target_pairs={{0,1},{1,0},{2,3},{3,2},{4,5},{5,4},{6,7},{7,6},{8,9},{9,8},{10,11... | collective-permute-start | bytes 1769480 | tf_op jit(solution)/shard_map/ppermute | solution.py:79
  153.0 27.7 %collective-permute-start.29 = (bf16[4,48,1792]{2,1,0:T(8,128)(2,1)}, bf16[4,48,1792]{2,1,0:T(8,128)(2,1)}, u32[]{:S(2)}, u32[]{:S(2)}) collective-permute-start(bf16[4,48,1792]{2,1,0:T(8,128)(2,1)} %collective-permute-done.25.refs_16_.refs_19_), channel_id=1, source_target_pairs={{0,1},{1,0},{2,3},{3,2},{4,5},{5,4},{6,7},{7,6},{8,9},{9,8},{10,11... | collective-permute-start | bytes 2064392 | tf_op jit(solution)/shard_map/ppermute | solution.py:79
  153.5 53.7 %collective-permute-start.31 = (bf16[48,49,256]{2,0,1:T(8,128)(2,1)S(1)}, bf16[48,49,256]{2,0,1:T(8,128)(2,1)S(1)}, u32[]{:S(2)}, u32[]{:S(2)}) collective-permute-start(bf16[48,49,256]{2,0,1:T(8,128)(2,1)S(1)} %copy.164), channel_id=1, source_target_pairs={{0,1},{1,0},{2,3},{3,2},{4,5},{5,4},{6,7},{7,6},{8,9},{9,8},{10,11... | collective-permute-start | bytes 3612680 | tf_op jit(solution)/shard_map/ppermute | solution.py:79
  251.6 86.3 %collective-permute-start.39 = (bf16[16,48,1536]{2,1,0:T(8,128)(2,1)}, bf16[16,48,1536]{2,1,0:T(8,128)(2,1)}, u32[]{:S(2)}, u32[]{:S(2)}) collective-permute-start(bf16[16,48,1536]{2,1,0:T(8,128)(2,1)} %get-tuple-element.130), channel_id=1, source_target_pairs={{0,1},{1,0},{2,3},{3,2},{4,5},{5,4},{6,7},{7,6},{8,9},{9,8},{10,11... | collective-permute-start | bytes 7077896 | tf_op jit(solution)/shard_map/ppermute | solution.py:79
  313.6 29.1 %collective-permute-start.33 = (bf16[16,48,1536]{2,1,0:T(8,128)(2,1)}, bf16[16,48,1536]{2,1,0:T(8,128)(2,1)}, u32[]{:S(2)}, u32[]{:S(2)}) collective-permute-start(bf16[16,48,1536]{2,1,0:T(8,128)(2,1)} %get-tuple-element.127), channel_id=1, source_target_pairs={{0,1},{1,0},{2,3},{3,2},{4,5},{5,4},{6,7},{7,6},{8,9},{9,8},{10,11... | collective-permute-start | bytes 7077896 | tf_op jit(solution)/shard_map/ppermute | solution.py:79
  336.2 18.0 %collective-permute-start.30 = (bf16[24,49,256]{2,0,1:T(8,128)(2,1)}, bf16[24,49,256]{2,0,1:T(8,128)(2,1)}, u32[]{:S(2)}, u32[]{:S(2)}) collective-permute-start(bf16[24,49,256]{2,0,1:T(8,128)(2,1)} %copy.158), channel_id=1, source_target_pairs={{0,1},{1,0},{2,3},{3,2},{4,5},{5,4},{6,7},{7,6},{8,9},{9,8},{10,11... | collective-permute-start | bytes 1806344 | tf_op jit(solution)/shard_map/ppermute | solution.py:79
  341.1 50.0 %collective-permute-start.40 = (bf16[8,48,1536]{2,1,0:T(8,128)(2,1)}, bf16[8,48,1536]{2,1,0:T(8,128)(2,1)}, u32[]{:S(2)}, u32[]{:S(2)}) collective-permute-start(bf16[8,48,1536]{2,1,0:T(8,128)(2,1)} %add_convert_fusion.1), channel_id=1, source_target_pairs={{0,4},{1,3},{2,6},{3,1},{4,0},{5,7},{6,2},{7,5},{8,12},{9,11},{10,... | collective-permute-start | bytes 3538952 | tf_op jit(solution)/shard_map/ppermute | solution.py:79
  345.4 49.3 %collective-permute-start.34 = (bf16[8,48,1536]{2,1,0:T(8,128)(2,1)}, bf16[8,48,1536]{2,1,0:T(8,128)(2,1)}, u32[]{:S(2)}, u32[]{:S(2)}) collective-permute-start(bf16[8,48,1536]{2,1,0:T(8,128)(2,1)} %add_convert_fusion.2), channel_id=1, source_target_pairs={{0,4},{1,3},{2,6},{3,1},{4,0},{5,7},{6,2},{7,5},{8,12},{9,11},{10,... | collective-permute-start | bytes 3538952 | tf_op jit(solution)/shard_map/ppermute | solution.py:79
  347.4 49.2 %collective-permute-start.46 = (bf16[8,48,1792]{2,1,0:T(8,128)(2,1)}, bf16[8,48,1792]{2,1,0:T(8,128)(2,1)}, u32[]{:S(2)}, u32[]{:S(2)}) collective-permute-start(bf16[8,48,1792]{2,1,0:T(8,128)(2,1)} %add_convert_fusion), channel_id=1, source_target_pairs={{0,4},{1,3},{2,6},{3,1},{4,0},{5,7},{6,2},{7,5},{8,12},{9,11},{10,... | collective-permute-start | bytes 4128776 | tf_op jit(solution)/shard_map/ppermute | solution.py:79
  349.7 36.1 %all-to-all-start.3 = ((f32[32,1,224]{2,1,0:T(1,128)}), f32[32,1,224]{2,1,0:T(1,128)S(1)}, u32[]{:S(2)}, u32[]{:S(2)}) async-start(f32[32,1,224]{2,1,0:T(1,128)} %all_to_all.28), calls=%async_computation.3 | async-start | bytes 65536 | tf_op jit(solution)/shard_map/all_to_all | solution.py:910
  357.6 142.7 %collective-permute-start.32 = (bf16[6,196,768]{2,1,0:T(8,128)(2,1)S(1)}, bf16[6,196,768]{2,1,0:T(8,128)(2,1)}, u32[]{:S(2)}, u32[]{:S(2)}) collective-permute-start(bf16[6,196,768]{2,1,0:T(8,128)(2,1)S(1)} %copy-done.8), channel_id=1, source_target_pairs={{0,1},{1,0},{2,3},{3,2},{4,5},{5,4},{6,7},{7,6},{8,9},{9,8},{10,11... | collective-permute-start | bytes 5419016 | tf_op jit(solution)/shard_map/ppermute | solution.py:79
  385.8 80.9 %all-to-all-start.1 = ((bf16[48,49,256]{2,1,0:T(8,128)(2,1)}), bf16[48,49,256]{2,1,0:T(8,128)(2,1)S(1)}, u32[]{:S(2)}, u32[]{:S(2)}) async-start(bf16[48,49,256]{2,1,0:T(8,128)(2,1)} %order_views.1), calls=%async_computation.1 | async-start | bytes 2752512 | tf_op jit(solution)/shard_map/all_to_all | solution.py:784
  396.4 23.2 %collective-permute-start.35 = (bf16[4,48,1536]{2,1,0:T(8,128)(2,1)S(1)}, bf16[4,48,1536]{2,1,0:T(8,128)(2,1)S(1)}, u32[]{:S(2)}, u32[]{:S(2)}) collective-permute-start(bf16[4,48,1536]{2,1,0:T(8,128)(2,1)S(1)} %add_convert_fusion.5), channel_id=1, source_target_pairs={{0,2},{1,5},{2,0},{3,7},{4,6},{5,1},{6,4},{7,3},{8,10},{9,13},{10,... | collective-permute-start | bytes 1769480 | tf_op jit(solution)/shard_map/ppermute | solution.py:79
  398.3 38.7 %collective-permute-start.47 = (bf16[4,48,1792]{2,1,0:T(8,128)(2,1)S(1)}, bf16[4,48,1792]{2,1,0:T(8,128)(2,1)S(1)}, u32[]{:S(2)}, u32[]{:S(2)}) collective-permute-start(bf16[4,48,1792]{2,1,0:T(8,128)(2,1)S(1)} %add_convert_fusion.3), channel_id=1, source_target_pairs={{0,2},{1,5},{2,0},{3,7},{4,6},{5,1},{6,4},{7,3},{8,10},{9,13},{10,... | collective-permute-start | bytes 2064392 | tf_op jit(solution)/shard_map/ppermute | solution.py:79
  405.5 15.7 %collective-permute-start.42 = (bf16[48,1536]{1,0:T(8,128)(2,1)S(1)}, bf16[48,1536]{1,0:T(8,128)(2,1)S(1)}, u32[]{:S(2)}, u32[]{:S(2)}) collective-permute-start(bf16[48,1536]{1,0:T(8,128)(2,1)S(1)} %get-tuple-element.424), channel_id=1, source_target_pairs={{0,8},{1,9},{2,10},{3,11},{4,12},{5,13},{6,14},{7,15},{8,0},{9,1},... | collective-permute-start | bytes 442376 | tf_op jit(solution)/shard_map/ppermute | solution.py:79
  408.9 24.2 %collective-permute-start.43 = (bf16[48,1536]{1,0:T(8,128)(2,1)S(1)}, bf16[48,1536]{1,0:T(8,128)(2,1)S(1)}, u32[]{:S(2)}, u32[]{:S(2)}) collective-permute-start(bf16[48,1536]{1,0:T(8,128)(2,1)S(1)} %get-tuple-element.426), channel_id=1, source_target_pairs={{0,16},{1,17},{2,18},{3,19},{4,20},{5,21},{6,22},{7,23},{8,24},{9,... | collective-permute-start | bytes 442376 | tf_op jit(solution)/shard_map/ppermute | solution.py:79
  421.2 26.5 %collective-permute-start.36 = (bf16[48,1536]{1,0:T(8,128)(2,1)S(1)}, bf16[48,1536]{1,0:T(8,128)(2,1)S(1)}, u32[]{:S(2)}, u32[]{:S(2)}) collective-permute-start(bf16[48,1536]{1,0:T(8,128)(2,1)S(1)} %get-tuple-element.427), channel_id=1, source_target_pairs={{0,8},{1,9},{2,10},{3,11},{4,12},{5,13},{6,14},{7,15},{8,0},{9,1},... | collective-permute-start | bytes 442376 | tf_op jit(solution)/shard_map/ppermute | solution.py:79
  433.1 15.1 %collective-permute-start.37 = (bf16[48,1536]{1,0:T(8,128)(2,1)S(1)}, bf16[48,1536]{1,0:T(8,128)(2,1)S(1)}, u32[]{:S(2)}, u32[]{:S(2)}) collective-permute-start(bf16[48,1536]{1,0:T(8,128)(2,1)S(1)} %get-tuple-element.429), channel_id=1, source_target_pairs={{0,16},{1,17},{2,18},{3,19},{4,20},{5,21},{6,22},{7,23},{8,24},{9,... | collective-permute-start | bytes 442376 | tf_op jit(solution)/shard_map/ppermute | solution.py:79
  433.1 17.1 %collective-permute-start.38 = (bf16[48,1536]{1,0:T(8,128)(2,1)S(1)}, bf16[48,1536]{1,0:T(8,128)(2,1)S(1)}, u32[]{:S(2)}, u32[]{:S(2)}) collective-permute-start(bf16[48,1536]{1,0:T(8,128)(2,1)S(1)} %get-tuple-element.428), channel_id=1, source_target_pairs={{0,24},{1,25},{2,26},{3,27},{4,28},{5,29},{6,30},{7,31},{8,16},{9,... | collective-permute-start | bytes 442376 | tf_op jit(solution)/shard_map/ppermute | solution.py:79
  438.5 14.4 %collective-permute-start.48 = (bf16[48,1792]{1,0:T(8,128)(2,1)S(1)}, bf16[48,1792]{1,0:T(8,128)(2,1)S(1)}, u32[]{:S(2)}, u32[]{:S(2)}) collective-permute-start(bf16[48,1792]{1,0:T(8,128)(2,1)S(1)} %get-tuple-element.421), channel_id=1, source_target_pairs={{0,8},{1,9},{2,10},{3,11},{4,12},{5,13},{6,14},{7,15},{8,0},{9,1},... | collective-permute-start | bytes 516104 | tf_op jit(solution)/shard_map/ppermute | solution.py:79
  447.7 14.1 %collective-permute-start.49 = (bf16[48,1792]{1,0:T(8,128)(2,1)S(1)}, bf16[48,1792]{1,0:T(8,128)(2,1)S(1)}, u32[]{:S(2)}, u32[]{:S(2)}) collective-permute-start(bf16[48,1792]{1,0:T(8,128)(2,1)S(1)} %get-tuple-element.423), channel_id=1, source_target_pairs={{0,16},{1,17},{2,18},{3,19},{4,20},{5,21},{6,22},{7,23},{8,24},{9,... | collective-permute-start | bytes 516104 | tf_op jit(solution)/shard_map/ppermute | solution.py:79
  448.2 13.6 %collective-permute-start.50 = (bf16[48,1792]{1,0:T(8,128)(2,1)S(1)}, bf16[48,1792]{1,0:T(8,128)(2,1)S(1)}, u32[]{:S(2)}, u32[]{:S(2)}) collective-permute-start(bf16[48,1792]{1,0:T(8,128)(2,1)S(1)} %get-tuple-element.422), channel_id=1, source_target_pairs={{0,24},{1,25},{2,26},{3,27},{4,28},{5,29},{6,30},{7,31},{8,16},{9,... | collective-permute-start | bytes 516104 | tf_op jit(solution)/shard_map/ppermute | solution.py:79
  466.7 22.4 %all-to-all-start.4 = ((f32[32,8,128]{2,1,0:T(8,128)}), f32[32,8,128]{2,1,0:T(8,128)S(1)}, u32[]{:S(2)}, u32[]{:S(2)}) async-start(f32[32,8,128]{2,1,0:T(8,128)} %squares.1), calls=%async_computation.4 | async-start | bytes 262144 | tf_op jit(solution)/shard_map/all_to_all | solution.py:954
  494.4 15.3 %all-to-all-start.5 = ((f32[32,8,128]{2,1,0:T(8,128)}), f32[32,8,128]{2,1,0:T(8,128)S(1)}, u32[]{:S(2)}, u32[]{:S(2)}) async-start(f32[32,8,128]{2,1,0:T(8,128)} %get-tuple-element.140), calls=%async_computation.5 | async-start | bytes 262144 | tf_op jit(solution)/shard_map/all_to_all | solution.py:964
  (31 other events, 415.8 us)

commit v2 on v1

--- a/solution.py
+++ b/solution.py
@@ -83,23 +83,85 @@
 Z_STEPS = (4, 8, 12)
 
 
-def gather_chunk(shard, peers):
-    if peers != FAST_PEERS:
-        return [lax.all_gather(lax.all_gather(shard, "dp", axis=0, tiled=True), "mp", axis=0)]
-    along = jnp.stack([shard] + [swap(shard, peers, bits) for bits in Z_STEPS])
-    first = swap(along, peers, (1, 2))
-    mine = [along, first, swap(along, peers, (2, 1)), swap(first, peers, (2, 1))]
-    return mine + [swap(piece, peers, 0, 1) for piece in mine]
+def after(array, *others):
+    return lax.optimization_barrier((array,) + others)[0]
+
+
+def reach_z(shard, peers):
+    return [swap(shard, peers, bits) for bits in Z_STEPS]
+
+
+def hold_all(arrays, others):
+    return list(lax.optimization_barrier((tuple(arrays), tuple(others)))[0])
+
+
+def gather_plain(shard):
+    return [lax.all_gather(lax.all_gather(shard, "dp", axis=0, tiled=True), "mp", axis=0)]
+
+
+class Gather:
+    def __init__(self, shards, peers):
+        self.peers = peers
+        self.one, self.two, self.three = shards
+
+    def near(self, array):
+        return swap(array, self.peers, (1, 2))
+
+    def far(self, array):
+        return swap(array, self.peers, (2, 1))
+
+    def across(self, array):
+        return swap(array, self.peers, 0, 1)
+
+    def begin(self, beside_z, beside_near):
+        z_one = reach_z(self.one, self.peers)
+        (along_one,) = hold_all([jnp.stack([self.one] + z_one)], beside_z)
+        (two,) = hold_all([self.two], z_one)
+        near_one, z_two = self.near(along_one), reach_z(two, self.peers)
+        done = [near_one] + z_two + list(beside_near(along_one))
+        half_one, along_two, three = hold_all(
+            [jnp.concatenate([along_one, near_one]), jnp.stack([two] + z_two), self.three], done
+        )
+        far_one, side_one = self.far(half_one), self.across(half_one)
+        near_two, z_three = self.near(along_two), reach_z(three, self.peers)
+        far_one, half_two, along_three = hold_all(
+            [far_one, jnp.concatenate([along_two, near_two]), jnp.stack([three] + z_three)],
+            [far_one, near_two] + z_three,
+        )
+        self.half_two, self.along_three = half_two, along_three
+        self.far_two, self.side_two = self.far(half_two), self.across(half_two)
+        self.near_three = self.near(along_three)
+        return [half_one, far_one, side_one, self.across(far_one)]
+
+    def later(self):
+        return [self.far_two, self.near_three, self.side_two]
+
+    def second(self, beside):
+        far_two, along_three, near_three = hold_all(
+            [self.far_two, self.along_three, self.near_three], [beside]
+        )
+        self.half_three = jnp.concatenate([along_three, near_three])
+        self.far_three, self.side_three = self.far(self.half_three), self.across(self.half_three)
+        self.parts_two = [self.half_two, far_two, self.side_two, self.across(far_two)]
+
+    def finish(self, beside):
+        (far_three,) = hold_all([self.far_three], [beside] + self.parts_two[2:])
+        parts_three = [self.half_three, far_three, self.side_three, self.across(far_three)]
+        return self.parts_two, parts_three
+
+
+PIECE = 8
 
 
 def gather_table(me, core):
     one = jnp.where(core == 0, 1, 2)
     two = 3 - one
-    zero = jnp.zeros_like(one)
-    bases = jnp.stack([zero, one, two, one * 0 + 3, zero, two, one, one * 0 + 3])
-    owners = me ^ bases[:, None] ^ jnp.array((0,) + Z_STEPS, jnp.int32)[None, :]
-    cores = jnp.stack([core] * 4 + [1 - core] * 4)
-    return jnp.concatenate([owners.reshape(-1), cores]).astype(jnp.int32)
+    along = jnp.array((0,) + Z_STEPS, jnp.int32)
+    mine = jnp.concatenate([along, along ^ one])
+    theirs = jnp.concatenate([along, along ^ two])
+    apart = jnp.concatenate([mine, mine ^ two, theirs, theirs ^ one])
+    cores = jnp.stack([core, core, 1 - core, 1 - core])
+    return jnp.concatenate([me ^ apart, cores]).astype(jnp.int32)
 
 
 def weight_copies(parts, table, target, sems):
@@ -107,13 +169,14 @@
         return [pltpu.make_async_copy(parts[0], target, sems.at[0])]
     copies = []
     for index, part in enumerate(parts):
-        half = table[len(parts) * 4 + index]
-        for inner in range(4):
+        half = table[len(parts) * PIECE + index]
+        for inner in range(PIECE):
+            at = index * PIECE + inner
             rows = part.shape[1]
-            start = pl.multiple_of(table[index * 4 + inner] * rows, ROUND)
+            start = pl.multiple_of(table[at] * rows, ROUND)
             copies.append(
                 pltpu.make_async_copy(
-                    part.at[inner], target.at[half, pl.ds(start, rows), :], sems.at[index * 4 + inner]
+                    part.at[inner], target.at[half, pl.ds(start, rows), :], sems.at[at]
                 )
             )
     return copies
@@ -128,21 +191,50 @@
     ).astype(jnp.int32)
 
 
-def scatter_chunk(mine, other, peers):
+def add(*terms):
+    return sum(term.astype(F32) for term in terms)
+
+
+def leaf(send):
+    return send[0] if isinstance(send, tuple) else send
+
+
+def scatter_start(pair, peers):
+    mine, got = pair
     if peers != FAST_PEERS:
-        whole = mine.astype(F32) + swap(other, peers, 0, 1).astype(F32)
+        return [mine, got]
+    return [(mine, got), add(mine[8:], got[8:]).astype(BF16)]
+
+
+def scatter_near(state, peers, *held):
+    if peers != FAST_PEERS:
+        return state
+    terms, send = state
+    got = swap(leaf(send), peers, (2, 1))
+    terms = terms + (after(got, *held) if held else got,)
+    return [terms, add(*(term[4:8] for term in terms)).astype(BF16)]
+
+
+def scatter_far(state, peers, *held):
+    if peers != FAST_PEERS:
+        return state
+    terms, send = state
+    got = swap(leaf(send), peers, (1, 2))
+    terms = terms + (after(got, *held) if held else got,)
+    return [terms, tuple(add(*(term[i] for term in terms)).astype(BF16) for i in (1, 2, 3))]
+
+
+def scatter_end(state, peers, *held):
+    if peers != FAST_PEERS:
+        mine, got = state
+        whole = mine.astype(F32) + got.astype(F32)
         return lax.psum_scatter(
             whole.reshape(-1, whole.shape[-1]), "dp", scatter_dimension=0, tiled=True
         )
-    got = swap(other, peers, 0, 1)
-    add = lambda *terms: sum(term.astype(F32) for term in terms)
-    got_one = swap(add(mine[8:], got[8:]).astype(BF16), peers, (2, 1))
-    got_two = swap(add(mine[4:8], got[4:8], got_one[4:]).astype(BF16), peers, (1, 2))
-    last = [
-        swap(add(mine[i], got[i], got_one[i], got_two[i]).astype(BF16), peers, Z_STEPS[i - 1])
-        for i in (1, 2, 3)
-    ]
-    return add(mine[0], got[0], got_one[0], got_two[0], *last)
+    terms, sends = state
+    last = [swap(send, peers, bits) for send, bits in zip(sends, Z_STEPS)]
+    last = hold_all(last, held) if held else last
+    return add(*(term[0] for term in terms), *last)
 
 
 def view_of(rows, per_view):
@@ -164,12 +256,9 @@
     return (low * scale).astype(BF16), ((1.0 - low) * scale).astype(BF16)
 
 
-def attn_forward(mp_s, counts_s, table, tokens, norms, *rest, nparts, per_view, part):
-    parts, (first_o, packed_o, attended_o, middle_o, second_o, lse_o), (weights, sems) = (
-        rest[:nparts],
-        rest[nparts : nparts + 6],
-        rest[nparts + 6 :],
-    )
+def attn_forward(mp_s, counts_s, table, tokens, norms, *rest, nparts, per_view, part, begin, here):
+    parts = rest[:nparts]
+    first_o, packed_o, attended_o, middle_o, second_o, lse_o, weights, sems = rest[-8:]
     step = pl.program_id(0)
     copies = weight_copies(parts, table, weights, sems)
 
@@ -186,7 +275,8 @@
     normed, _ = norm_rows(values)
     first = (normed * norms[0:1, :] + norms[1:2, :]).astype(BF16)
     first_o[...] = first
-    bias = allowed_bias(size, counts_s[mp_s[0] * pl.num_programs(0) + step], per_view)
+    bias = allowed_bias(size, counts_s[mp_s[0] * here + begin + step], per_view)
+    bias = jnp.concatenate([bias, bias], axis=0)
     masks = pair_masks(scale)
     lane = lax.broadcasted_iota(jnp.int32, (size, 2 * HEADDIM), 1)
     wide = 2 * HEADDIM
@@ -195,22 +285,27 @@
     for half in range(2):
         packed = mm(first, weights[half, :, : 3 * part]).astype(BF16)
         packed_o[:, half * 3 * part : (half + 1) * 3 * part] = packed
-        for pair in range(part // wide):
+        pairs = range(part // wide)
+        logits, probs = [], []
+        for pair in pairs:
             at = pair * wide
             query = packed[:, at : at + wide]
             key = packed[:, part + at : part + at + wide]
-            value = packed[:, 2 * part + at : 2 * part + at + wide]
-            outs = []
-            for which in range(2):
-                logits = mm(query * masks[which], key, NT) + bias
-                top = jnp.max(logits, axis=-1, keepdims=True)
-                exponent = jnp.exp(logits - top)
-                total = jnp.sum(exponent, axis=-1, keepdims=True)
-                probs = (exponent * (1.0 / total)).astype(BF16)
-                outs.append(mm(probs, value))
-                index = half * (part // HEADDIM) + pair * 2 + which
-                lse = jnp.where(lane == index, top + jnp.log(total), lse)
-            both = jnp.where(lane < HEADDIM, outs[0], outs[1]).astype(BF16)
+            both = jnp.concatenate([query * masks[0], query * masks[1]], axis=0)
+            logits.append(mm(both, key, NT) + bias)
+        for pair in pairs:
+            top = jnp.max(logits[pair], axis=-1, keepdims=True)
+            exponent = jnp.exp(logits[pair] - top)
+            total = jnp.sum(exponent, axis=-1, keepdims=True)
+            probs.append((exponent * (1.0 / total)).astype(BF16))
+            top = top + jnp.log(total)
+            index = half * (part // HEADDIM) + pair * 2
+            lse = jnp.where(lane == index, top[:size], lse)
+            lse = jnp.where(lane == index + 1, top[size:], lse)
+        for pair in pairs:
+            at = pair * wide
+            outs = mm(probs[pair], packed[:, 2 * part + at : 2 * part + at + wide])
+            both = jnp.where(lane < HEADDIM, outs[:size], outs[size:]).astype(BF16)
             attended_o[:, half * part + at : half * part + at + wide] = both
         attn = attn + mm(
             attended_o[:, half * part : (half + 1) * part], weights[half, :, 3 * part :], NT
@@ -324,13 +419,10 @@
 
 
 def attn_backward(
-    mp_s, counts_s, table, tokens, packed, lse, mid, norms, *rest, nparts, per_view, part
+    mp_s, counts_s, table, tokens, packed, lse, mid, norms, *rest, nparts, per_view, part, begin, here
 ):
-    parts, (packed_o, tokens_o, sums_o), (weights, sems) = (
-        rest[:nparts],
-        rest[nparts : nparts + 3],
-        rest[nparts + 3 :],
-    )
+    parts = rest[:nparts]
+    packed_o, tokens_o, sums_o, weights, sems = rest[-5:]
     step = pl.program_id(0)
     copies = weight_copies(parts, table, weights, sems)
 
@@ -345,8 +437,9 @@
     size = tokens.shape[0]
     scale = 1.0 / math.sqrt(HEADDIM)
     wide = 2 * HEADDIM
-    bias = allowed_bias(size, counts_s[mp_s[0] * pl.num_programs(0) + step], per_view)
-    scaled_masks, masks = pair_masks(scale), pair_masks(1.0)
+    bias = allowed_bias(size, counts_s[mp_s[0] * here + begin + step], per_view)
+    bias = jnp.concatenate([bias, bias], axis=0)
+    masks = pair_masks(1.0)
     lane = lax.broadcasted_iota(jnp.int32, (size, wide), 1)
     low = lane < HEADDIM
     middle = mid[...]
@@ -355,31 +448,39 @@
     for half in range(2):
         grad_att = mm(middle_low, weights[half, :, 3 * part :]).astype(BF16)
         base = half * 3 * part
-        for pair in range(part // wide):
+        pairs = range(part // wide)
+        sides, logits, grad_probs, lows = [], [], [], []
+        for pair in pairs:
             at = pair * wide
             query = packed[:, base + at : base + at + wide]
             key = packed[:, base + part + at : base + part + at + wide]
             value = packed[:, base + 2 * part + at : base + 2 * part + at + wide]
             grad = grad_att[:, at : at + wide]
-            outs = []
-            for which in range(2):
-                index = half * (part // HEADDIM) + pair * 2 + which
-                logits = mm(query * scaled_masks[which], key, NT) + bias
-                probs = jnp.exp(logits - lse[:, index : index + 1])
-                grad_probs = mm(grad * masks[which], value, NT)
-                weighted = probs * grad_probs
-                centre = jnp.sum(weighted, axis=-1, keepdims=True)
-                scores = ((weighted - probs * centre) * scale).astype(BF16)
-                outs.append(
-                    (
-                        mm(scores, key),
-                        mm(scores, query, TN),
-                        mm(probs.astype(BF16), grad, TN),
-                    )
-                )
-            for kind in range(3):
-                both = jnp.where(low, outs[0][kind], outs[1][kind]).astype(BF16)
-                packed_o[:, base + kind * part + at : base + kind * part + at + wide] = both
+            query = jnp.concatenate([query * masks[0], query * masks[1]], axis=0)
+            grad = jnp.concatenate([grad * masks[0], grad * masks[1]], axis=0)
+            sides.append((query, key, grad))
+            logits.append(mm(query, key, NT) * scale + bias)
+            grad_probs.append(mm(grad, value, NT))
+        for pair in pairs:
+            index = half * (part // HEADDIM) + pair * 2
+            top = jnp.concatenate([lse[:, index : index + 1], lse[:, index + 1 : index + 2]], axis=0)
+            probs = jnp.exp(logits[pair] - top)
+            weighted = probs * grad_probs[pair]
+            centre = jnp.sum(weighted, axis=-1, keepdims=True)
+            scores = ((weighted - probs * centre) * scale).astype(BF16)
+            lows.append((scores, probs.astype(BF16)))
+        for pair in pairs:
+            query, key, grad = sides[pair]
+            scores, probs = lows[pair]
+            at = base + pair * wide
+            grad_query = mm(scores, key)
+            packed_o[:, at : at + wide] = jnp.where(
+                low, grad_query[:size], grad_query[size:]
+            ).astype(BF16)
+            at = at + part
+            packed_o[:, at : at + wide] = mm(scores, query, TN).astype(BF16)
+            at = at + part
+            packed_o[:, at : at + wide] = mm(probs, grad, TN).astype(BF16)
         back = back + mm(packed_o[:, base : base + 3 * part], weights[half, :, : 3 * part], NT)
     normed, inverse = norm_rows(tokens[...].astype(F32))
     sums_o[0:1, :] += jnp.sum(back * normed, axis=0, keepdims=True)
@@ -388,72 +489,79 @@
     tokens_o[0] = grads[: tokens_o.shape[1]].astype(BF16)
 
 
-def weight_grad(mp_s, places, *rest, steps, rows_each):
-    count = 2 * len(steps)
-    sides, (other_o, mine_o), turned = rest[:count], rest[count : count + 2], rest[count + 2 :]
-    half, step = pl.program_id(0), pl.program_id(1)
+def weight_grad(side_s, places, *rest, steps, rows_each):
+    count = len(steps)
+    sides, (grads_o, left_pad, right_pad) = rest[: 2 * count], rest[2 * count :]
+    step = pl.program_id(0)
     begin = 0
-    blocks = other_o.shape[0]
+    blocks = grads_o.shape[0]
+
+    @pl.when(step == 0)
+    def _():
+        left_pad[...] = jnp.zeros_like(left_pad)
+        right_pad[...] = jnp.zeros_like(right_pad)
+
     for index, length in enumerate(steps):
-        left, right, flip = sides[2 * index], sides[2 * index + 1], turned[index]
-
-        @pl.when((half == 0) & (step == begin))
-        def _(left=left, flip=flip):
-            flip[...] = left[...].T
+        left, right = sides[2 * index], sides[2 * index + 1]
+
+        @pl.when(step == begin)
+        def _(left=left):
+            left_pad[: left.shape[0], :] = left[...]
 
         @pl.when((step >= begin) & (step < begin + length))
-        def _(right=right, flip=flip):
-            product = mm(flip[...], right[...]).astype(BF16)
-
-            @pl.when(half == 0)
-            def _():
-                for block in range(blocks):
-                    other_o[places[blocks + block]] = product[block * rows_each : (block + 1) * rows_each]
-
-            @pl.when(half == 1)
-            def _():
-                for block in range(blocks):
-                    mine_o[places[block]] = product[block * rows_each : (block + 1) * rows_each]
+        def _(right=right):
+            right_pad[: right.shape[0], :] = right[...]
 
         begin += length
-
-
-def take_cells(slot_s, live_s, spots, *rest, each):
-    cells, (rows_o, sums_o) = rest[:each], rest[each:]
+    product = mm(left_pad[...], right_pad[...], TN).astype(BF16)
+    for block in range(blocks):
+        grads_o[places[block]] = product[block * rows_each : (block + 1) * rows_each]
+
+
+def take_cells(where_s, marks, live_row, cells, rows_o, sums_o, *, per_view, stride):
     step = pl.program_id(0)
 
     @pl.when(step == 0)
     def _():
         sums_o[...] = jnp.zeros_like(sums_o)
 
-    grid, width = cells[0].shape[1], spots.shape[1]
-    per_view = rows_o.shape[1]
-    cell = lax.broadcasted_iota(jnp.int32, (grid, width), 0)
-    lane = lax.broadcasted_iota(jnp.int32, (grid, width), 1)
+    grid, each, dec = cells.shape
+    flat = cells[...].reshape(grid * each, dec)
+    lane = lax.broadcasted_iota(jnp.int32, (each * stride, grid * each), 1)
+    pick = (marks[...] == lane).astype(F32)
+    covered = jnp.sum(pick, axis=0, keepdims=True)
+    open_cells = jnp.broadcast_to(live_row[0] - covered, (8, grid * each)).astype(BF16)
+    taken = mm(pick.astype(BF16), flat)
+    masked = mm(open_cells, flat)
+    for index in range(each):
+        rows_o[where_s[step * each + index]] = taken[index * stride : index * stride + per_view].astype(BF16)
+    sums_o[0:1, :] += jnp.sum(taken, axis=0, keepdims=True)
+    sums_o[1:2, :] += masked[0:1]
+
+
+def put_cells(where_s, live_s, marks, mask, positions, rows, cells_o, held):
+    step = pl.program_id(0)
+    grid, each, dec = cells_o.shape
+    per_view = rows.shape[1]
+    stride = held.shape[0] // each
+
+    @pl.when(step == 0)
+    def _():
+        held[...] = jnp.zeros_like(held)
+
+    slot = lax.broadcasted_iota(jnp.int32, (1, each, 1), 1)
+    live = jnp.zeros((1, each, 1), F32)
     for index in range(each):
         at = step * each + index
-        live = live_s[at].astype(F32)
-        place = (spots[pl.ds(at, 1), :] == cell).astype(F32)
-        covered = jnp.sum(place, axis=1, keepdims=True)
-        pick = (jnp.where(lane == per_view, 1.0 - covered, place) * live).astype(BF16)
-        taken = mm(pick, cells[index][0], TN)
-        rows_o[index] = taken[:per_view].astype(BF16)
-        sums_o[0:1, :] += jnp.sum(taken[:per_view], axis=0, keepdims=True)
-        sums_o[1:2, :] += taken[per_view : per_view + 1]
-
-
-def put_cells(where_s, live_s, spots, mask, positions, *rest, each):
-    rows, (cells_o,) = rest[:each], rest[each:]
-    step = pl.program_id(0)
-    grid, per_view = cells_o.shape[1], rows[0].shape[1]
-    cell = lax.broadcasted_iota(jnp.int32, (grid, per_view), 0)
-    for index in range(each):
-        at = where_s[step * each + index]
-        live = live_s[at].astype(F32)
-        place = (spots[pl.ds(at, 1), :][:, :per_view] == cell).astype(F32)
-        covered = jnp.sum(place, axis=1, keepdims=True)
-        filled = mm(place.astype(BF16), rows[index][0]) + (1.0 - covered) * mask[...]
-        cells_o[index] = (live * filled + positions[...]).astype(BF16)
+        held[index * stride : index * stride + per_view, :] = rows[where_s[at]]
+        live = jnp.where(slot == index, live_s[at].astype(F32), live)
+    line = lax.broadcasted_iota(jnp.int32, (grid * each, held.shape[0]), 0)
+    place = (marks[0] == line).astype(F32)
+    covered = jnp.sum(place, axis=1, keepdims=True)
+    live = jnp.broadcast_to(live, (grid, each, 1)).reshape(grid * each, 1)
+    filled = mm(place.astype(BF16), held[...]) + (live - covered) * mask[...]
+    filled = filled.reshape(grid, each, dec) + positions[...][:, None, :]
+    cells_o[...] = filled.astype(BF16)
 
 
 def order_views(where_s, mp_s, own, theirs, out, sems):
@@ -661,83 +769,134 @@
         .astype(F32)
     )
     mask_token = lax.dynamic_index_in_dim(dec_full[1], core, 0, keepdims=True)
-    slot_pos, live_pos = got[:, 1], got[:, 2]
-    width = -(-(per_view + 1) // 8) * 8
-    spots = jnp.concatenate(
-        [got[:, 3:], jnp.full((npos, width - per_view), -1, jnp.int32)], axis=1
-    )
-    filled = (slot_pos[None, :] == jnp.arange(nviews, dtype=jnp.int32)[:, None]) & (
+    held_slot = got[:, 1]
+    filled = (held_slot[None, :] == jnp.arange(nviews, dtype=jnp.int32)[:, None]) & (
         got[:, 0][None, :] > 0
     )
     where_slot = jnp.sum(
         jnp.where(filled, jnp.arange(npos, dtype=jnp.int32)[None, :], 0), axis=1
     ).astype(jnp.int32)
-
-    parts_a, parts_b, parts_c = (gather_chunk(c, peers) for c in (chunk_a, chunk_b, chunk_c))
-    nparts = len(parts_a)
-    table = gather_table(me, core)
-    nsem = 4 * nparts if fast else 1
-
-    each = 4
-    cot_spec = lambda index: pl.BlockSpec(
-        (1, cells, dec), lambda i, slot, live, index=index: (slot[i * each + index], 0, 0)
-    )
-    returned, dec_sums = pl.pallas_call(
-        lambda *refs: take_cells(*refs, each=each),
+    owned = jnp.dot(
+        filled.astype(BF16), got.astype(BF16), preferred_element_type=F32
+    ).astype(jnp.int32)
+    live_slot, owned_spots = owned[:, 2], owned[:, 3:]
+    each = 8
+    groups = nviews // each
+    marks = jnp.where(
+        live_slot[:, None] > 0,
+        owned_spots * each + (jnp.arange(nviews, dtype=jnp.int32) % each)[:, None],
+        -1,
+    )
+    stride_take, stride_put = -(-per_view // 8) * 8, -(-per_view // 64) * 64
+    take_marks = jnp.pad(marks, ((0, 0), (0, stride_take - per_view)), constant_values=-1)
+    take_marks = take_marks.reshape(nviews * stride_take, 1)
+    put_marks = jnp.pad(marks, ((0, 0), (0, stride_put - per_view)), constant_values=-1)
+    put_marks = put_marks.reshape(groups, 1, each * stride_put)
+    live_row = jnp.broadcast_to(
+        live_slot.astype(F32).reshape(groups, 1, each), (groups, cells, each)
+    ).reshape(groups, 1, cells * each)
+
+    take_call = pl.pallas_call(
+        lambda *refs: take_cells(*refs, per_view=per_view, stride=stride_take),
         out_shape=[shape((npos, per_view, dec), BF16), shape((8, dec))],
         grid_spec=pltpu.PrefetchScalarGridSpec(
-            num_scalar_prefetch=2,
-            grid=(npos // each,),
-            in_specs=[pl.BlockSpec((npos, width), lambda i, *_: (0, 0))]
-            + [cot_spec(index) for index in range(each)],
+            num_scalar_prefetch=1,
+            grid=(groups,),
+            in_specs=[
+                pl.BlockSpec((each * stride_take, 1), lambda i, _: (i, 0)),
+                pl.BlockSpec((1, 1, cells * each), lambda i, _: (i, 0, 0)),
+                pl.BlockSpec((cells, each, dec), lambda i, _: (0, i, 0)),
+            ],
             out_specs=[
-                pl.BlockSpec((each, per_view, dec), lambda i, *_: (i, 0, 0)),
-                pl.BlockSpec((8, dec), lambda i, *_: (0, 0)),
+                pl.BlockSpec((npos, per_view, dec), lambda i, _: (0, 0, 0)),
+                pl.BlockSpec((8, dec), lambda i, _: (0, 0)),
             ],
         ),
         compiler_params=params(),
-        cost_estimate=cost(2 * npos * cells * 56 * dec, cotangent.size * 2),
+        cost_estimate=cost(2 * nviews * stride_take * cells * each * dec, cotangent.size * 2),
         name="take_cells",
-    )(slot_pos, live_pos, spots, *([cotangent] * each))
-    came_mine = lax.all_to_all(returned, "dp", split_axis=0, concat_axis=0, tiled=True)
-    came_theirs = swap(came_mine, peers, 0, 1)
+    )
 
     start = core * (here * span)
     own = lax.dynamic_slice_in_dim(tokens, start, here * span, 0).reshape(here, span, model)
     own = jnp.pad(own, ((0, 0), (0, size - span), (0, 0))).reshape(rows, model)
+    taken = []
+
+    def take(*others):
+        marks_held = after(take_marks, *others) if others else take_marks
+        taken.extend(take_call(where_slot, marks_held, live_row, cotangent.transpose(1, 0, 2)))
+        return taken[:1]
+
+    if fast:
+        gather = Gather((chunk_a, chunk_b, chunk_c), peers)
+        parts_a = gather.begin((own, take_marks), take)
+    else:
+        take()
+        parts_a = gather_plain(chunk_a)
+    returned, dec_sums = taken
+    nparts = len(parts_a)
+    table = gather_table(me, core)
+    nsem = PIECE * nparts if fast else 1
+
     smem = pl.BlockSpec(memory_space=pltpu.SMEM)
-    ep = lambda cols: pl.BlockSpec((size, cols), lambda i: (i, 0))
     fixed = lambda dims: pl.BlockSpec(dims, lambda i: (0,) * len(dims))
     chunk_cols = [chunk_a.shape[1], chunk_b.shape[1], chunk_c.shape[1]]
     weight_bytes = [2 * 2 * model * cols for cols in chunk_cols]
-    first, packed, attended, middle, second, lse = pl.pallas_call(
-        lambda *refs: attn_forward(*refs, nparts=nparts, per_view=per_view, part=part),
-        grid=(here,),
-        out_shape=[
-            shape((rows, model), BF16),
-            shape((rows, 6 * part), BF16),
-            shape((rows, 2 * part), BF16),
-            shape((rows, model)),
-            shape((rows, model), BF16),
-            shape((rows, 2 * HEADDIM)),
-        ],
-        in_specs=[smem, smem, smem, ep(model), fixed((8, model))] + [any_spec()] * nparts,
-        out_specs=[ep(model), ep(6 * part), ep(2 * part), ep(model), ep(model), ep(2 * HEADDIM)],
-        scratch_shapes=[
-            pltpu.VMEM((2, model, chunk_cols[0]), BF16),
-            pltpu.SemaphoreType.DMA((nsem,)),
-        ],
-        compiler_params=params(),
-        cost_estimate=cost(3 * 2 * rows * model * 8 * part, weight_bytes[0] + rows * model * 16),
-        name="attn_forward",
-    )(core_s, counts, table, own, norms, *parts_a)
+    calls = 2 if here % 2 == 0 else 1
+    each_call = here // calls
+
+    def attn_forward_call(call, own, earlier):
+        begin = call * each_call
+        ep = lambda cols: pl.BlockSpec((size, cols), lambda i: (i + begin, 0))
+        return pl.pallas_call(
+            lambda *refs: attn_forward(
+                *refs, nparts=nparts, per_view=per_view, part=part, begin=begin, here=here
+            ),
+            grid=(each_call,),
+            out_shape=[
+                shape((rows, model), BF16),
+                shape((rows, 6 * part), BF16),
+                shape((rows, 2 * part), BF16),
+                shape((rows, model)),
+                shape((rows, model), BF16),
+                shape((rows, 2 * HEADDIM)),
+            ],
+            in_specs=[smem, smem, smem, ep(model), fixed((8, model))]
+            + [any_spec()] * (nparts + len(earlier)),
+            out_specs=[ep(model), ep(6 * part), ep(2 * part), ep(model), ep(model), ep(2 * HEADDIM)],
+            scratch_shapes=[
+                pltpu.VMEM((2, model, chunk_cols[0]), BF16),
+                pltpu.SemaphoreType.DMA((nsem,)),
+            ],
+            input_output_aliases={5 + nparts + index: index for index in range(len(earlier))},
+            compiler_params=params(),
+            cost_estimate=cost(
+                6 * rows * model * 8 * part // calls, weight_bytes[0] + rows * model * 16 // calls
+            ),
+            name="attn_forward",
+        )(core_s, counts, table, own, norms, *parts_a, *earlier)
+
+    attn = []
+    for call in range(calls):
+        gates = gather.later() if fast and call > 0 else []
+        attn = attn_forward_call(call, after(own, *gates) if gates else own, attn)
+        if call == 0 and fast:
+            returned = after(returned, gather.near_three)
+            gather.second(attn[0])
+    if fast:
+        parts_b, parts_c = gather.finish(attn[0])
+    else:
+        parts_b, parts_c = gather_plain(chunk_b), gather_plain(chunk_c)
+    came_mine = lax.all_to_all(returned, "dp", split_axis=0, concat_axis=0, tiled=True)
+    came_theirs = swap(came_mine, peers, 0, 1)
+    first, packed, attended, middle, second, lse = attn
 
     group = 2
     chunk = group * size
     steps = here // group
     gviews = group * views_each
     blk = lambda cols: pl.BlockSpec((chunk, cols), lambda i: (i, 0))
-    wide = 512 if hidden % 512 == 0 else hidden
+    wide = hidden
     mlp_scratch = [
         pltpu.VMEM((2, model, chunk_cols[1]), BF16),
         pltpu.VMEM((2, model, chunk_cols[2]), BF16),
@@ -770,19 +929,6 @@
         name="mlp_forward",
     )(core_s, table, second, middle, dec_full[0], *parts_b, *parts_c)
 
-    emb_other = swap(emb_send, peers, 0, 1)
-    outgoing = pl.pallas_call(
-        order_views,
-        out_shape=shape((npos, per_view, dec), BF16),
-        in_specs=[smem, smem, any_spec(), any_spec()],
-        out_specs=any_spec(),
-        scratch_shapes=[pltpu.SemaphoreType.DMA((nviews,))],
-        compiler_params=params(8 << 20),
-        cost_estimate=cost(0, 4 * nviews * per_view * dec),
-        name="order_views",
-    )(where_view, core_s, emb_keep, emb_other)
-    arrived = lax.all_to_all(outgoing, "dp", split_axis=0, concat_axis=0, tiled=True)
-
     where_mine = lax.dynamic_slice_in_dim(where_view, core * (nviews // cores), nviews // cores)
     emb_rows, glow, gpre, gmid, gmid_low, ln_two = pl.pallas_call(
         lambda *refs: mlp_backward(
@@ -815,85 +961,133 @@
         name="mlp_backward",
     )(core_s, where_mine, table, came_mine, came_theirs, slope, middle, norms, *parts_b, *parts_c)
 
+    emb_other = swap(emb_send, peers, 0, 1)
+    if fast:
+        emb_other = after(emb_other, glow)
+    outgoing = pl.pallas_call(
+        order_views,
+        out_shape=shape((npos, per_view, dec), BF16),
+        in_specs=[smem, smem, any_spec(), any_spec()],
+        out_specs=any_spec(),
+        scratch_shapes=[pltpu.SemaphoreType.DMA((nviews,))],
+        compiler_params=params(8 << 20),
+        cost_estimate=cost(0, 4 * nviews * per_view * dec),
+        name="order_views",
+    )(where_view, core_s, emb_keep, emb_other)
+    arrived = lax.all_to_all(outgoing, "dp", split_axis=0, concat_axis=0, tiled=True)
+
     blocks = FAST_PEERS
     if fast:
-        places = jnp.concatenate([place_table(me, core), place_table(me, 1 - core)])
+        places = [place_table(me, core), place_table(me, 1 - core)]
     else:
-        places = jnp.tile(jnp.arange(blocks, dtype=jnp.int32), 2)
-
-    def grads_of(pairs, block, name):
+        places = [jnp.arange(blocks, dtype=jnp.int32)] * 2
+
+    deep = -(-rows // 256) * 256
+
+    def side_grads(pairs, block, name, mine):
         lengths = [right.shape[1] // 2 // block for _, right in pairs]
         many = sum(lengths)
         begins = [sum(lengths[:index]) for index in range(len(lengths))]
 
         def column(begin, length):
-            def at(h, j, core_ref, places_ref):
-                side = jnp.where(h == 0, 1 - core_ref[0], core_ref[0])
-                return (0, side * length + jnp.clip(j - begin, 0, length - 1))
-
-            return at
+            return lambda j, side, _: (0, side[0] * length + jnp.clip(j - begin, 0, length - 1))
 
         in_specs, operands = [], []
-        for (left, right), begin, length in zip(pairs, begins, lengths):
+        for index, (left, right) in enumerate(pairs):
             in_specs += [
-                pl.BlockSpec((rows, model), lambda h, j, *_: (0, 0)),
-                pl.BlockSpec((rows, block), column(begin, length)),
+                pl.BlockSpec((rows, model), lambda j, *_: (0, 0)),
+                pl.BlockSpec((rows, block), column(begins[index], lengths[index])),
             ]
             operands += [left, right]
-        other, mine = pl.pallas_call(
+        grad_shape = (blocks, model // blocks, many * block)
+        return pl.pallas_call(
             lambda *refs: weight_grad(*refs, steps=lengths, rows_each=model // blocks),
-            out_shape=[shape((blocks, model // blocks, many * block), BF16)] * 2,
+            out_shape=shape(grad_shape, BF16),
             grid_spec=pltpu.PrefetchScalarGridSpec(
                 num_scalar_prefetch=2,
-                grid=(2, many),
+                grid=(many,),
                 in_specs=in_specs,
-                out_specs=[
-                    pl.BlockSpec(
-                        (blocks, model // blocks, block),
-                        lambda h, j, *_: (0, 0, jnp.where(h == 0, j, many - 1)),
-                    ),
-                    pl.BlockSpec(
-                        (blocks, model // blocks, block),
-                        lambda h, j, *_: (0, 0, jnp.where(h == 0, 0, j)),
-                    ),
-                ],
-                scratch_shapes=[pltpu.VMEM((model, rows), BF16)] * len(pairs),
+                out_specs=pl.BlockSpec(grad_shape[:2] + (block,), lambda j, *_: (0, 0, j)),
+                scratch_shapes=[pltpu.VMEM((deep, model), BF16), pltpu.VMEM((deep, block), BF16)],
             ),
             compiler_params=params(),
+            cost_estimate=cost(2 * rows * model * many * block, 2 * rows * (many * block + model)),
+            name=name,
+        )(core_s if mine else 1 - core_s, places[0 if mine else 1], *operands)
+
+    def attn_backward_call(call, mid, earlier):
+        begin = call * each_call
+        ep = lambda cols: pl.BlockSpec((size, cols), lambda i: (i + begin, 0))
+        return pl.pallas_call(
+            lambda *refs: attn_backward(
+                *refs, nparts=nparts, per_view=per_view, part=part, begin=begin, here=here
+            ),
+            grid=(each_call,),
+            out_shape=[
+                shape((rows, 6 * part), BF16),
+                shape((here, span, model), BF16),
+                shape((8, model)),
+            ],
+            in_specs=[smem, smem, smem, ep(model), ep(6 * part), ep(2 * HEADDIM), ep(model), fixed((8, model))]
+            + [any_spec()] * (nparts + len(earlier)),
+            out_specs=[
+                ep(6 * part),
+                pl.BlockSpec((1, span, model), lambda i: (i + begin, 0, 0)),
+                fixed((8, model)),
+            ],
+            scratch_shapes=[
+                pltpu.VMEM((2, model, chunk_cols[0]), BF16),
+                pltpu.SemaphoreType.DMA((nsem,)),
+            ],
+            input_output_aliases={8 + nparts + index: index for index in range(len(earlier))},
+            compiler_params=params(),
             cost_estimate=cost(
-                4 * rows * model * many * block, 2 * rows * (2 * many * block + model)
+                8 * rows * model * 8 * part // calls, weight_bytes[0] + rows * model * 16 // calls
             ),
-            name=name,
-        )(core_s, places, *operands)
-        return scatter_chunk(mine, other, peers)
-
-    sum_c = grads_of([(glow, act), (final, emb_rows)], 256, "grad_down_emb")
-    sum_b = grads_of([(second, gpre)], 512, "grad_up")
-
-    grad_packed, grad_own, ln_one = pl.pallas_call(
-        lambda *refs: attn_backward(*refs, nparts=nparts, per_view=per_view, part=part),
-        grid=(here,),
-        out_shape=[
-            shape((rows, 6 * part), BF16),
-            shape((here, span, model), BF16),
-            shape((8, model)),
-        ],
-        in_specs=[smem, smem, smem, ep(model), ep(6 * part), ep(2 * HEADDIM), ep(model), fixed((8, model))]
-        + [any_spec()] * nparts,
-        out_specs=[
-            ep(6 * part),
-            pl.BlockSpec((1, span, model), lambda i: (i, 0, 0)),
-            fixed((8, model)),
-        ],
-        scratch_shapes=[
-            pltpu.VMEM((2, model, chunk_cols[0]), BF16),
-            pltpu.SemaphoreType.DMA((nsem,)),
-        ],
-        compiler_params=params(),
-        cost_estimate=cost(4 * 2 * rows * model * 8 * part, weight_bytes[0] + rows * model * 16),
-        name="attn_backward",
-    )(core_s, counts, table, own, packed, lse, gmid, norms, *parts_a)
-    sum_a = grads_of([(first, grad_packed), (gmid_low, attended)], part, "grad_in_out")
+            name="attn_backward",
+        )(core_s, counts, table, own, packed, lse, mid, norms, *parts_a, *earlier)
+
+    hold = after if fast else (lambda array, *others: array)
+    leaves = jax.tree.leaves
+
+    def holds(state, *others):
+        return [state[0], tuple(hold_all(leaves(state[1]), leaves(others)))] if fast else state
+
+    def chunk_start(pairs, block, name, *gate):
+        left, right = pairs[0]
+        pairs = [(left, hold(right, *gate))] + pairs[1:]
+        other = side_grads(pairs, block, name + "_send", False)
+        got = swap(other, peers, 0, 1)
+        left, right = pairs[0]
+        pairs = [(left, hold(right, other))] + pairs[1:]
+        mine = side_grads(pairs, block, name + "_keep", True)
+        return scatter_start((mine, got), peers), mine
+
+    sum_c, last = chunk_start([(glow, act), (final, emb_rows)], 256, "grad_down_emb", outgoing)
+    sum_b, last = chunk_start(
+        [(second, gpre), (gmid_low, attended)], part, "grad_up_out", last, sum_c[1]
+    )
+    sum_c = scatter_near(sum_c, peers, last)
+    ln_one = jnp.zeros((8, model), F32)
+    back = []
+    for call in range(calls):
+        if call == 0:
+            gates = [last, sum_c[1], sum_b[1], arrived]
+        else:
+            gates = [sum_c[1], sum_b[1]]
+        *back, sums = attn_backward_call(call, hold(gmid, *leaves(gates)), back)
+        ln_one = ln_one + sums
+        if call == 0:
+            sum_c = scatter_far(sum_c, peers, back[0])
+            sum_b = scatter_near(sum_b, peers, back[0])
+    grad_packed, grad_own = back
+    sum_c = scatter_end(sum_c, peers, grad_own)
+    sum_b = scatter_far(sum_b, peers, grad_own)
+    sum_a, last = chunk_start(
+        [(first, grad_packed)], part, "grad_in", sum_c, *leaves(sum_b[1])
+    )
+    sum_a = scatter_near(sum_a, peers)
+    sum_b = scatter_end(sum_b, peers, last)
 
     grad_other = swap(grad_own, peers, 0, 1)
     grad_tokens = jnp.where(
@@ -918,32 +1112,33 @@
     positions = lax.dynamic_slice_in_dim(
         grid_positions(math.isqrt(cells), dec * cores), core * dec, dec, 1
     )
-    row_spec = lambda index: pl.BlockSpec(
-        (1, per_view, dec), lambda i, where, live, index=index: (where[i * each + index], 0, 0)
-    )
     decoded = pl.pallas_call(
-        lambda *refs: put_cells(*refs, each=each),
-        out_shape=shape((nviews, cells, dec), BF16),
+        put_cells,
+        out_shape=shape((cells, nviews, dec), BF16),
         grid_spec=pltpu.PrefetchScalarGridSpec(
             num_scalar_prefetch=2,
-            grid=(nviews // each,),
+            grid=(groups,),
             in_specs=[
-                pl.BlockSpec((npos, width), lambda i, *_: (0, 0)),
+                pl.BlockSpec((1, 1, each * stride_put), lambda i, *_: (i, 0, 0)),
                 pl.BlockSpec((1, dec), lambda i, *_: (0, 0)),
                 pl.BlockSpec((cells, dec), lambda i, *_: (0, 0)),
-            ]
-            + [row_spec(index) for index in range(each)],
-            out_specs=pl.BlockSpec((each, cells, dec), lambda i, *_: (i, 0, 0)),
+                pl.BlockSpec((npos, per_view, dec), lambda i, *_: (0, 0, 0)),
+            ],
+            out_specs=pl.BlockSpec((cells, each, dec), lambda i, *_: (0, i, 0)),
+            scratch_shapes=[pltpu.VMEM((each * stride_put, dec), BF16)],
         ),
         compiler_params=params(),
-        cost_estimate=cost(2 * nviews * cells * 56 * dec, cotangent.size * 2),
+        cost_estimate=cost(2 * nviews * stride_put * cells * each * dec, cotangent.size * 2),
         name="put_cells",
-    )(where_slot, live_pos, spots, mask_token, positions, *([arrived] * each))
+    )(where_slot, live_slot, hold(put_marks, last), mask_token, positions, arrived)
+    sum_a = scatter_far(holds(sum_a, decoded, sum_b), peers)
+    decoded = decoded.transpose(1, 0, 2)
+    sum_a = scatter_end(holds(sum_a, grad_tokens), peers)
 
     grads = [
-        sum_a[:, : 3 * part],
-        sum_a[:, 3 * part :],
-        sum_b,
+        sum_a,
+        sum_b[:, hidden:],
+        sum_b[:, :hidden],
         sum_c[:, :hidden],
         sum_c[:, hidden:],
         grad_ln,

time: 523 us -> 472 us (0.902)
  waiting for transfers between devices: 127 us -> 59.4 us
  blocking collectives: 0 us -> 23 us
  starting transfers between devices: 88.6 us -> 71 us
  Pallas kernels: 208 us -> 218 us
    ppermute x51 -> x42, waiting for transfers between devices: 99.2 us -> 49 us  [swap(): return lax.ppermute(array, AXES, pairs)]
    all_to_all x1, waiting for transfers between devices: 27.9 us -> 4.12 us  [per_device(): lax.all_to_all(small_send.reshape(peers * cores, -1), AXES, split_axis=0,...]
    all_to_all x0 -> x2, blocking collectives: none -> 23 us  [the longest x1 11.5 us: per_device(): lax.all_to_all(lamb[29], AXES, split_axis=0, concat_axis=0, tiled=True)]
    ppermute x51 -> x42, starting transfers between devices: 64 us -> 46.1 us  [swap(): return lax.ppermute(array, AXES, pairs)]
    unnamed x48 -> x29, local copies, waits for them, and re-layouts: 15.1 us -> 1.92 us
    pallas_call x7 -> x12, Pallas kernels: 141 us -> 154 us  [the longest x6 59.3 us: side_grads(): pl.pallas_call(lambda *refs: weight_grad(*refs, steps=lengths, rows_each=...]
    all_to_all x2 -> x0, starting transfers between devices: 11.6 us -> none  [the longest x1 5.84 us: per_device(): lax.all_to_all(lamb[29], AXES, split_axis=0, concat_axis=0, tiled=True)]
    all_to_all x1, waiting for transfers between devices: 0.01 us -> 6.31 us  [per_device(): lax.all_to_all(returned, 'dp', split_axis=0, concat_axis=0, tiled=True)]
  transfers between devices with their start and end apart: 57 -> 46, of which waited for: 12 -> 13; matrix products, arithmetic and copies ran while one was open for 16% -> 16% of each run, Pallas kernels for 31% -> 38%
where the time goes in v2:
time: 472 us; the launch traced here: 463 us
  Pallas kernels  218 us (46%)
  starting transfers between devices  71 us (15%)
  waiting for transfers between devices  59.4 us (13%)
  other arithmetic  45.1 us (10%)
  local copies, waits for them, and re-layouts  44.2 us (9%)
  blocking collectives  23 us (5%)
    pallas_call x6, Pallas kernels, side_grads(): pl.pallas_call(lambda *refs: weight_grad(*refs, steps=lengths, rows_each=...  59.3 us
    ppermute x42, waiting for transfers between devices, swap(): return lax.ppermute(array, AXES, pairs)  49 us
    pallas_call x2, Pallas kernels, attn_backward_call(): pl.pallas_call(lambda *refs: attn_backward(*refs, nparts=nparts, per_view...  46.6 us
    ppermute x42, starting transfers between devices, swap(): return lax.ppermute(array, AXES, pairs)  46.1 us
    pallas_call x1, Pallas kernels, per_device(): pl.pallas_call(lambda *refs: mlp_backward(*refs, nparts=nparts, per_view=...  30 us
    pallas_call x2, Pallas kernels, attn_forward_call(): pl.pallas_call(lambda *refs: attn_forward(*refs, nparts=nparts, per_view=...  29.3 us
    pallas_call x1, Pallas kernels, per_device(): pl.pallas_call(lambda *refs: mlp_forward(*refs, nparts=nparts, per_view=p...  22.8 us
    all_to_all x1, blocking collectives, per_device(): lax.all_to_all(lamb[29], AXES, split_axis=0, concat_axis=0, tiled=True)  11.5 us
  transfers between devices with their start and end apart: 46, of which 13 were waited for; matrix products, arithmetic and copies ran while one was open for 16% of the time, Pallas kernels for 38%

profile of v2, /device:TPU:0, one launch (start us, length us, event | category | flops | bytes accessed | tf_op | source)
XLA Modules:
  0.0 463.4 jit_solution(1282821338691683426)
XLA Ops:
  2.6 5.1 %collective-permute-start.2 = (bf16[48,1536]{1,0:T(8,128)(2,1)S(1)}, bf16[48,1536]{1,0:T(8,128)(2,1)S(1)}, u32[]{:S(2)}, u32[]{:S(2)}) collective-permute-start(bf16[48,1536]{1,0:T(8,128)(2,1)S(1)} %get-tuple-element.554), channel_id=1, source_target_pairs={{0,24},{1,25},{2,26},{3,27},{4,28},{5,29},{6,30},{7,31},{8,16},{9,... | collective-permute-start | bytes 442376 | tf_op jit(solution)/shard_map/ppermute | solution.py:79
  16.4 6.0 %all-to-all-start = ((bf16[32,2,190]{2,1,0:T(2,128)(2,1)}), bf16[32,2,190]{2,1,0:T(2,128)(2,1)S(1)}, u32[]{:S(2)}, u32[]{:S(2)}) async-start(bf16[32,2,190]{2,1,0:T(2,128)(2,1)} %reshape.395), calls=%async_computation | async-start | bytes 65536 | tf_op jit(solution)/shard_map/all_to_all | solution.py:751
  23.3 2.8 constant_dynamic-slice_fusion.1
  26.1 2.5 reshape.356
  34.9 3.3 collective-permute-start.6
  40.8 9.5 %take_cells.1 = (bf16[48,49,256]{2,1,0:T(8,128)(2,1)}, f32[8,256]{1,0:T(8,128)}) custom-call(s32[48]{0:T(128)} %select_reduce_fusion.refs_0_.where_s, s32[2688,1]{1,0:T(8,128)} %copy.170.refs_1_, f32[6,1,1568]{2,1,0:T(1,128)} %reshape.369.refs_2_, bf16[196,48,256]{2,1,0:T(8,128)(2,1)} %bitcast.165), custom_call_target="tpu_custom_call" | custom-call | flops 2157969408 | bytes 4816896 | tf_op jit(solution)/shard_map/take_cells/pallas_call | solution.py:827
  53.2 2.8 collective-permute-start.11
  57.6 4.7 %collective-permute-done.11 = bf16[48,1792]{1,0:T(8,128)(2,1)S(1)} collective-permute-done((bf16[48,1792]{1,0:T(8,128)(2,1)S(1)}, bf16[48,1792]{1,0:T(8,128)(2,1)S(1)}, u32[]{:S(2)}, u32[]{:S(2)}) %collective-permute-start.11) | collective-permute-done | bytes 172064 | tf_op jit(solution)/shard_map/ppermute | solution.py:79
  62.3 7.2 %collective-permute-done.10 = bf16[48,1792]{1,0:T(8,128)(2,1)S(1)} collective-permute-done((bf16[48,1792]{1,0:T(8,128)(2,1)S(1)}, bf16[48,1792]{1,0:T(8,128)(2,1)S(1)}, u32[]{:S(2)}, u32[]{:S(2)}) %collective-permute-start.10) | collective-permute-done | bytes 172064 | tf_op jit(solution)/shard_map/ppermute | solution.py:79
  70.8 3.0 collective-permute-done.7.refs_6_.refs_9_
  77.7 14.7 %attn_forward.2 = (bf16[1248,768]{1,0:T(8,128)(2,1)}, bf16[1248,2304]{1,0:T(8,128)(2,1)}, bf16[1248,768]{1,0:T(8,128)(2,1)}, f32[1248,768]{1,0:T(8,128)}, bf16[1...) custom-call(s32[1]{0:T(128)} %bitcast.4.refs_0_.mp_s, s32[12]{0:T(128)} %refs_1_.7, s32[36]{0:T(128)} %concatenate.64.refs_2_.refs_1_, ...), custom_call_target="tpu_custom_call" | custom-call | flops 8833204224 | bytes 12386304 | tf_op jit(solution)/shard_map/attn_forward/pallas_call | solution.py:851
  94.6 3.3 collective-permute-done.12.refs_6_.refs_9_
  100.0 5.5 %all-to-all-start.1 = ((bf16[48,49,256]{2,1,0:T(8,128)(2,1)}), bf16[48,49,256]{2,1,0:T(8,128)(2,1)S(1)}, u32[]{:S(2)}, u32[]{:S(2)}) async-start(bf16[48,49,256]{2,1,0:T(8,128)(2,1)} %get-tuple-element.174), calls=%async_computation.1 | async-start | bytes 2752512 | tf_op jit(solution)/shard_map/all_to_all | solution.py:890
  105.9 14.7 %attn_forward.3 = (bf16[1248,768]{1,0:T(8,128)(2,1)}, bf16[1248,2304]{1,0:T(8,128)(2,1)}, bf16[1248,768]{1,0:T(8,128)(2,1)}, f32[1248,768]{1,0:T(8,128)}, bf16[1...) custom-call(s32[1]{0:T(128)} %bitcast.4.refs_0_.mp_s, ...), custom_call_target="tpu_custom_call", output_to_operand_aliasing={{0}: (9, {}), {1}: (10, {}), {2}: (11, {}), {3}: (12, {}), ... | custom-call | flops 8833204224 | bytes 12386304 | tf_op jit(solution)/shard_map/attn_forward/pallas_call | solution.py:851
  120.5 7.9 %collective-permute-done.19.refs_10_.refs_13_ = bf16[8,48,1792]{2,1,0:T(8,128)(2,1)} collective-permute-done((bf16[8,48,1792]{2,1,0:T(8,128)(2,1)}, bf16[8,48,1792]{2,1,0:T(8,128)(2,1)}, u32[]{:S(2)}, u32[]{:S(2)}) %collective-permute-start.19) | collective-permute-done | bytes 1376288 | tf_op jit(solution)/shard_map/ppermute | solution.py:79
  129.7 6.3 %all-to-all-done.1.refs_3_ = bf16[48,49,256]{2,1,0:T(8,128)(2,1)S(1)} async-done(((bf16[48,49,256]{2,1,0:T(8,128)(2,1)}), bf16[48,49,256]{2,1,0:T(8,128)(2,1)S(1)}, u32[]{:S(2)}, u32[]{:S(2)}) %all-to-all-start.1) | async-done | bytes 1204256 | tf_op jit(solution)/shard_map/all_to_all | solution.py:890
  138.8 22.8 %mlp_forward.1 = (bf16[1248,3072]{1,0:T(8,128)(2,1)}, bf16[1248,3072]{1,0:T(8,128)(2,1)}, bf16[1248,768]{1,0:T(8,128)(2,1)}, bf16[24,49,256]{2,1,0:T(8,128)(2,1)}, bf16[24,49,256]{2,1,0:T(8,128)(2,1)}) custom-call(s32[1]{0:T(128)} %bitcast.4.refs_0_.mp_s, s32[36]{0:T(128)} %concatenate.64.refs_2_.refs_1_, bf16[1248,768]{1,0:T(8,128)(2,1)} %get-tuple-element.175.refs_2_, ...), custom_call_target="tpu_custom_call" | custom-call | flops 11777605632 | bytes 25559040 | tf_op jit(solution)/shard_map/mlp_forward/pallas_call | solution.py:904
  165.0 30.0 %mlp_backward.1 = (bf16[1248,512]{1,0:T(8,128)(2,1)}, bf16[1248,768]{1,0:T(8,128)(2,1)}, bf16[1248,3072]{1,0:T(8,128)(2,1)}, f32[1248,768]{1,0:T(8,128)}, bf16[1248,768]{1,0:T(8,128)(2,1)}, /*index=5*/f32[8,768]{1,0:T(8,128)}) custom-call(s32[1]{0:T(128)} %bitcast.4.refs_0_.mp_s, s32[24]{0:T(128)} %dynamic_slice.20.refs_1_, s32[36]{0:T(128)} %concatenate.64.refs_2_.refs_1_, ...), custom_call_target="tpu_custom_call" | custom-call | flops 11777605632 | bytes 25559040 | tf_op jit(solution)/shard_map/mlp_backward/pallas_call | solution.py:933
  197.3 10.8 %grad_down_emb_send.1 = bf16[16,48,1792]{2,1,0:T(8,128)(2,1)} custom-call(s32[1]{0:T(128)S(6)} %sub.31.refs_0_.once_s, s32[16]{0:T(128)} %fusion.43.refs_1_, bf16[1248,768]{1,0:T(8,128)(2,1)} %get-tuple-element.183.refs_2_, bf16[1248,3072]{1,0:T(8,128)(2,1)} %get-tuple-element.191.refs_3_, bf16[1248,768]{1,0:T(8,128)(2,1)} %get-tuple-element.189.refs_4_, ...), custom_call_target="tpu_custom_call" | custom-call | flops 3435134976 | bytes 6389760 | tf_op jit(solution)/shard_map/grad_down_emb_send/pallas_call | solution.py:1003
  208.7 10.8 %grad_down_emb_keep.1 = bf16[16,48,1792]{2,1,0:T(8,128)(2,1)} custom-call(s32[1]{0:T(128)} %bitcast.4.refs_0_.mp_s, s32[16]{0:T(128)} %fusion.41.refs_1_, bf16[1248,768]{1,0:T(8,128)(2,1)} %get-tuple-element.183.refs_2_, bf16[1248,3072]{1,0:T(8,128)(2,1)} %get-tuple-element.191.refs_3_, bf16[1248,768]{1,0:T(8,128)(2,1)} %get-tuple-element.189.refs_4_, ...), custom_call_target="tpu_custom_call" | custom-call | flops 3435134976 | bytes 6389760 | tf_op jit(solution)/shard_map/grad_down_emb_keep/pallas_call | solution.py:1003
  219.5 3.9 add_convert_fusion.1
  223.4 11.3 %grad_up_out_send.1 = bf16[16,48,1920]{2,1,0:T(8,128)(2,1)} custom-call(s32[1]{0:T(128)S(6)} %sub.31.refs_0_.once_s, s32[16]{0:T(128)} %fusion.43.refs_1_, bf16[1248,768]{1,0:T(8,128)(2,1)} %get-tuple-element.175.refs_2_, bf16[1248,3072]{1,0:T(8,128)(2,1)} %get-tuple-element.196.refs_3_, bf16[1248,768]{1,0:T(8,128)(2,1)} %get-tuple-element.194.refs_4_, ...), custom_call_target="tpu_custom_call" | custom-call | flops 3680501760 | bytes 6709248 | tf_op jit(solution)/shard_map/grad_up_out_send/pallas_call | solution.py:1003
  235.2 2.4 collective-permute-start.24
  237.5 6.6 %all-to-all-start.2 = ((bf16[48,49,256]{2,1,0:T(8,128)(2,1)}), bf16[48,49,256]{2,1,0:T(8,128)(2,1)}, u32[]{:S(2)}, u32[]{:S(2)}) async-start(bf16[48,49,256]{2,1,0:T(8,128)(2,1)} %order_views.1), calls=%async_computation.2 | async-start | bytes 2752512 | tf_op jit(solution)/shard_map/all_to_all | solution.py:977
  244.1 11.3 %grad_up_out_keep.1 = bf16[16,48,1920]{2,1,0:T(8,128)(2,1)} custom-call(s32[1]{0:T(128)} %bitcast.4.refs_0_.mp_s, s32[16]{0:T(128)} %fusion.41.refs_1_, bf16[1248,768]{1,0:T(8,128)(2,1)} %get-tuple-element.175.refs_2_, bf16[1248,3072]{1,0:T(8,128)(2,1)} %get-tuple-element.196.refs_3_, bf16[1248,768]{1,0:T(8,128)(2,1)} %get-tuple-element.194.refs_4_, ...), custom_call_target="tpu_custom_call" | custom-call | flops 3680501760 | bytes 6709248 | tf_op jit(solution)/shard_map/grad_up_out_keep/pallas_call | solution.py:1003
  255.4 11.3 %collective-permute-done.24 = bf16[8,48,1792]{2,1,0:T(8,128)(2,1)} collective-permute-done((bf16[8,48,1792]{2,1,0:T(8,128)(2,1)}, bf16[8,48,1792]{2,1,0:T(8,128)(2,1)}, u32[]{:S(2)}, u32[]{:S(2)}) %collective-permute-start.24) | collective-permute-done | bytes 1376288 | tf_op jit(solution)/shard_map/ppermute | solution.py:79
  266.7 2.6 add_convert_fusion.4
  270.0 3.9 add_convert_fusion
  273.9 2.5 collective-permute-start.27
  276.4 23.3 %attn_backward.2 = (bf16[1248,2304]{1,0:T(8,128)(2,1)}, bf16[6,196,768]{2,1,0:T(8,128)(2,1)}, f32[8,768]{1,0:T(8,128)}) custom-call(s32[1]{0:T(128)} %bitcast.4.refs_0_.mp_s, s32[12]{0:T(128)} %refs_1_.7, s32[36]{0:T(128)} %concatenate.64.refs_2_.refs_1_, bf16[1248,768]{1,0:T(8,128)(2,1)} %bitcast.132, bf16[1248,2304]{1,0:T(8,128)(2,1)} %get-tuple-element.172.refs_4_, ...), custom_call_target="tpu_custom_call" | custom-call | flops 11777605632 | bytes 12386304 | tf_op jit(solution)/shard_map/attn_backward/pallas_call | solution.py:1021
  301.6 2.7 collective-permute-start.28
  309.7 23.3 %attn_backward.3 = (bf16[1248,2304]{1,0:T(8,128)(2,1)}, bf16[6,196,768]{2,1,0:T(8,128)(2,1)}, f32[8,768]{1,0:T(8,128)}) custom-call(s32[1]{0:T(128)} %bitcast.4.refs_0_.mp_s, s32[12]{0:T(128)} %refs_1_.7, s32[36]{0:T(128)} %concatenate.64.refs_2_.refs_1_, bf16[1248,768]{1,0:T(8,128)(2,1)} %bitcast.133, ...), custom_call_target="tpu_custom_call", output_to_operand_aliasing={{0}: (12, {}), {1}: (13, {})} | custom-call | flops 11777605632 | bytes 12386304 | tf_op jit(solution)/shard_map/attn_backward/pallas_call | solution.py:1021
  337.0 7.6 %grad_in_send.1 = bf16[16,48,1152]{2,1,0:T(8,128)(2,1)} custom-call(s32[1]{0:T(128)S(6)} %sub.31.refs_0_.once_s, s32[16]{0:T(128)} %fusion.43.refs_1_, bf16[1248,768]{1,0:T(8,128)(2,1)} %get-tuple-element.171.refs_2_, bf16[1248,2304]{1,0:T(8,128)(2,1)} %get-tuple-element.211.refs_3_), custom_call_target="tpu_custom_call" | custom-call | flops 2208301056 | bytes 4792320 | tf_op jit(solution)/shard_map/grad_in_send/pallas_call | solution.py:1003
  351.5 7.6 %grad_in_keep.1 = bf16[16,48,1152]{2,1,0:T(8,128)(2,1)} custom-call(s32[1]{0:T(128)} %bitcast.4.refs_0_.mp_s, s32[16]{0:T(128)} %fusion.41.refs_1_, bf16[1248,768]{1,0:T(8,128)(2,1)} %get-tuple-element.171.refs_2_, bf16[1248,2304]{1,0:T(8,128)(2,1)} %get-tuple-element.211.refs_3_), custom_call_target="tpu_custom_call" | custom-call | flops 2208301056 | bytes 4792320 | tf_op jit(solution)/shard_map/grad_in_keep/pallas_call | solution.py:1003
  359.2 2.6 add_convert_fusion.2
  367.6 3.0 collective-permute-start.36
  371.2 8.8 %put_cells.1 = bf16[196,48,256]{2,1,0:T(8,128)(2,1)} custom-call(s32[48]{0:T(128)} %select_reduce_fusion.refs_0_.where_s, s32[48]{0:T(128)} %slice_bitcast_fusion.3.live_s, s32[6,1,512]{2,1,0:T(1,128)} %reshape.354.marks, f32[1,256]{1,0:T(1,128)} %fusion.38.mask, f32[196,256]{1,0:T(8,128)} %fusion.8.positions, bf16[48,49,256]{2,1,0:T(8,128)(2,1)} %all-to-all-done.2.rows), custom_call_target="tpu_custom_call" | custom-call | flops 2466250752 | bytes 4816896 | tf_op jit(solution)/shard_map/put_cells/pallas_call | solution.py:1115
  379.9 4.1 collective-permute-done.36
  388.6 6.8 %all-to-all-start.3 = ((f32[32,1,224]{2,1,0:T(1,128)}), f32[32,1,224]{2,1,0:T(1,128)S(1)}, u32[]{:S(2)}, u32[]{:S(2)}) async-start(f32[32,1,224]{2,1,0:T(1,128)} %all_to_all.28), calls=%async_computation.3 | async-start | bytes 65536 | tf_op jit(solution)/shard_map/all_to_all | solution.py:1104
  398.5 4.1 all-to-all-done.3
  402.9 3.8 maximum_select_fusion
  406.7 5.7 %select_n.122 = bf16[2352,768]{1,0:T(8,128)(2,1)} reshape(bf16[12,196,768]{2,1,0:T(8,128)(2,1)} %maximum_select_fusion) | data formatting | bytes 7225344 | tf_op jit(solution)/shard_map/jit(_where)/select_n | solution.py:1093
  421.7 4.1 collective-permute-done.40
  427.6 2.4 squares.1
  430.0 11.5 %all_to_all.39.tiles = f32[32,8,128]{2,1,0:T(8,128)} all-to-all(f32[32,8,128]{2,1,0:T(8,128)} %squares.1), channel_id=1, replica_groups=mesh['dp'=16,'mp'=2] {'dp','mp'}, dimensions={0} | all-to-all | bytes 262144 | tf_op jit(solution)/shard_map/all_to_all | solution.py:1149
  441.5 4.7 %lamb.1 = (f32[3,48,384]{2,1,0:T(8,128)}, f32[48,384]{1,0:T(8,128)}, f32[48,1536]{1,0:T(8,128)}, f32[48,1536]{1,0:T(8,128)}, f32[48,256]{1,0:T(8,128)}, /*index=...) custom-call(s32[1]{0:T(128)S(6)} %sub.31.refs_0_.once_s, ...), custom_call_target="tpu_custom_call" | custom-call | tf_op jit(solution)/shard_map/lamb/pallas_call | solution.py:673
  446.2 11.5 %all_to_all.40.tiles = f32[32,8,128]{2,1,0:T(8,128)} all-to-all(f32[32,8,128]{2,1,0:T(8,128)} %get-tuple-element.224), channel_id=1, replica_groups=mesh['dp'=16,'mp'=2] {'dp','mp'}, dimensions={0} | all-to-all | bytes 262144 | tf_op jit(solution)/shard_map/all_to_all | solution.py:1159
  457.7 2.8 update.1
  (222 shorter events, 91.7 us)
Async XLA Ops:
  2.6 28.5 %collective-permute-start.2 = (bf16[48,1536]{1,0:T(8,128)(2,1)S(1)}, bf16[48,1536]{1,0:T(8,128)(2,1)S(1)}, u32[]{:S(2)}, u32[]{:S(2)}) collective-permute-start(bf16[48,1536]{1,0:T(8,128)(2,1)S(1)} %get-tuple-element.554), channel_id=1, source_target_pairs={{0,24},{1,25},{2,26},{3,27},{4,28},{5,29},{6,30},{7,31},{8,16},{9,... | collective-permute-start | bytes 442376 | tf_op jit(solution)/shard_map/ppermute | solution.py:79
  7.7 23.4 %collective-permute-start.1 = (bf16[48,1536]{1,0:T(8,128)(2,1)S(1)}, bf16[48,1536]{1,0:T(8,128)(2,1)S(1)}, u32[]{:S(2)}, u32[]{:S(2)}) collective-permute-start(bf16[48,1536]{1,0:T(8,128)(2,1)S(1)} %get-tuple-element.554), channel_id=1, source_target_pairs={{0,16},{1,17},{2,18},{3,19},{4,20},{5,21},{6,22},{7,23},{8,24},{9,... | collective-permute-start | bytes 442376 | tf_op jit(solution)/shard_map/ppermute | solution.py:79
  7.8 23.4 %collective-permute-start = (bf16[48,1536]{1,0:T(8,128)(2,1)S(1)}, bf16[48,1536]{1,0:T(8,128)(2,1)S(1)}, u32[]{:S(2)}, u32[]{:S(2)}) collective-permute-start(bf16[48,1536]{1,0:T(8,128)(2,1)S(1)} %get-tuple-element.554), channel_id=1, source_target_pairs={{0,8},{1,9},{2,10},{3,11},{4,12},{5,13},{6,14},{7,15},{8,0},{9,1},... | collective-permute-start | bytes 442376 | tf_op jit(solution)/shard_map/ppermute | solution.py:79
  16.4 13.6 %all-to-all-start = ((bf16[32,2,190]{2,1,0:T(2,128)(2,1)}), bf16[32,2,190]{2,1,0:T(2,128)(2,1)S(1)}, u32[]{:S(2)}, u32[]{:S(2)}) async-start(bf16[32,2,190]{2,1,0:T(2,128)(2,1)} %reshape.395), calls=%async_computation | async-start | bytes 65536 | tf_op jit(solution)/shard_map/all_to_all | solution.py:751
  31.3 19.7 %collective-permute-start.3 = (bf16[4,48,1536]{2,1,0:T(8,128)(2,1)S(1)}, bf16[4,48,1536]{2,1,0:T(8,128)(2,1)S(1)}, u32[]{:S(2)}, u32[]{:S(2)}) collective-permute-start(bf16[4,48,1536]{2,1,0:T(8,128)(2,1)S(1)} %pad_maximum_fusion.3), channel_id=1, source_target_pairs={{0,2},{1,5},{2,0},{3,7},{4,6},{5,1},{6,4},{7,3},{8,10},{9,13},{10,... | collective-permute-start | bytes 1769480 | tf_op jit(solution)/shard_map/ppermute | solution.py:79
  34.9 15.5 %collective-permute-start.6 = (bf16[48,1536]{1,0:T(8,128)(2,1)S(1)}, bf16[48,1536]{1,0:T(8,128)(2,1)S(1)}, u32[]{:S(2)}, u32[]{:S(2)}) collective-permute-start(bf16[48,1536]{1,0:T(8,128)(2,1)S(1)} %convert_element_type.409), channel_id=1, source_target_pairs={{0,24},{1,25},{2,26},{3,27},{4,28},{5,29},{6,30},{7,31},{8,16},{9,... | collective-permute-start | bytes 442376 | tf_op jit(solution)/shard_map/ppermute | solution.py:79
  38.2 12.7 %collective-permute-start.5 = (bf16[48,1536]{1,0:T(8,128)(2,1)S(1)}, bf16[48,1536]{1,0:T(8,128)(2,1)S(1)}, u32[]{:S(2)}, u32[]{:S(2)}) collective-permute-start(bf16[48,1536]{1,0:T(8,128)(2,1)S(1)} %convert_element_type.409), channel_id=1, source_target_pairs={{0,16},{1,17},{2,18},{3,19},{4,20},{5,21},{6,22},{7,23},{8,24},{9,... | collective-permute-start | bytes 442376 | tf_op jit(solution)/shard_map/ppermute | solution.py:79
  38.2 12.7 %collective-permute-start.4 = (bf16[48,1536]{1,0:T(8,128)(2,1)S(1)}, bf16[48,1536]{1,0:T(8,128)(2,1)S(1)}, u32[]{:S(2)}, u32[]{:S(2)}) collective-permute-start(bf16[48,1536]{1,0:T(8,128)(2,1)S(1)} %convert_element_type.409), channel_id=1, source_target_pairs={{0,8},{1,9},{2,10},{3,11},{4,12},{5,13},{6,14},{7,15},{8,0},{9,1},... | collective-permute-start | bytes 442376 | tf_op jit(solution)/shard_map/ppermute | solution.py:79
  51.1 22.7 %collective-permute-start.7 = (bf16[8,48,1536]{2,1,0:T(8,128)(2,1)S(1)}, bf16[8,48,1536]{2,1,0:T(8,128)(2,1)}, u32[]{:S(2)}, u32[]{:S(2)}) collective-permute-start(bf16[8,48,1536]{2,1,0:T(8,128)(2,1)S(1)} %pad_maximum_fusion.refs_5_.refs_8_), channel_id=1, source_target_pairs={{0,4},{1,3},{2,6},{3,1},{4,0},{5,7},{6,2},{7,5},{8,12},{9,11},{10,... | collective-permute-start | bytes 3538952 | tf_op jit(solution)/shard_map/ppermute | solution.py:79
  52.1 17.5 %collective-permute-start.8 = (bf16[4,48,1536]{2,1,0:T(8,128)(2,1)S(1)}, bf16[4,48,1536]{2,1,0:T(8,128)(2,1)S(1)}, u32[]{:S(2)}, u32[]{:S(2)}) collective-permute-start(bf16[4,48,1536]{2,1,0:T(8,128)(2,1)S(1)} %pad_maximum_fusion.4), channel_id=1, source_target_pairs={{0,2},{1,5},{2,0},{3,7},{4,6},{5,1},{6,4},{7,3},{8,10},{9,13},{10,... | collective-permute-start | bytes 1769480 | tf_op jit(solution)/shard_map/ppermute | solution.py:79
  53.2 9.1 %collective-permute-start.11 = (bf16[48,1792]{1,0:T(8,128)(2,1)S(1)}, bf16[48,1792]{1,0:T(8,128)(2,1)S(1)}, u32[]{:S(2)}, u32[]{:S(2)}) collective-permute-start(bf16[48,1792]{1,0:T(8,128)(2,1)S(1)} %pad_maximum_fusion.5), channel_id=1, source_target_pairs={{0,24},{1,25},{2,26},{3,27},{4,28},{5,29},{6,30},{7,31},{8,16},{9,... | collective-permute-start | bytes 516104 | tf_op jit(solution)/shard_map/ppermute | solution.py:79
  56.0 13.5 %collective-permute-start.10 = (bf16[48,1792]{1,0:T(8,128)(2,1)S(1)}, bf16[48,1792]{1,0:T(8,128)(2,1)S(1)}, u32[]{:S(2)}, u32[]{:S(2)}) collective-permute-start(bf16[48,1792]{1,0:T(8,128)(2,1)S(1)} %pad_maximum_fusion.5), channel_id=1, source_target_pairs={{0,16},{1,17},{2,18},{3,19},{4,20},{5,21},{6,22},{7,23},{8,24},{9,... | collective-permute-start | bytes 516104 | tf_op jit(solution)/shard_map/ppermute | solution.py:79
  56.0 13.5 %collective-permute-start.9 = (bf16[48,1792]{1,0:T(8,128)(2,1)S(1)}, bf16[48,1792]{1,0:T(8,128)(2,1)S(1)}, u32[]{:S(2)}, u32[]{:S(2)}) collective-permute-start(bf16[48,1792]{1,0:T(8,128)(2,1)S(1)} %pad_maximum_fusion.5), channel_id=1, source_target_pairs={{0,8},{1,9},{2,10},{3,11},{4,12},{5,13},{6,14},{7,15},{8,0},{9,1},... | collective-permute-start | bytes 516104 | tf_op jit(solution)/shard_map/ppermute | solution.py:79
  62.3 15.5 %collective-permute-start.15 = (bf16[8,48,1536]{2,1,0:T(8,128)(2,1)S(1)}, bf16[8,48,1536]{2,1,0:T(8,128)(2,1)}, u32[]{:S(2)}, u32[]{:S(2)}) collective-permute-start(bf16[8,48,1536]{2,1,0:T(8,128)(2,1)S(1)} %pad_maximum_fusion.refs_5_.refs_8_), channel_id=1, source_target_pairs={{0,1},{1,0},{2,3},{3,2},{4,5},{5,4},{6,7},{7,6},{8,9},{9,8},{10,11... | collective-permute-start | bytes 3538952 | tf_op jit(solution)/shard_map/ppermute | solution.py:79
  73.8 4.0 collective-permute-start.16
  73.9 23.9 %collective-permute-start.12 = (bf16[8,48,1536]{2,1,0:T(8,128)(2,1)}, bf16[8,48,1536]{2,1,0:T(8,128)(2,1)}, u32[]{:S(2)}, u32[]{:S(2)}) collective-permute-start(bf16[8,48,1536]{2,1,0:T(8,128)(2,1)} %pad_maximum_fusion.1.refs_5_.refs_8_), channel_id=1, source_target_pairs={{0,4},{1,3},{2,6},{3,1},{4,0},{5,7},{6,2},{7,5},{8,12},{9,11},{10,... | collective-permute-start | bytes 3538952 | tf_op jit(solution)/shard_map/ppermute | solution.py:79
  75.9 30.0 %collective-permute-start.14 = (bf16[8,48,1536]{2,1,0:T(8,128)(2,1)}, bf16[8,48,1536]{2,1,0:T(8,128)(2,1)}, u32[]{:S(2)}, u32[]{:S(2)}) collective-permute-start(bf16[8,48,1536]{2,1,0:T(8,128)(2,1)} %pad_maximum_fusion.1.refs_5_.refs_8_), channel_id=1, source_target_pairs={{0,1},{1,0},{2,3},{3,2},{4,5},{5,4},{6,7},{7,6},{8,9},{9,8},{10,11... | collective-permute-start | bytes 3538952 | tf_op jit(solution)/shard_map/ppermute | solution.py:79
  76.2 18.4 %collective-permute-start.13 = (bf16[4,48,1792]{2,1,0:T(8,128)(2,1)S(1)}, bf16[4,48,1792]{2,1,0:T(8,128)(2,1)S(1)}, u32[]{:S(2)}, u32[]{:S(2)}) collective-permute-start(bf16[4,48,1792]{2,1,0:T(8,128)(2,1)S(1)} %pad_maximum_fusion.2), channel_id=1, source_target_pairs={{0,2},{1,5},{2,0},{3,7},{4,6},{5,1},{6,4},{7,3},{8,10},{9,13},{10,... | collective-permute-start | bytes 2064392 | tf_op jit(solution)/shard_map/ppermute | solution.py:79
  99.6 28.8 %collective-permute-start.19 = (bf16[8,48,1792]{2,1,0:T(8,128)(2,1)}, bf16[8,48,1792]{2,1,0:T(8,128)(2,1)}, u32[]{:S(2)}, u32[]{:S(2)}) collective-permute-start(bf16[8,48,1792]{2,1,0:T(8,128)(2,1)} %constant_dynamic-update-slice_fusion.refs_9_.refs_12_), channel_id=1, source_target_pairs={{0,4},{1,3},{2,6},{3,1},{4,0},{5,7},{6,2},{7,5},{8,12},{9,11},{10,... | collective-permute-start | bytes 4128776 | tf_op jit(solution)/shard_map/ppermute | solution.py:79
  100.0 20.5 %collective-permute-start.18 = (bf16[8,48,1536]{2,1,0:T(8,128)(2,1)}, bf16[8,48,1536]{2,1,0:T(8,128)(2,1)S(1)}, u32[]{:S(2)}, u32[]{:S(2)}) collective-permute-start(bf16[8,48,1536]{2,1,0:T(8,128)(2,1)} %collective-permute-done.12.refs_6_.refs_9_), channel_id=1, source_target_pairs={{0,1},{1,0},{2,3},{3,2},{4,5},{5,4},{6,7},{7,6},{8,9},{9,8},{10,11... | collective-permute-start | bytes 3538952 | tf_op jit(solution)/shard_map/ppermute | solution.py:79
  100.0 35.9 %all-to-all-start.1 = ((bf16[48,49,256]{2,1,0:T(8,128)(2,1)}), bf16[48,49,256]{2,1,0:T(8,128)(2,1)S(1)}, u32[]{:S(2)}, u32[]{:S(2)}) async-start(bf16[48,49,256]{2,1,0:T(8,128)(2,1)} %get-tuple-element.174), calls=%async_computation.1 | async-start | bytes 2752512 | tf_op jit(solution)/shard_map/all_to_all | solution.py:890
  105.6 33.2 %collective-permute-start.20 = (bf16[8,48,1792]{2,1,0:T(8,128)(2,1)}, bf16[8,48,1792]{2,1,0:T(8,128)(2,1)}, u32[]{:S(2)}, u32[]{:S(2)}) collective-permute-start(bf16[8,48,1792]{2,1,0:T(8,128)(2,1)} %constant_dynamic-update-slice_fusion.refs_9_.refs_12_), channel_id=1, source_target_pairs={{0,1},{1,0},{2,3},{3,2},{4,5},{5,4},{6,7},{7,6},{8,9},{9,8},{10,11... | collective-permute-start | bytes 4128776 | tf_op jit(solution)/shard_map/ppermute | solution.py:79
  128.4 10.4 %collective-permute-start.21 = (bf16[8,48,1792]{2,1,0:T(8,128)(2,1)}, bf16[8,48,1792]{2,1,0:T(8,128)(2,1)}, u32[]{:S(2)}, u32[]{:S(2)}) collective-permute-start(bf16[8,48,1792]{2,1,0:T(8,128)(2,1)} %collective-permute-done.19.refs_10_.refs_13_), channel_id=1, source_target_pairs={{0,1},{1,0},{2,3},{3,2},{4,5},{5,4},{6,7},{7,6},{8,9},{9,8},{10,11... | collective-permute-start | bytes 4128776 | tf_op jit(solution)/shard_map/ppermute | solution.py:79
  137.5 26.0 %collective-permute-start.17 = (bf16[48,49,256]{2,0,1:T(8,128)(2,1)}, bf16[48,49,256]{2,0,1:T(8,128)(2,1)S(1)}, u32[]{:S(2)}, u32[]{:S(2)}) collective-permute-start(bf16[48,49,256]{2,0,1:T(8,128)(2,1)} %copy.173), channel_id=1, source_target_pairs={{0,1},{1,0},{2,3},{3,2},{4,5},{5,4},{6,7},{7,6},{8,9},{9,8},{10,11... | collective-permute-start | bytes 3612680 | tf_op jit(solution)/shard_map/ppermute | solution.py:79
  162.9 32.2 %collective-permute-start.22 = (bf16[24,49,256]{2,0,1:T(8,128)(2,1)S(1)}, bf16[24,49,256]{2,0,1:T(8,128)(2,1)S(1)}, u32[]{:S(2)}, u32[]{:S(2)}) collective-permute-start(bf16[24,49,256]{2,0,1:T(8,128)(2,1)S(1)} %copy.176), channel_id=1, source_target_pairs={{0,1},{1,0},{2,3},{3,2},{4,5},{5,4},{6,7},{7,6},{8,9},{9,8},{10,11... | collective-permute-start | bytes 1806344 | tf_op jit(solution)/shard_map/ppermute | solution.py:79
  165.0 30.2 %copy-start = (bf16[24,49,256]{2,1,0:T(8,128)(2,1)S(1)}, bf16[24,49,256]{2,1,0:T(8,128)(2,1)}, u32[]{:S(2)}) copy-start(bf16[24,49,256]{2,1,0:T(8,128)(2,1)} %get-tuple-element.185.own) | copy-start | bytes 1806340
  208.1 11.4 %collective-permute-start.23 = (bf16[16,48,1792]{2,1,0:T(8,128)(2,1)}, bf16[16,48,1792]{2,1,0:T(8,128)(2,1)S(1)}, u32[]{:S(2)}, u32[]{:S(2)}) collective-permute-start(bf16[16,48,1792]{2,1,0:T(8,128)(2,1)} %grad_down_emb_send.1), channel_id=1, source_target_pairs={{0,1},{1,0},{2,3},{3,2},{4,5},{5,4},{6,7},{7,6},{8,9},{9,8},{10,11... | collective-permute-start | bytes 8257544 | tf_op jit(solution)/shard_map/ppermute | solution.py:79
  234.7 35.3 %collective-permute-start.26 = (bf16[16,48,1920]{2,1,0:T(8,128)(2,1)}, bf16[16,48,1920]{2,1,0:T(8,128)(2,1)S(1)}, u32[]{:S(2)}, u32[]{:S(2)}) collective-permute-start(bf16[16,48,1920]{2,1,0:T(8,128)(2,1)} %grad_up_out_send.1), channel_id=1, source_target_pairs={{0,1},{1,0},{2,3},{3,2},{4,5},{5,4},{6,7},{7,6},{8,9},{9,8},{10,11... | collective-permute-start | bytes 8847368 | tf_op jit(solution)/shard_map/ppermute | solution.py:79
  235.2 31.6 %collective-permute-start.24 = (bf16[8,48,1792]{2,1,0:T(8,128)(2,1)}, bf16[8,48,1792]{2,1,0:T(8,128)(2,1)}, u32[]{:S(2)}, u32[]{:S(2)}) collective-permute-start(bf16[8,48,1792]{2,1,0:T(8,128)(2,1)} %add_convert_fusion.1), channel_id=1, source_target_pairs={{0,4},{1,3},{2,6},{3,1},{4,0},{5,7},{6,2},{7,5},{8,12},{9,11},{10,... | collective-permute-start | bytes 4128776 | tf_op jit(solution)/shard_map/ppermute | solution.py:79
  237.5 38.9 %all-to-all-start.2 = ((bf16[48,49,256]{2,1,0:T(8,128)(2,1)}), bf16[48,49,256]{2,1,0:T(8,128)(2,1)}, u32[]{:S(2)}, u32[]{:S(2)}) async-start(bf16[48,49,256]{2,1,0:T(8,128)(2,1)} %order_views.1), calls=%async_computation.2 | async-start | bytes 2752512 | tf_op jit(solution)/shard_map/all_to_all | solution.py:977
  269.3 30.4 %collective-permute-start.25 = (bf16[4,48,1792]{2,1,0:T(8,128)(2,1)}, bf16[4,48,1792]{2,1,0:T(8,128)(2,1)}, u32[]{:S(2)}, u32[]{:S(2)}) collective-permute-start(bf16[4,48,1792]{2,1,0:T(8,128)(2,1)} %add_convert_fusion.4), channel_id=1, source_target_pairs={{0,2},{1,5},{2,0},{3,7},{4,6},{5,1},{6,4},{7,3},{8,10},{9,13},{10,... | collective-permute-start | bytes 2064392 | tf_op jit(solution)/shard_map/ppermute | solution.py:79
  273.9 33.4 %collective-permute-start.27 = (bf16[8,48,1920]{2,1,0:T(8,128)(2,1)}, bf16[8,48,1920]{2,1,0:T(8,128)(2,1)}, u32[]{:S(2)}, u32[]{:S(2)}) collective-permute-start(bf16[8,48,1920]{2,1,0:T(8,128)(2,1)} %add_convert_fusion), channel_id=1, source_target_pairs={{0,4},{1,3},{2,6},{3,1},{4,0},{5,7},{6,2},{7,5},{8,12},{9,11},{10,... | collective-permute-start | bytes 4423688 | tf_op jit(solution)/shard_map/ppermute | solution.py:79
  276.4 30.9 %copy-start.1 = (bf16[16,48,1920]{2,1,0:T(8,128)(2,1)S(1)}, bf16[16,48,1920]{2,1,0:T(8,128)(2,1)}, u32[]{:S(2)}) copy-start(bf16[16,48,1920]{2,1,0:T(8,128)(2,1)} %grad_up_out_keep.1) | copy-start | bytes 8847364
  301.6 31.4 %collective-permute-start.28 = (bf16[48,1792]{1,0:T(8,128)(2,1)S(1)}, bf16[48,1792]{1,0:T(8,128)(2,1)S(1)}, u32[]{:S(2)}, u32[]{:S(2)}) collective-permute-start(bf16[48,1792]{1,0:T(8,128)(2,1)S(1)} %get-tuple-element.549), channel_id=1, source_target_pairs={{0,8},{1,9},{2,10},{3,11},{4,12},{5,13},{6,14},{7,15},{8,0},{9,1},... | collective-permute-start | bytes 516104 | tf_op jit(solution)/shard_map/ppermute | solution.py:79
  304.3 28.7 %collective-permute-start.29 = (bf16[48,1792]{1,0:T(8,128)(2,1)S(1)}, bf16[48,1792]{1,0:T(8,128)(2,1)S(1)}, u32[]{:S(2)}, u32[]{:S(2)}) collective-permute-start(bf16[48,1792]{1,0:T(8,128)(2,1)S(1)} %get-tuple-element.548), channel_id=1, source_target_pairs={{0,16},{1,17},{2,18},{3,19},{4,20},{5,21},{6,22},{7,23},{8,24},{9,... | collective-permute-start | bytes 516104 | tf_op jit(solution)/shard_map/ppermute | solution.py:79
  305.9 27.2 %collective-permute-start.30 = (bf16[48,1792]{1,0:T(8,128)(2,1)S(1)}, bf16[48,1792]{1,0:T(8,128)(2,1)S(1)}, u32[]{:S(2)}, u32[]{:S(2)}) collective-permute-start(bf16[48,1792]{1,0:T(8,128)(2,1)S(1)} %get-tuple-element.547), channel_id=1, source_target_pairs={{0,24},{1,25},{2,26},{3,27},{4,28},{5,29},{6,30},{7,31},{8,16},{9,... | collective-permute-start | bytes 516104 | tf_op jit(solution)/shard_map/ppermute | solution.py:79
  309.0 26.2 %collective-permute-start.31 = (bf16[4,48,1920]{2,1,0:T(8,128)(2,1)S(1)}, bf16[4,48,1920]{2,1,0:T(8,128)(2,1)S(1)}, u32[]{:S(2)}, u32[]{:S(2)}) collective-permute-start(bf16[4,48,1920]{2,1,0:T(8,128)(2,1)S(1)} %add_convert_fusion.3), channel_id=1, source_target_pairs={{0,2},{1,5},{2,0},{3,7},{4,6},{5,1},{6,4},{7,3},{8,10},{9,13},{10,... | collective-permute-start | bytes 2211848 | tf_op jit(solution)/shard_map/ppermute | solution.py:79
  344.6 14.6 %collective-permute-start.33 = (bf16[16,48,1152]{2,1,0:T(8,128)(2,1)}, bf16[16,48,1152]{2,1,0:T(8,128)(2,1)}, u32[]{:S(2)}, u32[]{:S(2)}) collective-permute-start(bf16[16,48,1152]{2,1,0:T(8,128)(2,1)} %grad_in_send.1), channel_id=1, source_target_pairs={{0,1},{1,0},{2,3},{3,2},{4,5},{5,4},{6,7},{7,6},{8,9},{9,8},{10,11... | collective-permute-start | bytes 5308424 | tf_op jit(solution)/shard_map/ppermute | solution.py:79
  351.0 51.8 %collective-permute-start.32 = (bf16[6,196,768]{2,1,0:T(8,128)(2,1)}, bf16[6,196,768]{2,1,0:T(8,128)(2,1)}, u32[]{:S(2)}, u32[]{:S(2)}) collective-permute-start(bf16[6,196,768]{2,1,0:T(8,128)(2,1)} %get-tuple-element.205), channel_id=1, source_target_pairs={{0,1},{1,0},{2,3},{3,2},{4,5},{5,4},{6,7},{7,6},{8,9},{9,8},{10,11... | collective-permute-start | bytes 5419016 | tf_op jit(solution)/shard_map/ppermute | solution.py:79
  361.8 23.6 %collective-permute-start.34 = (bf16[8,48,1152]{2,1,0:T(8,128)(2,1)}, bf16[8,48,1152]{2,1,0:T(8,128)(2,1)}, u32[]{:S(2)}, u32[]{:S(2)}) collective-permute-start(bf16[8,48,1152]{2,1,0:T(8,128)(2,1)} %add_convert_fusion.2), channel_id=1, source_target_pairs={{0,4},{1,3},{2,6},{3,1},{4,0},{5,7},{6,2},{7,5},{8,12},{9,11},{10,... | collective-permute-start | bytes 2654216 | tf_op jit(solution)/shard_map/ppermute | solution.py:79
  366.8 13.2 %collective-permute-start.35 = (bf16[48,1920]{1,0:T(8,128)(2,1)S(1)}, bf16[48,1920]{1,0:T(8,128)(2,1)S(1)}, u32[]{:S(2)}, u32[]{:S(2)}) collective-permute-start(bf16[48,1920]{1,0:T(8,128)(2,1)S(1)} %get-tuple-element.546), channel_id=1, source_target_pairs={{0,8},{1,9},{2,10},{3,11},{4,12},{5,13},{6,14},{7,15},{8,0},{9,1},... | collective-permute-start | bytes 552968 | tf_op jit(solution)/shard_map/ppermute | solution.py:79
  367.6 16.4 %collective-permute-start.36 = (bf16[48,1920]{1,0:T(8,128)(2,1)S(1)}, bf16[48,1920]{1,0:T(8,128)(2,1)S(1)}, u32[]{:S(2)}, u32[]{:S(2)}) collective-permute-start(bf16[48,1920]{1,0:T(8,128)(2,1)S(1)} %get-tuple-element.545), channel_id=1, source_target_pairs={{0,16},{1,17},{2,18},{3,19},{4,20},{5,21},{6,22},{7,23},{8,24},{9,... | collective-permute-start | bytes 552968 | tf_op jit(solution)/shard_map/ppermute | solution.py:79
  370.6 13.5 %collective-permute-start.37 = (bf16[48,1920]{1,0:T(8,128)(2,1)S(1)}, bf16[48,1920]{1,0:T(8,128)(2,1)S(1)}, u32[]{:S(2)}, u32[]{:S(2)}) collective-permute-start(bf16[48,1920]{1,0:T(8,128)(2,1)S(1)} %get-tuple-element.544), channel_id=1, source_target_pairs={{0,24},{1,25},{2,26},{3,27},{4,28},{5,29},{6,30},{7,31},{8,16},{9,... | collective-permute-start | bytes 552968 | tf_op jit(solution)/shard_map/ppermute | solution.py:79
  386.9 25.5 %collective-permute-start.38 = (bf16[4,48,1152]{2,1,0:T(8,128)(2,1)S(1)}, bf16[4,48,1152]{2,1,0:T(8,128)(2,1)S(1)}, u32[]{:S(2)}, u32[]{:S(2)}) collective-permute-start(bf16[4,48,1152]{2,1,0:T(8,128)(2,1)S(1)} %add_convert_fusion.5), channel_id=1, source_target_pairs={{0,2},{1,5},{2,0},{3,7},{4,6},{5,1},{6,4},{7,3},{8,10},{9,13},{10,... | collective-permute-start | bytes 1327112 | tf_op jit(solution)/shard_map/ppermute | solution.py:79
  388.6 14.0 %all-to-all-start.3 = ((f32[32,1,224]{2,1,0:T(1,128)}), f32[32,1,224]{2,1,0:T(1,128)S(1)}, u32[]{:S(2)}, u32[]{:S(2)}) async-start(f32[32,1,224]{2,1,0:T(1,128)} %all_to_all.28), calls=%async_computation.3 | async-start | bytes 65536 | tf_op jit(solution)/shard_map/all_to_all | solution.py:1104
  413.9 7.9 %collective-permute-start.41 = (bf16[48,1152]{1,0:T(8,128)(2,1)S(1)}, bf16[48,1152]{1,0:T(8,128)(2,1)S(1)}, u32[]{:S(2)}, u32[]{:S(2)}) collective-permute-start(bf16[48,1152]{1,0:T(8,128)(2,1)S(1)} %get-tuple-element.219), channel_id=1, source_target_pairs={{0,24},{1,25},{2,26},{3,27},{4,28},{5,29},{6,30},{7,31},{8,16},{9,... | collective-permute-start | bytes 331784 | tf_op jit(solution)/shard_map/ppermute | solution.py:79
  414.6 11.3 %collective-permute-start.40 = (bf16[48,1152]{1,0:T(8,128)(2,1)S(1)}, bf16[48,1152]{1,0:T(8,128)(2,1)S(1)}, u32[]{:S(2)}, u32[]{:S(2)}) collective-permute-start(bf16[48,1152]{1,0:T(8,128)(2,1)S(1)} %get-tuple-element.218), channel_id=1, source_target_pairs={{0,16},{1,17},{2,18},{3,19},{4,20},{5,21},{6,22},{7,23},{8,24},{9,... | collective-permute-start | bytes 331784 | tf_op jit(solution)/shard_map/ppermute | solution.py:79
  416.0 9.8 %collective-permute-start.39 = (bf16[48,1152]{1,0:T(8,128)(2,1)S(1)}, bf16[48,1152]{1,0:T(8,128)(2,1)S(1)}, u32[]{:S(2)}, u32[]{:S(2)}) collective-permute-start(bf16[48,1152]{1,0:T(8,128)(2,1)S(1)} %get-tuple-element.217), channel_id=1, source_target_pairs={{0,8},{1,9},{2,10},{3,11},{4,12},{5,13},{6,14},{7,15},{8,0},{9,1},... | collective-permute-start | bytes 331784 | tf_op jit(solution)/shard_map/ppermute | solution.py:79
  (10 other events, 130.6 us)
